TPU v7x, 32 devices: a whole 2x2x4 slice. The times are simulated.
32 devices in a mesh: dp: 4 (over y, core), expert: 8 (over z, x).
Axes of the slice: x: 2, y: 2, z: 4, core: 2. Of those that a mesh axis runs over, the one named last changes fastest.
Arguments:
- tokens: bfloat16 [4096, 2048], P(('dp', 'expert')), may hold values from -6 to 6
- out_grad: bfloat16 [4096, 2048], P(('dp', 'expert')), may hold values from -3 to 3
- expert_ids: int32 [4096, 8], P(('dp', 'expert')), may hold values from 0 to 15, all different within a row; in each aligned block of 128 rows (0 to 127, 128 to 255, ...) at most 68 rows name the same one
- gate_probs: bfloat16 [4096, 8], P(('dp', 'expert')), may hold values from 0.019897461 to 0.3984375
- gate_up_weight: bfloat16 [16, 2048, 768], P('expert'), may hold values from -0.125 to 0.125
- down_weight: bfloat16 [16, 384, 2048], P('expert'), may hold values from -0.3125 to 0.3125
Outputs:
- grad_tokens: bfloat16 [4096, 2048], P(('dp', 'expert'))
- grad_probs: bfloat16 [4096, 8], P(('dp', 'expert'))
- grad_weights: bfloat16 [2048, 16, 1152], P('dp', 'expert')
Inputs may be any that keep to these rules, and one draw needn't show every extreme that they name: `expert_ids`: each row names 8 distinct experts; in each aligned block of 128 rows no expert is named by more than 68 rows.
All inputs are finite; a program needn't handle non-finite values.
Results may differ from a plain program's by a relative error of at most 0.013.
Values may be sent and summed in bfloat16 or wider, within the bound.
No kernel may reach another device: no remote copies, remote signals or barrier semaphores. Data moves between devices by JAX's collectives and lax.ppermute only.
A program may use at most 128 MiB of HBM per device.

v0:
```python
import functools

import jax
import jax.numpy as jnp
from jax import lax
from jax.experimental import pallas as pl
from jax.experimental.pallas import tpu as pltpu
from jax.sharding import PartitionSpec as P


def ring_order(size):
    half = size // 2
    return [2 * p if p < half else 2 * (size - 1 - p) + 1 for p in range(size)]


def joined(refs):
    parts = [ref[...] for ref in refs]
    return parts[0] if len(parts) == 1 else jnp.concatenate(parts, axis=0)


def expert_kernel(count, size, scalars, *refs):
    g_refs, gate_refs = refs[:count], refs[count : 2 * count]
    first, (w_in, w_out, pre_ref, hidden_ref) = 2 * count, refs[-(count + 5) : -(count + 1)]
    row_refs, total = refs[-(count + 1) : -1], refs[-1]
    e, last = pl.program_id(0), pl.num_programs(0) - 1
    units, width = w_out.shape[1:]
    x_refs = refs[first : -(count + 5)]
    pre = jnp.dot(joined(x_refs), w_in[0], preferred_element_type=jnp.float32)
    back = lax.dot_general(
        joined(g_refs), w_out[0], (((1,), (1,)), ((), ())), preferred_element_type=jnp.float32
    )
    gates = [ref[0].astype(jnp.float32) for ref in gate_refs]
    gates = gates[0] if count == 1 else jnp.concatenate(gates, axis=0)
    column = lax.broadcasted_iota(jnp.int32, gates.shape, 1) == e
    weight = jnp.sum(jnp.where(column, gates, 0.0), axis=1, keepdims=True)
    gate_pre, up_pre = pre[:, :units], pre[:, units:]
    logistic = 1.0 / (1.0 + jnp.exp(-gate_pre))
    active = gate_pre * logistic
    slope = logistic * (1.0 + gate_pre * (1.0 - logistic))
    hidden = (active * up_pre).astype(jnp.bfloat16).astype(jnp.float32)
    probs = jnp.sum(hidden * back, axis=1, keepdims=True)
    hidden_ref[0] = (weight * hidden).astype(jnp.bfloat16)
    grad_hidden = weight * back
    pre_ref[0, :, :units] = (grad_hidden * up_pre * slope).astype(jnp.bfloat16)
    pre_ref[0, :, units:] = (grad_hidden * active).astype(jnp.bfloat16)
    rows = lax.dot_general(
        pre_ref[0], w_in[0], (((1,), (1,)), ((), ())), preferred_element_type=jnp.float32
    )
    lane = lax.broadcasted_iota(jnp.int32, (rows.shape[0], total.shape[1] - width), 1)
    tail = jnp.where(lane == scalars[size] * pl.num_programs(0) + e, probs, 0.0)

    @pl.when(e == 0)
    def _():
        total[:, :width] = rows
        total[:, width:] = tail

    @pl.when(e > 0)
    def _():
        total[:, :width] += rows
        total[:, width:] += tail

    @pl.when(e == last)
    def _():
        at = 0
        for ref in row_refs:
            ref[...] = total[at : at + ref.shape[0]].astype(jnp.bfloat16)
            at += ref.shape[0]


def expert_blocks(blocks, table, gates, weight_in, weight_out):
    count = len(blocks)
    experts, width, wide = weight_in.shape
    units = weight_out.shape[1]
    sizes = [b[2] - b[1] for b in blocks]
    rows = sum(sizes)
    full = width + -(-gates.shape[0] * experts // 128) * 128
    whole = lambda n, w=width: pl.BlockSpec((n, w), lambda e, s: (0, 0))

    def gate_spec(offset, lo, n):
        return pl.BlockSpec((1, n, experts), lambda e, s: (s[offset], lo // n, 0))

    per_expert = lambda a, b: pl.BlockSpec((1, a, b), lambda e, s: (e, 0, 0))
    out = pl.pallas_call(
        functools.partial(expert_kernel, count, gates.shape[0]),
        out_shape=[
            jax.ShapeDtypeStruct((experts, rows, wide), jnp.bfloat16),
            jax.ShapeDtypeStruct((experts, rows, units), jnp.bfloat16),
        ]
        + [jax.ShapeDtypeStruct((n, full), jnp.bfloat16) for n in sizes],
        grid_spec=pltpu.PrefetchScalarGridSpec(
            num_scalar_prefetch=1,
            grid=(experts,),
            in_specs=[whole(n) for n in sizes]
            + [gate_spec(b[0], b[1], b[2] - b[1]) for b in blocks]
            + [whole(n) for n in sizes]
            + [per_expert(width, wide), per_expert(units, width)],
            out_specs=[per_expert(rows, wide), per_expert(rows, units)]
            + [whole(n, full) for n in sizes],
            scratch_shapes=[pltpu.VMEM((rows, full), jnp.float32)],
        ),
        cost_estimate=pl.CostEstimate(
            flops=2 * rows * experts * width * (2 * wide + units),
            bytes_accessed=2 * experts * width * (wide + units) + 8 * rows * width,
            transcendentals=0,
        ),
        name="experts",
    )(table, *[b[4] for b in blocks], *[gates] * count, *[b[3] for b in blocks], weight_in, weight_out)
    return out[0], out[1], out[2:]


def weight_kernel(x_rows, p_rows, start, depth, *refs):
    x_refs, p_refs = refs[: len(x_rows)], refs[len(x_rows) : len(x_rows) + len(p_rows)]
    sent, kept, held, gradients, result, x_sems, p_sems, sems = refs[len(x_rows) + len(p_rows) :]
    outer, experts = sent.shape[0], p_refs[0].shape[0]
    size = sent.shape[2] // experts

    core, mine = lax.axis_index("dp") & 1, lax.axis_index("dp") >> 1

    def slabs(i):
        for place in range(outer):
            block = 2 * lax.rem(mine + 1 + place, outer) + (1 - core if i == 0 else core)
            column = pl.multiple_of(block * depth, depth)
            row = 0
            for k, n in enumerate(x_rows):
                yield pltpu.make_async_copy(
                    x_refs[k].at[:, pl.ds(column, depth)],
                    held.at[i, row : row + n, place * depth : (place + 1) * depth],
                    x_sems.at[i, place, k],
                )
                row += n

    def gradient_copies():
        row = 0
        for k, n in enumerate(p_rows):
            for e in range(experts):
                yield pltpu.make_async_copy(
                    p_refs[k].at[e, :, start : start + size],
                    gradients.at[row : row + n, e * size : (e + 1) * size],
                    p_sems.at[k, e],
                )
            row += n

    for copy in [*slabs(0), *gradient_copies(), *slabs(1)]:
        copy.start()
    for copy in gradient_copies():
        copy.wait()
    stores = []
    for i, out in enumerate((sent, kept)):
        for copy in slabs(i):
            copy.wait()
        part = lax.dot_general(
            held[i], gradients[...], (((0,), (0,)), ((), ())), preferred_element_type=jnp.float32
        )
        result[i] = part.astype(jnp.bfloat16).reshape(result.shape[1:])
        stores.append(pltpu.make_async_copy(result.at[i], out, sems.at[i]))
        stores[-1].start()
    for store in stores:
        store.wait()


def weight_parts(xs, ps, start, size, replicas):
    width = xs[0].shape[1]
    experts = ps[0].shape[0]
    outer, depth = replicas // 2, width // replicas
    x_rows, p_rows = [x.shape[0] for x in xs], [p.shape[1] for p in ps]
    rows, columns = sum(x_rows), experts * size

    anywhere = pl.BlockSpec(memory_space=pl.ANY)
    return pl.pallas_call(
        functools.partial(weight_kernel, x_rows, p_rows, start, depth),
        out_shape=[jax.ShapeDtypeStruct((outer, depth, columns), jnp.bfloat16)] * 2,
        in_specs=[anywhere] * (len(xs) + len(ps)),
        out_specs=[anywhere] * 2,
        scratch_shapes=[
            pltpu.VMEM((2, rows, outer * depth), jnp.bfloat16),
            pltpu.VMEM((rows, columns), jnp.bfloat16),
            pltpu.VMEM((2, outer, depth, columns), jnp.bfloat16),
            pltpu.SemaphoreType.DMA((2, outer, len(xs))),
            pltpu.SemaphoreType.DMA((len(ps), experts)),
            pltpu.SemaphoreType.DMA((2,)),
        ],
        cost_estimate=pl.CostEstimate(
            flops=2 * rows * width * columns,
            bytes_accessed=2 * (rows * (width + columns) + width * columns),
            transcendentals=0,
        ),
        name="weights",
    )(*xs, *ps)


def place_kernel(count, *refs):
    total = refs[0][...].astype(jnp.float32)
    for ref in refs[1:count]:
        total += ref[...].astype(jnp.float32)
    out = refs[-1]
    size = out.shape[2]
    for e in range(out.shape[1]):
        out[:, e, :] = total[:, e * size : (e + 1) * size].astype(jnp.bfloat16)


def place_chunk(pieces, at, experts, columns, held=None):
    depth, size = pieces[0].shape[1], pieces[0].shape[2] // experts
    tile = depth
    specs = [
        pl.BlockSpec((None, tile, experts * size), lambda i, last=p.shape[0] - 1: (last, i, 0))
        for p in pieces
    ]
    args = list(pieces) + ([] if held is None else [held])
    return pl.pallas_call(
        functools.partial(place_kernel, len(pieces)),
        out_shape=jax.ShapeDtypeStruct((depth, experts, columns), jnp.bfloat16),
        grid=(depth // tile,),
        in_specs=specs
        + ([] if held is None else [pl.BlockSpec(memory_space=pl.ANY)]),
        out_specs=pl.BlockSpec((tile, experts, size), lambda i: (i, 0, at)),
        input_output_aliases={} if held is None else {len(pieces): 0},
        name="place",
    )(*args)


def layer(tokens, out_grad, expert_ids, gate_probs, gate_up_weight, down_weight):
    rows, width = tokens.shape
    local_experts = gate_up_weight.shape[0]
    size = lax.axis_size("expert")
    expert_count = local_experts * size
    half, mid = size // 2, rows // 2
    order = ring_order(size)
    forward = [(order[p], order[(p + 1) % size]) for p in range(size)]
    backward = [(b, a) for a, b in forward]
    me = lax.axis_index("expert")
    experts = jnp.arange(expert_count, dtype=jnp.int32)
    onehot = expert_ids[:, :, None] == experts[None, None, :]
    dense_gates = jnp.sum(
        jnp.where(onehot, gate_probs[:, :, None].astype(jnp.float32), 0.0), axis=1
    ).astype(jnp.bfloat16)
    gates = lax.all_to_all(dense_gates, "expert", split_axis=1, concat_axis=0, tiled=True)
    gates = gates.reshape(size, rows, local_experts)
    followers = [[order[(order.index(e) + k) % size] for k in range(size)] for e in range(size)]
    mine = lax.broadcasted_iota(jnp.int32, (size, size), 0) == me
    table = jnp.sum(jnp.where(mine, jnp.asarray(followers, jnp.int32), 0), axis=0)
    table = jnp.concatenate([table, me[None].astype(jnp.int32)])

    blocks = [(0, 0, rows, tokens, out_grad)]
    left, right = (tokens, out_grad), (tokens, out_grad)
    for step in range(1, half + 1):
        if step == half:
            left, right = tuple(a[:mid] for a in left), tuple(a[mid:] for a in right)
        xl = lax.ppermute(left[0], "expert", forward)
        xr = lax.ppermute(right[0], "expert", backward)
        left = (xl, lax.ppermute(left[1], "expert", forward))
        right = (xr, lax.ppermute(right[1], "expert", backward))
        if step < half:
            blocks.append((size - step, 0, rows) + left)
            blocks.append((step, 0, rows) + right)
    blocks.append((half, 0, mid) + left)
    blocks.append((half, mid, rows) + right)

    groups = [blocks[:3]] + [blocks[i : i + 2] for i in range(3, len(blocks), 2)]
    results = []
    for group in groups:
        results.append(
            expert_blocks(group, table, gates, gate_up_weight, down_weight)
        )
    partial_rows = [r for result in results for r in result[2]]

    narrow = lambda a: a.astype(jnp.bfloat16)
    to_left, to_right = partial_rows[-2], partial_rows[-1]
    for step in range(half - 1, -1, -1):
        from_right = lax.ppermute(to_left, "expert", backward).astype(jnp.float32)
        from_left = lax.ppermute(to_right, "expert", forward).astype(jnp.float32)
        if step == half - 1:
            pad = jnp.zeros((mid, from_left.shape[1]), jnp.float32)
            from_right = jnp.concatenate([from_right, pad])
            from_left = jnp.concatenate([pad, from_left])
        if step > 0:
            to_left = narrow(partial_rows[2 * step - 1].astype(jnp.float32) + from_right)
            to_right = narrow(partial_rows[2 * step].astype(jnp.float32) + from_left)
    returned = narrow(partial_rows[0].astype(jnp.float32) + from_right + from_left)
    grad_tokens = returned[:, :width]
    probs = returned[:, width : width + expert_count].astype(jnp.float32)
    grad_probs = narrow(jnp.sum(jnp.where(onehot, probs[:, None, :], 0.0), axis=2))

    replicas = lax.axis_size("dp")
    outer = replicas // 2
    swap = [(i, i ^ 1) for i in range(replicas)]
    xs, gs = [b[3] for b in blocks], [b[4] for b in blocks]
    pres, hiddens = [r[0] for r in results], [r[1] for r in results]
    units = down_weight.shape[1]
    third = 2 * units // 3
    chunks = [(xs, pres, 2 * third, third), (gs, hiddens, 0, units), (xs, pres, 0, 2 * third)]
    places = [2, 2, 0]
    parts = []
    for chunk in chunks:
        parts += weight_parts(*chunk, replicas)
    weight_total = None
    for number, at in enumerate(places):
        sent, kept = parts[2 * number : 2 * number + 2]
        arrived = lax.ppermute(sent, "dp", swap)
        pieces = [kept, arrived]
        for shift in range(1, outer):
            pairs = [
                (2 * y + c, 2 * ((y + shift) % outer) + c) for y in range(outer) for c in range(2)
            ]
            both = kept[shift - 1].astype(jnp.float32) + arrived[shift - 1].astype(jnp.float32)
            pieces.append(lax.ppermute(narrow(both)[None], "dp", pairs))
        weight_total = place_chunk(pieces, at, local_experts, 3 * units, weight_total)
    return (grad_tokens, grad_probs, weight_total)


def solution(mesh):
    in_specs = (
        P(("dp", "expert"), None),
        P(("dp", "expert"), None),
        P(("dp", "expert"), None),
        P(("dp", "expert"), None),
        P("expert", None, None),
        P("expert", None, None),
    )
    out_specs = (P(("dp", "expert"), None), P(("dp", "expert"), None), P("dp", "expert", None))
    return jax.shard_map(layer, mesh=mesh, in_specs=in_specs, out_specs=out_specs, check_vma=False)
```

profile of v0, /device:TPU:0, one launch (start us, length us, event | category | flops | bytes accessed | tf_op | source)
XLA Modules:
  0.0 223.2 jit_solution(17771036116157569875)
XLA Ops:
  0.6 3.0 %collective-permute-start.1 = (bf16[128,2048]{1,0:T(8,128)(2,1)}, bf16[128,2048]{1,0:T(8,128)(2,1)S(1)}, u32[]{:S(2)}, u32[]{:S(2)}) collective-permute-start(bf16[128,2048]{1,0:T(8,128)(2,1)} %refs_0_.6), channel_id=1, source_target_pairs={{2,0},{4,2},{6,4},{7,6},{5,7},{3,5},{1,3},{0,1},{10,8},{12,10},{14... | collective-permute-start | bytes 1572872 | tf_op jit(solution)/shard_map/ppermute | solution.py:251
  3.8 1.9 collective-permute-start.3
  5.8 10.9 %collective-permute-done.1.refs_2_ = bf16[128,2048]{1,0:T(8,128)(2,1)S(1)} collective-permute-done((bf16[128,2048]{1,0:T(8,128)(2,1)}, bf16[128,2048]{1,0:T(8,128)(2,1)S(1)}, u32[]{:S(2)}, u32[]{:S(2)}) %collective-permute-start.1) | collective-permute-done | bytes 524320 | tf_op jit(solution)/shard_map/ppermute | solution.py:251
  16.7 1.9 collective-permute-start.5
  18.8 9.1 %collective-permute-done.3.refs_8_.refs_2_ = bf16[128,2048]{1,0:T(8,128)(2,1)S(1)} collective-permute-done((bf16[128,2048]{1,0:T(8,128)(2,1)}, bf16[128,2048]{1,0:T(8,128)(2,1)S(1)}, u32[]{:S(2)}, u32[]{:S(2)}) %collective-permute-start.3) | collective-permute-done | bytes 524320 | tf_op jit(solution)/shard_map/ppermute | solution.py:249
  28.0 1.9 collective-permute-start.7
  32.1 6.1 %all-to-all-start = ((bf16[128,8,2]{0,2,1:T(2,128)(2,1)}), bf16[128,8,2]{0,2,1:T(2,128)(2,1)S(1)}, u32[]{:S(2)}, u32[]{:S(2)}) async-start(bf16[128,8,2]{0,2,1:T(2,128)(2,1)} %bitcast.1), calls=%async_computation | async-start | bytes 8192 | tf_op jit(solution)/shard_map/all_to_all | solution.py:236
  39.6 14.5 %all-to-all-done = bf16[128,8,2]{0,2,1:T(2,128)(2,1)S(1)} async-done(((bf16[128,8,2]{0,2,1:T(2,128)(2,1)}), bf16[128,8,2]{0,2,1:T(2,128)(2,1)S(1)}, u32[]{:S(2)}, u32[]{:S(2)}) %all-to-all-start) | async-done | bytes 4128 | tf_op jit(solution)/shard_map/all_to_all | solution.py:236
  59.0 14.3 %experts.4 = (bf16[2,384,768]{2,1,0:T(8,128)(2,1)}, bf16[2,384,384]{2,1,0:T(8,128)(2,1)}, bf16[128,2176]{1,0:T(8,128)(2,1)}, bf16[128,2176]{1,0:T(8,128)(2,1)}, bf16[128,2176]{1,0:T(8,128)(2,1)}) custom-call(s32[9]{0:T(128)} %pad_add_fusion.scalars, bf16[128,2048]{1,0:T(8,128)(2,1)} %refs_0_.6, bf16[128,2048]{1,0:T(8,128)(2,1)} %copy-done.25, ...), custom_call_target="tpu_custom_call" | custom-call | flops 6039797760 | bytes 15728640 | tf_op jit(solution)/shard_map/experts/pallas_call | solution.py:83
  73.3 10.9 %experts.5 = (bf16[2,256,768]{2,1,0:T(8,128)(2,1)}, bf16[2,256,384]{2,1,0:T(8,128)(2,1)}, bf16[128,2176]{1,0:T(8,128)(2,1)}, bf16[128,2176]{1,0:T(8,128)(2,1)}) custom-call(s32[9]{0:T(128)} %pad_add_fusion.scalars, bf16[128,2048]{1,0:T(8,128)(2,1)} %collective-permute-done.4.refs_0_.refs_3_, bf16[128,2048]{1,0:T(8,128)(2,1)} %collective-permute-done.5.refs_1_.refs_4_, ...), custom_call_target="tpu_custom_call" | custom-call | flops 4026531840 | bytes 13631488 | tf_op jit(solution)/shard_map/experts/pallas_call | solution.py:83
  88.8 11.0 %experts.6 = (bf16[2,256,768]{2,1,0:T(8,128)(2,1)}, bf16[2,256,384]{2,1,0:T(8,128)(2,1)}, bf16[128,2176]{1,0:T(8,128)(2,1)}, bf16[128,2176]{1,0:T(8,128)(2,1)}) custom-call(s32[9]{0:T(128)} %pad_add_fusion.scalars, bf16[128,2048]{1,0:T(8,128)(2,1)} %copy-done.20, bf16[128,2048]{1,0:T(8,128)(2,1)} %copy-done.19, bf16[8,128,2]{2,1,0:T(8,128)(2,1)} %bitcast.8, ...), custom_call_target="tpu_custom_call" | custom-call | flops 4026531840 | bytes 13631488 | tf_op jit(solution)/shard_map/experts/pallas_call | solution.py:83
  101.4 8.7 %experts.7 = (bf16[2,128,768]{2,1,0:T(8,128)(2,1)}, bf16[2,128,384]{2,1,0:T(8,128)(2,1)}, bf16[64,2176]{1,0:T(8,128)(2,1)}, bf16[64,2176]{1,0:T(8,128)(2,1)}) custom-call(s32[9]{0:T(128)} %pad_add_fusion.scalars, bf16[64,2048]{1,0:T(8,128)(2,1)} %copy-done.16, bf16[64,2048]{1,0:T(8,128)(2,1)} %copy-done.15, bf16[8,128,2]{2,1,0:T(8,128)(2,1)} %bitcast.10, ...), custom_call_target="tpu_custom_call" | custom-call | flops 2013265920 | bytes 11534336 | tf_op jit(solution)/shard_map/experts/pallas_call | solution.py:83
  112.2 9.1 %weights.4 = (bf16[2,512,768]{2,1,0:T(8,128)(2,1)}, bf16[2,512,768]{2,1,0:T(8,128)(2,1)}) custom-call(bf16[128,2048]{1,0:T(8,128)(2,1)} %refs_0_.6, bf16[128,2048]{1,0:T(8,128)(2,1)} %copy-done.25, bf16[128,2048]{1,0:T(8,128)(2,1)} %copy-done.24, bf16[128,2048]{1,0:T(8,128)(2,1)} %collective-permute-done.4.refs_0_.refs_3_, ...), custom_call_target="tpu_custom_call" | custom-call | flops 3221225472 | bytes 8912896 | tf_op jit(solution)/shard_map/weights/pallas_call | solution.py:169
  121.4 6.5 %weights.5 = (bf16[2,512,512]{2,1,0:T(8,128)(2,1)}, bf16[2,512,512]{2,1,0:T(8,128)(2,1)}) custom-call(bf16[128,2048]{1,0:T(8,128)(2,1)} %refs_0_.7, bf16[128,2048]{1,0:T(8,128)(2,1)} %copy-done.23, bf16[128,2048]{1,0:T(8,128)(2,1)} %copy-done.22, bf16[128,2048]{1,0:T(8,128)(2,1)} %collective-permute-done.6.refs_4_.refs_3_, ...), custom_call_target="tpu_custom_call" | custom-call | flops 2147483648 | bytes 7340032 | tf_op jit(solution)/shard_map/weights/pallas_call | solution.py:169
  128.5 9.4 %weights.3 = (bf16[2,512,1024]{2,1,0:T(8,128)(2,1)}, bf16[2,512,1024]{2,1,0:T(8,128)(2,1)}) custom-call(bf16[128,2048]{1,0:T(8,128)(2,1)} %refs_0_.7, bf16[128,2048]{1,0:T(8,128)(2,1)} %copy-done.23, bf16[128,2048]{1,0:T(8,128)(2,1)} %copy-done.22, bf16[128,2048]{1,0:T(8,128)(2,1)} %collective-permute-done.6.refs_4_.refs_3_, ...), custom_call_target="tpu_custom_call" | custom-call | flops 4294967296 | bytes 10485760 | tf_op jit(solution)/shard_map/weights/pallas_call | solution.py:169
  141.4 12.8 %collective-permute-done.17 = bf16[128,2176]{1,0:T(8,128)(2,1)S(1)} collective-permute-done((bf16[128,2176]{1,0:T(8,128)(2,1)S(1)}, bf16[128,2176]{1,0:T(8,128)(2,1)S(1)}, u32[]{:S(2)}, u32[]{:S(2)}) %collective-permute-start.17) | collective-permute-done | bytes 557088 | tf_op jit(solution)/shard_map/ppermute | solution.py:269
  156.7 1.6 collective-permute-start.29
  158.3 10.1 %collective-permute-done.18 = bf16[128,2176]{1,0:T(8,128)(2,1)S(1)} collective-permute-done((bf16[128,2176]{1,0:T(8,128)(2,1)S(1)}, bf16[128,2176]{1,0:T(8,128)(2,1)S(1)}, u32[]{:S(2)}, u32[]{:S(2)}) %collective-permute-start.18) | collective-permute-done | bytes 557088 | tf_op jit(solution)/shard_map/ppermute | solution.py:269
  172.4 3.5 %place.3.refs_3_ = bf16[512,2,1152]{2,1,0:T(2,128)(2,1)} custom-call(bf16[2,512,512]{2,1,0:T(8,128)(2,1)} %get-tuple-element.47.refs_0_, bf16[2,512,512]{2,1,0:T(8,128)(2,1)} %copy-done.4, bf16[1,512,512]{2,1,0:T(8,128)(2,1)} %collective-permute-done.29.refs_2_), custom_call_target="tpu_custom_call" | custom-call | tf_op jit(solution)/shard_map/place/pallas_call | solution.py:209
  178.8 1.7 add_convert_fusion
  187.5 10.6 %collective-permute-done.27.refs_2_ = bf16[1,512,768]{2,1,0:T(8,128)(2,1)} collective-permute-done((bf16[1,512,768]{2,1,0:T(8,128)(2,1)}, bf16[1,512,768]{2,1,0:T(8,128)(2,1)}, u32[]{:S(2)}, u32[]{:S(2)}) %collective-permute-start.27) | collective-permute-done | bytes 786464 | tf_op jit(solution)/shard_map/ppermute | solution.py:305
  198.0 4.0 %place.4.refs_3_ = bf16[512,2,1152]{2,1,0:T(2,128)(2,1)} custom-call(bf16[2,512,768]{2,1,0:T(8,128)(2,1)} %get-tuple-element.45.refs_0_, bf16[2,512,768]{2,1,0:T(8,128)(2,1)} %copy-done.2, bf16[1,512,768]{2,1,0:T(8,128)(2,1)} %collective-permute-done.27.refs_2_, bf16[512,2,1152]{2,1,0:T(2,128)(2,1)} %place.3.refs_3_), custom_call_target="tpu_custom_call", output_to_operand_aliasing={{}: (3, {})} | custom-call | tf_op jit(solution)/shard_map/place/pallas_call | solution.py:209
  202.1 15.6 %collective-permute-done.25.refs_2_ = bf16[1,512,1024]{2,1,0:T(8,128)(2,1)S(1)} collective-permute-done((bf16[1,512,1024]{2,1,0:T(8,128)(2,1)S(1)}, bf16[1,512,1024]{2,1,0:T(8,128)(2,1)S(1)}, u32[]{:S(2)}, u32[]{:S(2)}) %collective-permute-start.25) | collective-permute-done | bytes 1048608 | tf_op jit(solution)/shard_map/ppermute | solution.py:305
  218.7 4.5 %place.5 = bf16[512,2,1152]{2,1,0:T(2,128)(2,1)} custom-call(bf16[2,512,1024]{2,1,0:T(8,128)(2,1)} %get-tuple-element.39.refs_0_, bf16[2,512,1024]{2,1,0:T(8,128)(2,1)} %collective-permute-done.24.refs_1_, bf16[1,512,1024]{2,1,0:T(8,128)(2,1)} %copy-done.5, bf16[512,2,1152]{2,1,0:T(2,128)(2,1)} %place.4.refs_3_), custom_call_target="tpu_custom_call", output_to_operand_aliasing={{}: (3, {})} | custom-call | tf_op jit(solution)/shard_map/place/pallas_call | solution.py:209
  (124 shorter events, 38.6 us)
Async XLA Ops:
  0.6 16.1 %collective-permute-start.1 = (bf16[128,2048]{1,0:T(8,128)(2,1)}, bf16[128,2048]{1,0:T(8,128)(2,1)S(1)}, u32[]{:S(2)}, u32[]{:S(2)}) collective-permute-start(bf16[128,2048]{1,0:T(8,128)(2,1)} %refs_0_.6), channel_id=1, source_target_pairs={{2,0},{4,2},{6,4},{7,6},{5,7},{3,5},{1,3},{0,1},{10,8},{12,10},{14... | collective-permute-start | bytes 1572872 | tf_op jit(solution)/shard_map/ppermute | solution.py:251
  3.6 15.0 %collective-permute-start = (bf16[128,2048]{1,0:T(8,128)(2,1)}, bf16[128,2048]{1,0:T(8,128)(2,1)S(1)}, u32[]{:S(2)}, u32[]{:S(2)}) collective-permute-start(bf16[128,2048]{1,0:T(8,128)(2,1)} %refs_0_.6), channel_id=1, source_target_pairs={{0,2},{2,4},{4,6},{6,7},{7,5},{5,3},{3,1},{1,0},{8,10},{10,12},{12... | collective-permute-start | bytes 1572872 | tf_op jit(solution)/shard_map/ppermute | solution.py:250
  3.8 24.2 %collective-permute-start.3 = (bf16[128,2048]{1,0:T(8,128)(2,1)}, bf16[128,2048]{1,0:T(8,128)(2,1)S(1)}, u32[]{:S(2)}, u32[]{:S(2)}) collective-permute-start(bf16[128,2048]{1,0:T(8,128)(2,1)} %refs_0_.7), channel_id=1, source_target_pairs={{2,0},{4,2},{6,4},{7,6},{5,7},{3,5},{1,3},{0,1},{10,8},{12,10},{14... | collective-permute-start | bytes 1572872 | tf_op jit(solution)/shard_map/ppermute | solution.py:249
  5.7 24.2 %collective-permute-start.2 = (bf16[128,2048]{1,0:T(8,128)(2,1)}, bf16[128,2048]{1,0:T(8,128)(2,1)S(1)}, u32[]{:S(2)}, u32[]{:S(2)}) collective-permute-start(bf16[128,2048]{1,0:T(8,128)(2,1)} %refs_0_.7), channel_id=1, source_target_pairs={{0,2},{2,4},{4,6},{6,7},{7,5},{5,3},{3,1},{1,0},{8,10},{10,12},{12... | collective-permute-start | bytes 1572872 | tf_op jit(solution)/shard_map/ppermute | solution.py:248
  16.7 38.2 %collective-permute-start.5 = (bf16[128,2048]{1,0:T(8,128)(2,1)S(1)}, bf16[128,2048]{1,0:T(8,128)(2,1)}, u32[]{:S(2)}, u32[]{:S(2)}) collective-permute-start(bf16[128,2048]{1,0:T(8,128)(2,1)S(1)} %collective-permute-done.1.refs_2_), channel_id=1, source_target_pairs={{2,0},{4,2},{6,4},{7,6},{5,7},{3,5},{1,3},{0,1},{10,8},{12,10},{14... | collective-permute-start | bytes 1572872 | tf_op jit(solution)/shard_map/ppermute | solution.py:251
  18.7 36.8 %collective-permute-start.4 = (bf16[128,2048]{1,0:T(8,128)(2,1)S(1)}, bf16[128,2048]{1,0:T(8,128)(2,1)}, u32[]{:S(2)}, u32[]{:S(2)}) collective-permute-start(bf16[128,2048]{1,0:T(8,128)(2,1)S(1)} %collective-permute-done.refs_1_), channel_id=1, source_target_pairs={{0,2},{2,4},{4,6},{6,7},{7,5},{5,3},{3,1},{1,0},{8,10},{10,12},{12... | collective-permute-start | bytes 1572872 | tf_op jit(solution)/shard_map/ppermute | solution.py:250
  28.0 29.0 %collective-permute-start.7 = (bf16[128,2048]{1,0:T(8,128)(2,1)S(1)}, bf16[128,2048]{1,0:T(8,128)(2,1)}, u32[]{:S(2)}, u32[]{:S(2)}) collective-permute-start(bf16[128,2048]{1,0:T(8,128)(2,1)S(1)} %collective-permute-done.3.refs_8_.refs_2_), channel_id=1, source_target_pairs={{2,0},{4,2},{6,4},{7,6},{5,7},{3,5},{1,3},{0,1},{10,8},{12,10},{14... | collective-permute-start | bytes 1572872 | tf_op jit(solution)/shard_map/ppermute | solution.py:249
  29.9 27.6 %collective-permute-start.6 = (bf16[128,2048]{1,0:T(8,128)(2,1)S(1)}, bf16[128,2048]{1,0:T(8,128)(2,1)}, u32[]{:S(2)}, u32[]{:S(2)}) collective-permute-start(bf16[128,2048]{1,0:T(8,128)(2,1)S(1)} %collective-permute-done.2.refs_7_.refs_1_), channel_id=1, source_target_pairs={{0,2},{2,4},{4,6},{6,7},{7,5},{5,3},{3,1},{1,0},{8,10},{10,12},{12... | collective-permute-start | bytes 1572872 | tf_op jit(solution)/shard_map/ppermute | solution.py:248
  32.1 22.0 %all-to-all-start = ((bf16[128,8,2]{0,2,1:T(2,128)(2,1)}), bf16[128,8,2]{0,2,1:T(2,128)(2,1)S(1)}, u32[]{:S(2)}, u32[]{:S(2)}) async-start(bf16[128,8,2]{0,2,1:T(2,128)(2,1)} %bitcast.1), calls=%async_computation | async-start | bytes 8192 | tf_op jit(solution)/shard_map/all_to_all | solution.py:236
  54.9 29.3 %collective-permute-start.9 = (bf16[128,2048]{1,0:T(8,128)(2,1)}, bf16[128,2048]{1,0:T(8,128)(2,1)S(1)}, u32[]{:S(2)}, u32[]{:S(2)}) collective-permute-start(bf16[128,2048]{1,0:T(8,128)(2,1)} %collective-permute-done.5.refs_1_.refs_4_), channel_id=1, source_target_pairs={{2,0},{4,2},{6,4},{7,6},{5,7},{3,5},{1,3},{0,1},{10,8},{12,10},{14... | collective-permute-start | bytes 1572872 | tf_op jit(solution)/shard_map/ppermute | solution.py:251
  55.5 29.5 %collective-permute-start.8 = (bf16[128,2048]{1,0:T(8,128)(2,1)}, bf16[128,2048]{1,0:T(8,128)(2,1)S(1)}, u32[]{:S(2)}, u32[]{:S(2)}) collective-permute-start(bf16[128,2048]{1,0:T(8,128)(2,1)} %collective-permute-done.4.refs_0_.refs_3_), channel_id=1, source_target_pairs={{0,2},{2,4},{4,6},{6,7},{7,5},{5,3},{3,1},{1,0},{8,10},{10,12},{12... | collective-permute-start | bytes 1572872 | tf_op jit(solution)/shard_map/ppermute | solution.py:250
  57.0 29.5 %collective-permute-start.11 = (bf16[128,2048]{1,0:T(8,128)(2,1)}, bf16[128,2048]{1,0:T(8,128)(2,1)S(1)}, u32[]{:S(2)}, u32[]{:S(2)}) collective-permute-start(bf16[128,2048]{1,0:T(8,128)(2,1)} %collective-permute-done.7.refs_5_.refs_4_), channel_id=1, source_target_pairs={{2,0},{4,2},{6,4},{7,6},{5,7},{3,5},{1,3},{0,1},{10,8},{12,10},{14... | collective-permute-start | bytes 1572872 | tf_op jit(solution)/shard_map/ppermute | solution.py:249
  57.5 29.7 %collective-permute-start.10 = (bf16[128,2048]{1,0:T(8,128)(2,1)}, bf16[128,2048]{1,0:T(8,128)(2,1)S(1)}, u32[]{:S(2)}, u32[]{:S(2)}) collective-permute-start(bf16[128,2048]{1,0:T(8,128)(2,1)} %collective-permute-done.6.refs_4_.refs_3_), channel_id=1, source_target_pairs={{0,2},{2,4},{4,6},{6,7},{7,5},{5,3},{3,1},{1,0},{8,10},{10,12},{12... | collective-permute-start | bytes 1572872 | tf_op jit(solution)/shard_map/ppermute | solution.py:248
  84.3 15.5 %collective-permute-start.13 = (bf16[64,2048]{1,0:T(8,128)(2,1)S(1)}, bf16[64,2048]{1,0:T(8,128)(2,1)S(1)}, u32[]{:S(2)}, u32[]{:S(2)}) collective-permute-start(bf16[64,2048]{1,0:T(8,128)(2,1)S(1)} %slice.49), channel_id=1, source_target_pairs={{2,0},{4,2},{6,4},{7,6},{5,7},{3,5},{1,3},{0,1},{10,8},{12,10},{14... | collective-permute-start | bytes 786440 | tf_op jit(solution)/shard_map/ppermute | solution.py:251
  110.1 27.9 %collective-permute-start.16 = (bf16[64,2176]{1,0:T(8,128)(2,1)}, bf16[64,2176]{1,0:T(8,128)(2,1)}, u32[]{:S(2)}, u32[]{:S(2)}) collective-permute-start(bf16[64,2176]{1,0:T(8,128)(2,1)} %get-tuple-element.30), channel_id=1, source_target_pairs={{2,0},{4,2},{6,4},{7,6},{5,7},{3,5},{1,3},{0,1},{10,8},{12,10},{14... | collective-permute-start | bytes 835592 | tf_op jit(solution)/shard_map/ppermute | solution.py:269
  110.9 29.0 %collective-permute-start.20 = (bf16[64,2176]{1,0:T(8,128)(2,1)}, bf16[64,2176]{1,0:T(8,128)(2,1)S(1)}, u32[]{:S(2)}, u32[]{:S(2)}) collective-permute-start(bf16[64,2176]{1,0:T(8,128)(2,1)} %get-tuple-element.34), channel_id=1, source_target_pairs={{0,2},{2,4},{4,6},{6,7},{7,5},{5,3},{3,1},{1,0},{8,10},{10,12},{12... | collective-permute-start | bytes 835592 | tf_op jit(solution)/shard_map/ppermute | solution.py:270
  121.3 54.6 %collective-permute-start.26 = (bf16[2,512,768]{2,1,0:T(8,128)(2,1)}, bf16[2,512,768]{2,1,0:T(8,128)(2,1)S(1)}, u32[]{:S(2)}, u32[]{:S(2)}) collective-permute-start(bf16[2,512,768]{2,1,0:T(8,128)(2,1)} %get-tuple-element.46), channel_id=1, source_target_pairs={{0,8},{8,0},{16,24},{24,16},{1,9},{9,1},{17,25},{25,17},{2,10},{10... | collective-permute-start | bytes 4718600 | tf_op jit(solution)/shard_map/ppermute | solution.py:298
  127.9 28.6 %collective-permute-start.28 = (bf16[2,512,512]{2,1,0:T(8,128)(2,1)}, bf16[2,512,512]{2,1,0:T(8,128)(2,1)S(1)}, u32[]{:S(2)}, u32[]{:S(2)}) collective-permute-start(bf16[2,512,512]{2,1,0:T(8,128)(2,1)} %get-tuple-element.48), channel_id=1, source_target_pairs={{0,8},{8,0},{16,24},{24,16},{1,9},{9,1},{17,25},{25,17},{2,10},{10... | collective-permute-start | bytes 3145736 | tf_op jit(solution)/shard_map/ppermute | solution.py:298
  137.9 40.9 %collective-permute-start.24 = (bf16[2,512,1024]{2,1,0:T(8,128)(2,1)}, bf16[2,512,1024]{2,1,0:T(8,128)(2,1)}, u32[]{:S(2)}, u32[]{:S(2)}) collective-permute-start(bf16[2,512,1024]{2,1,0:T(8,128)(2,1)} %get-tuple-element.40), channel_id=1, source_target_pairs={{0,8},{8,0},{16,24},{24,16},{1,9},{9,1},{17,25},{25,17},{2,10},{10... | collective-permute-start | bytes 6291464 | tf_op jit(solution)/shard_map/ppermute | solution.py:298
  139.1 15.0 %collective-permute-start.17 = (bf16[128,2176]{1,0:T(8,128)(2,1)S(1)}, bf16[128,2176]{1,0:T(8,128)(2,1)S(1)}, u32[]{:S(2)}, u32[]{:S(2)}) collective-permute-start(bf16[128,2176]{1,0:T(8,128)(2,1)S(1)} %add_convert_fusion.8), channel_id=1, source_target_pairs={{2,0},{4,2},{6,4},{7,6},{5,7},{3,5},{1,3},{0,1},{10,8},{12,10},{14... | collective-permute-start | bytes 1671176 | tf_op jit(solution)/shard_map/ppermute | solution.py:269
  140.0 15.1 %collective-permute-start.21 = (bf16[128,2176]{1,0:T(8,128)(2,1)S(1)}, bf16[128,2176]{1,0:T(8,128)(2,1)S(1)}, u32[]{:S(2)}, u32[]{:S(2)}) collective-permute-start(bf16[128,2176]{1,0:T(8,128)(2,1)S(1)} %add_convert_fusion.5), channel_id=1, source_target_pairs={{0,2},{2,4},{4,6},{6,7},{7,5},{5,3},{3,1},{1,0},{8,10},{10,12},{12... | collective-permute-start | bytes 1671176 | tf_op jit(solution)/shard_map/ppermute | solution.py:270
  156.7 15.7 %collective-permute-start.29 = (bf16[1,512,512]{2,1,0:T(8,128)(2,1)S(1)}, bf16[1,512,512]{2,1,0:T(8,128)(2,1)}, u32[]{:S(2)}, u32[]{:S(2)}) collective-permute-start(bf16[1,512,512]{2,1,0:T(8,128)(2,1)S(1)} %add_convert_fusion.9), channel_id=1, source_target_pairs={{0,16},{8,24},{16,0},{24,8},{1,17},{9,25},{17,1},{25,9},{2,18},{10... | collective-permute-start | bytes 1572872 | tf_op jit(solution)/shard_map/ppermute | solution.py:305
  177.3 20.7 %collective-permute-start.27 = (bf16[1,512,768]{2,1,0:T(8,128)(2,1)}, bf16[1,512,768]{2,1,0:T(8,128)(2,1)}, u32[]{:S(2)}, u32[]{:S(2)}) collective-permute-start(bf16[1,512,768]{2,1,0:T(8,128)(2,1)} %add_convert_fusion.1), channel_id=1, source_target_pairs={{0,16},{8,24},{16,0},{24,8},{1,17},{9,25},{17,1},{25,9},{2,18},{10... | collective-permute-start | bytes 2359304 | tf_op jit(solution)/shard_map/ppermute | solution.py:305
  180.5 37.2 %collective-permute-start.25 = (bf16[1,512,1024]{2,1,0:T(8,128)(2,1)S(1)}, bf16[1,512,1024]{2,1,0:T(8,128)(2,1)S(1)}, u32[]{:S(2)}, u32[]{:S(2)}) collective-permute-start(bf16[1,512,1024]{2,1,0:T(8,128)(2,1)S(1)} %add_convert_fusion), channel_id=1, source_target_pairs={{0,16},{8,24},{16,0},{24,8},{1,17},{9,25},{17,1},{25,9},{2,18},{10... | collective-permute-start | bytes 3145736 | tf_op jit(solution)/shard_map/ppermute | solution.py:305
  (33 other events, 345.2 us)
where the time goes:
time: 224 us; the launch traced here: 223 us
  waiting for transfers between devices  86.5 us (39%)
  Pallas kernels  81.9 us (37%)
  starting transfers between devices  37.1 us (17%)
  other arithmetic  11.7 us (5%)
  local copies, waits for them, and re-layouts  4.99 us (2%)
    pallas_call x4, Pallas kernels, expert_blocks(): pl.pallas_call(functools.partial(expert_kernel, count, gates.shape[0]), o...  44.9 us
    ppermute x3, waiting for transfers between devices, layer(): pieces.append(lax.ppermute(narrow(both)[None], 'dp', pairs))  26.2 us
    pallas_call x3, Pallas kernels, weight_parts(): pl.pallas_call(functools.partial(weight_kernel, x_rows, p_rows, start, de...  25.1 us
    ppermute x4, waiting for transfers between devices, layer(): from_right = lax.ppermute(to_left, 'expert', backward).astype(jnp.float32)  24.4 us
    all_to_all x1, waiting for transfers between devices, layer(): lax.all_to_all(dense_gates, 'expert', split_axis=1, concat_axis=0, tiled=...  14.5 us
    pallas_call x3, Pallas kernels, place_chunk(): pl.pallas_call(functools.partial(place_kernel, len(pieces)), out_shape=ja...  12 us
    ppermute x4, waiting for transfers between devices, layer(): right = (xr, lax.ppermute(right[1], 'expert', backward))  10.9 us
    ppermute x4, waiting for transfers between devices, layer(): xr = lax.ppermute(right[0], 'expert', backward)  9.15 us
  transfers between devices with their start and end apart: 31, of which 9 were waited for; matrix products, arithmetic and copies ran while one was open for 6% of the time, Pallas kernels for 31%

commit v1 on v0

--- a/solution.py
+++ b/solution.py
@@ -18,17 +18,40 @@
     return parts[0] if len(parts) == 1 else jnp.concatenate(parts, axis=0)
 
 
-def expert_kernel(count, size, scalars, *refs):
-    g_refs, gate_refs = refs[:count], refs[count : 2 * count]
-    first, (w_in, w_out, pre_ref, hidden_ref) = 2 * count, refs[-(count + 5) : -(count + 1)]
-    row_refs, total = refs[-(count + 1) : -1], refs[-1]
+def row_totals(total, rows, tail, row_refs):
     e, last = pl.program_id(0), pl.num_programs(0) - 1
-    units, width = w_out.shape[1:]
-    x_refs = refs[first : -(count + 5)]
+    width = rows.shape[1]
+
+    @pl.when(e == 0)
+    def _():
+        total[:, :width] = rows
+        total[:, width:] = tail
+
+    @pl.when(e > 0)
+    def _():
+        total[:, :width] += rows
+        total[:, width:] += tail
+
+    @pl.when(e == last)
+    def _():
+        at = 0
+        for ref in row_refs:
+            ref[...] = total[at : at + ref.shape[0]].astype(jnp.bfloat16)
+            at += ref.shape[0]
+
+
+def times_transposed(left, right):
+    return lax.dot_general(left, right, (((1,), (1,)), ((), ())), preferred_element_type=jnp.float32)
+
+
+def expert_kernel(count, size, with_rows, scalars, *refs):
+    x_refs, g_refs, gate_refs = refs[:count], refs[count : 2 * count], refs[2 * count : 3 * count]
+    w_in, w_out, pre_ref, hidden_ref = refs[3 * count : 3 * count + 4]
+    outs = refs[3 * count + 4 :]
+    e = pl.program_id(0)
+    units = w_out.shape[1]
     pre = jnp.dot(joined(x_refs), w_in[0], preferred_element_type=jnp.float32)
-    back = lax.dot_general(
-        joined(g_refs), w_out[0], (((1,), (1,)), ((), ())), preferred_element_type=jnp.float32
-    )
+    back = times_transposed(joined(g_refs), w_out[0])
     gates = [ref[0].astype(jnp.float32) for ref in gate_refs]
     gates = gates[0] if count == 1 else jnp.concatenate(gates, axis=0)
     column = lax.broadcasted_iota(jnp.int32, gates.shape, 1) == e
@@ -43,68 +66,93 @@
     grad_hidden = weight * back
     pre_ref[0, :, :units] = (grad_hidden * up_pre * slope).astype(jnp.bfloat16)
     pre_ref[0, :, units:] = (grad_hidden * active).astype(jnp.bfloat16)
-    rows = lax.dot_general(
-        pre_ref[0], w_in[0], (((1,), (1,)), ((), ())), preferred_element_type=jnp.float32
-    )
-    lane = lax.broadcasted_iota(jnp.int32, (rows.shape[0], total.shape[1] - width), 1)
+    extra = outs[-1].shape[-1] - (w_out.shape[2] if with_rows else 0)
+    lane = lax.broadcasted_iota(jnp.int32, (pre.shape[0], extra), 1)
     tail = jnp.where(lane == scalars[size] * pl.num_programs(0) + e, probs, 0.0)
-
-    @pl.when(e == 0)
-    def _():
-        total[:, :width] = rows
-        total[:, width:] = tail
-
-    @pl.when(e > 0)
-    def _():
-        total[:, :width] += rows
-        total[:, width:] += tail
-
-    @pl.when(e == last)
-    def _():
-        at = 0
-        for ref in row_refs:
-            ref[...] = total[at : at + ref.shape[0]].astype(jnp.bfloat16)
-            at += ref.shape[0]
-
-
-def expert_blocks(blocks, table, gates, weight_in, weight_out):
+    if with_rows:
+        row_totals(outs[-1], times_transposed(pre_ref[0], w_in[0]), tail, outs[:-1])
+    else:
+        outs[0][0] = tail
+
+
+def row_kernel(count, *refs):
+    p_refs, tail_refs, w_in = refs[:count], refs[count : 2 * count], refs[2 * count]
+    parts = [ref[0] for ref in p_refs]
+    tails = [ref[0] for ref in tail_refs]
+    rows = times_transposed(jnp.concatenate(parts, axis=0), w_in[0])
+    row_totals(refs[-1], rows, jnp.concatenate(tails, axis=0), refs[2 * count + 1 : -1])
+
+
+def row_blocks(pres, tails, sizes, weight_in):
+    experts, width, wide = weight_in.shape
+    rows, full = sum(sizes), width + tails[0].shape[2]
+    per_expert = lambda a: pl.BlockSpec((1,) + a.shape[1:], lambda e: (e, 0, 0))
+    return pl.pallas_call(
+        functools.partial(row_kernel, len(pres)),
+        out_shape=[jax.ShapeDtypeStruct((n, full), jnp.bfloat16) for n in sizes],
+        grid=(experts,),
+        in_specs=[per_expert(a) for a in [*pres, *tails, weight_in]],
+        out_specs=[pl.BlockSpec((n, full), lambda e: (0, 0)) for n in sizes],
+        scratch_shapes=[pltpu.VMEM((rows, full), jnp.float32)],
+        cost_estimate=pl.CostEstimate(
+            flops=2 * rows * experts * width * wide,
+            bytes_accessed=2 * experts * width * wide + 4 * rows * width,
+            transcendentals=0,
+        ),
+        name="rows",
+    )(*pres, *tails, weight_in)
+
+
+def expert_blocks(blocks, table, gates, weight_in, weight_out, with_rows):
     count = len(blocks)
     experts, width, wide = weight_in.shape
     units = weight_out.shape[1]
     sizes = [b[2] - b[1] for b in blocks]
     rows = sum(sizes)
-    full = width + -(-gates.shape[0] * experts // 128) * 128
+    extra = -(-gates.shape[0] * experts // 128) * 128
     whole = lambda n, w=width: pl.BlockSpec((n, w), lambda e, s: (0, 0))
 
     def gate_spec(offset, lo, n):
         return pl.BlockSpec((1, n, experts), lambda e, s: (s[offset], lo // n, 0))
 
     per_expert = lambda a, b: pl.BlockSpec((1, a, b), lambda e, s: (e, 0, 0))
+    if with_rows:
+        more = [jax.ShapeDtypeStruct((n, width + extra), jnp.bfloat16) for n in sizes]
+        more_specs = [whole(n, width + extra) for n in sizes]
+        scratch = [pltpu.VMEM((rows, width + extra), jnp.float32)]
+    else:
+        more = [jax.ShapeDtypeStruct((experts, rows, extra), jnp.float32)]
+        more_specs, scratch = [per_expert(rows, extra)], []
     out = pl.pallas_call(
-        functools.partial(expert_kernel, count, gates.shape[0]),
+        functools.partial(expert_kernel, count, gates.shape[0], with_rows),
         out_shape=[
             jax.ShapeDtypeStruct((experts, rows, wide), jnp.bfloat16),
             jax.ShapeDtypeStruct((experts, rows, units), jnp.bfloat16),
         ]
-        + [jax.ShapeDtypeStruct((n, full), jnp.bfloat16) for n in sizes],
+        + more,
         grid_spec=pltpu.PrefetchScalarGridSpec(
             num_scalar_prefetch=1,
             grid=(experts,),
-            in_specs=[whole(n) for n in sizes]
+            in_specs=[whole(n) for n in sizes] * 2
             + [gate_spec(b[0], b[1], b[2] - b[1]) for b in blocks]
-            + [whole(n) for n in sizes]
             + [per_expert(width, wide), per_expert(units, width)],
-            out_specs=[per_expert(rows, wide), per_expert(rows, units)]
-            + [whole(n, full) for n in sizes],
-            scratch_shapes=[pltpu.VMEM((rows, full), jnp.float32)],
+            out_specs=[per_expert(rows, wide), per_expert(rows, units)] + more_specs,
+            scratch_shapes=scratch,
         ),
         cost_estimate=pl.CostEstimate(
-            flops=2 * rows * experts * width * (2 * wide + units),
+            flops=2 * rows * experts * width * ((1 + with_rows) * wide + units),
             bytes_accessed=2 * experts * width * (wide + units) + 8 * rows * width,
             transcendentals=0,
         ),
         name="experts",
-    )(table, *[b[4] for b in blocks], *[gates] * count, *[b[3] for b in blocks], weight_in, weight_out)
+    )(
+        table,
+        *[b[3] for b in blocks],
+        *[b[4] for b in blocks],
+        *[gates] * count,
+        weight_in,
+        weight_out,
+    )
     return out[0], out[1], out[2:]
 
 
@@ -257,11 +305,17 @@
 
     groups = [blocks[:3]] + [blocks[i : i + 2] for i in range(3, len(blocks), 2)]
     results = []
-    for group in groups:
+    for number, group in enumerate(groups):
         results.append(
-            expert_blocks(group, table, gates, gate_up_weight, down_weight)
+            expert_blocks(group, table, gates, gate_up_weight, down_weight, number < half - 2)
         )
-    partial_rows = [r for result in results for r in result[2]]
+    partial_rows = [r for result in results[:-2] for r in result[2]]
+    partial_rows += row_blocks(
+        [r[0] for r in results[-2:]],
+        [r[2][0] for r in results[-2:]],
+        [rows, rows, mid, mid],
+        gate_up_weight,
+    )
 
     narrow = lambda a: a.astype(jnp.bfloat16)
     to_left, to_right = partial_rows[-2], partial_rows[-1]

time: 224 us -> 232 us (1.036)
  waiting for transfers between devices: 86.5 us -> 91.5 us
    ppermute x4, waiting for transfers between devices: 9.15 us -> 14.2 us  [layer(): xr = lax.ppermute(right[0], 'expert', backward)]
    pallas_call x4 -> x5, Pallas kernels: 44.9 us -> 46.4 us  [the longest x4 39.4 us: expert_blocks(): pl.pallas_call(functools.partial(expert_kernel, count, gates.shape[0], wi...]
  transfers between devices with their start and end apart: 31 -> 31, of which waited for: 9 -> 10; matrix products, arithmetic and copies ran while one was open for 6% -> 7% of each run, Pallas kernels for 31% -> 28%
where the time goes in v1:
time: 232 us
  waiting for transfers between devices  91.5 us (39%)
  Pallas kernels  83.4 us (36%)
  starting transfers between devices  36.9 us (16%)
  other arithmetic  11.7 us (5%)
  local copies, waits for them, and re-layouts  7.06 us (3%)
    pallas_call x4, Pallas kernels, expert_blocks(): pl.pallas_call(functools.partial(expert_kernel, count, gates.shape[0], wi...  39.4 us
    ppermute x3, waiting for transfers between devices, layer(): pieces.append(lax.ppermute(narrow(both)[None], 'dp', pairs))  26.3 us
    pallas_call x3, Pallas kernels, weight_parts(): pl.pallas_call(functools.partial(weight_kernel, x_rows, p_rows, start, de...  25.1 us
    ppermute x4, waiting for transfers between devices, layer(): from_right = lax.ppermute(to_left, 'expert', backward).astype(jnp.float32)  24.4 us
    all_to_all x1, waiting for transfers between devices, layer(): lax.all_to_all(dense_gates, 'expert', split_axis=1, concat_axis=0, tiled=...  14.4 us
    ppermute x4, waiting for transfers between devices, layer(): xr = lax.ppermute(right[0], 'expert', backward)  14.2 us
    pallas_call x3, Pallas kernels, place_chunk(): pl.pallas_call(functools.partial(place_kernel, len(pieces)), out_shape=ja...  12 us
    ppermute x4, waiting for transfers between devices, layer(): right = (xr, lax.ppermute(right[1], 'expert', backward))  10.9 us
  transfers between devices with their start and end apart: 31, of which 10 were waited for; matrix products, arithmetic and copies ran while one was open for 7% of the time, Pallas kernels for 28%

profile of v1, /device:TPU:0, one launch (start us, length us, event | category | flops | bytes accessed | tf_op | source)
XLA Modules:
  0.0 231.6 jit_solution(9535817871233354039)
XLA Ops:
  0.6 3.0 %collective-permute-start.3 = (bf16[128,2048]{1,0:T(8,128)(2,1)}, bf16[128,2048]{1,0:T(8,128)(2,1)S(1)}, u32[]{:S(2)}, u32[]{:S(2)}) collective-permute-start(bf16[128,2048]{1,0:T(8,128)(2,1)} %refs_0_.6), channel_id=1, source_target_pairs={{2,0},{4,2},{6,4},{7,6},{5,7},{3,5},{1,3},{0,1},{10,8},{12,10},{14... | collective-permute-start | bytes 1572872 | tf_op jit(solution)/shard_map/ppermute | solution.py:299
  3.8 1.9 collective-permute-start.1
  5.8 10.9 %collective-permute-done.3.refs_5_.refs_2_ = bf16[128,2048]{1,0:T(8,128)(2,1)S(1)} collective-permute-done((bf16[128,2048]{1,0:T(8,128)(2,1)}, bf16[128,2048]{1,0:T(8,128)(2,1)S(1)}, u32[]{:S(2)}, u32[]{:S(2)}) %collective-permute-start.3) | collective-permute-done | bytes 524320 | tf_op jit(solution)/shard_map/ppermute | solution.py:299
  16.7 1.9 collective-permute-start.7
  18.8 9.1 %collective-permute-done.1.refs_2_ = bf16[128,2048]{1,0:T(8,128)(2,1)S(1)} collective-permute-done((bf16[128,2048]{1,0:T(8,128)(2,1)}, bf16[128,2048]{1,0:T(8,128)(2,1)S(1)}, u32[]{:S(2)}, u32[]{:S(2)}) %collective-permute-start.1) | collective-permute-done | bytes 524320 | tf_op jit(solution)/shard_map/ppermute | solution.py:297
  28.0 1.9 collective-permute-start.5
  32.1 6.1 %all-to-all-start = ((bf16[128,8,2]{0,2,1:T(2,128)(2,1)}), bf16[128,8,2]{0,2,1:T(2,128)(2,1)S(1)}, u32[]{:S(2)}, u32[]{:S(2)}) async-start(bf16[128,8,2]{0,2,1:T(2,128)(2,1)} %bitcast.1), calls=%async_computation | async-start | bytes 8192 | tf_op jit(solution)/shard_map/all_to_all | solution.py:284
  39.6 14.4 %all-to-all-done = bf16[128,8,2]{0,2,1:T(2,128)(2,1)S(1)} async-done(((bf16[128,8,2]{0,2,1:T(2,128)(2,1)}), bf16[128,8,2]{0,2,1:T(2,128)(2,1)S(1)}, u32[]{:S(2)}, u32[]{:S(2)}) %all-to-all-start) | async-done | bytes 4128 | tf_op jit(solution)/shard_map/all_to_all | solution.py:284
  59.0 14.2 %experts.4 = (bf16[2,384,768]{2,1,0:T(8,128)(2,1)}, bf16[2,384,384]{2,1,0:T(8,128)(2,1)}, bf16[128,2176]{1,0:T(8,128)(2,1)}, bf16[128,2176]{1,0:T(8,128)(2,1)}, bf16[128,2176]{1,0:T(8,128)(2,1)}) custom-call(s32[9]{0:T(128)} %pad_add_fusion.scalars, bf16[128,2048]{1,0:T(8,128)(2,1)} %refs_0_.7, bf16[128,2048]{1,0:T(8,128)(2,1)} %copy-done.23, ...), custom_call_target="tpu_custom_call" | custom-call | flops 6039797760 | bytes 15728640 | tf_op jit(solution)/shard_map/experts/pallas_call | solution.py:126
  76.2 5.0 %collective-permute-done.9.refs_1_.refs_6_ = bf16[128,2048]{1,0:T(8,128)(2,1)S(1)} collective-permute-done((bf16[128,2048]{1,0:T(8,128)(2,1)}, bf16[128,2048]{1,0:T(8,128)(2,1)S(1)}, u32[]{:S(2)}, u32[]{:S(2)}) %collective-permute-start.9) | collective-permute-done | bytes 524320 | tf_op jit(solution)/shard_map/ppermute | solution.py:297
  84.7 10.9 %experts.5 = (bf16[2,256,768]{2,1,0:T(8,128)(2,1)}, bf16[2,256,384]{2,1,0:T(8,128)(2,1)}, bf16[128,2176]{1,0:T(8,128)(2,1)}, bf16[128,2176]{1,0:T(8,128)(2,1)}) custom-call(s32[9]{0:T(128)} %pad_add_fusion.scalars, bf16[128,2048]{1,0:T(8,128)(2,1)} %collective-permute-done.4.refs_0_.refs_3_, bf16[128,2048]{1,0:T(8,128)(2,1)} %collective-permute-done.5.refs_1_.refs_4_, ...), custom_call_target="tpu_custom_call" | custom-call | flops 4026531840 | bytes 13631488 | tf_op jit(solution)/shard_map/experts/pallas_call | solution.py:126
  95.7 7.7 %experts.6 = (bf16[2,256,768]{2,1,0:T(8,128)(2,1)}, bf16[2,256,384]{2,1,0:T(8,128)(2,1)}, f32[2,256,128]{2,1,0:T(8,128)}) custom-call(s32[9]{0:T(128)} %pad_add_fusion.scalars, bf16[128,2048]{1,0:T(8,128)(2,1)} %copy-done.6, bf16[128,2048]{1,0:T(8,128)(2,1)} %copy-done.5, bf16[128,2048]{1,0:T(8,128)(2,1)} %copy-done.8, bf16[128,2048]{1,0:T(8,128)(2,1)} %copy-done.7, ...), custom_call_target="tpu_custom_call" | custom-call | flops 2415919104 | bytes 13631488 | tf_op jit(solution)/shard_map/experts/pallas_call | solution.py:126
  105.0 6.5 %experts.7 = (bf16[2,128,768]{2,1,0:T(8,128)(2,1)}, bf16[2,128,384]{2,1,0:T(8,128)(2,1)}, f32[2,128,128]{2,1,0:T(8,128)}) custom-call(s32[9]{0:T(128)} %pad_add_fusion.scalars, bf16[64,2048]{1,0:T(8,128)(2,1)} %copy-done.18, bf16[64,2048]{1,0:T(8,128)(2,1)} %copy-done.17, bf16[64,2048]{1,0:T(8,128)(2,1)} %copy-done.20, bf16[64,2048]{1,0:T(8,128)(2,1)} %copy-done.19, ...), custom_call_target="tpu_custom_call" | custom-call | flops 1207959552 | bytes 11534336 | tf_op jit(solution)/shard_map/experts/pallas_call | solution.py:126
  111.5 7.0 %rows.1 = (bf16[128,2176]{1,0:T(8,128)(2,1)}, bf16[128,2176]{1,0:T(8,128)(2,1)}, bf16[64,2176]{1,0:T(8,128)(2,1)}, bf16[64,2176]{1,0:T(8,128)(2,1)}) custom-call(bf16[2,256,768]{2,1,0:T(8,128)(2,1)} %get-tuple-element.31.refs_0_.refs_11_, bf16[2,128,768]{2,1,0:T(8,128)(2,1)} %get-tuple-element.32.refs_1_.refs_12_, f32[2,256,128]{2,1,0:T(8,128)} %get-tuple-element.33.refs_2_, ...), custom_call_target="tpu_custom_call" | custom-call | flops 2415919104 | bytes 9437184 | tf_op jit(solution)/shard_map/rows/pallas_call | solution.py:90
  120.6 9.1 %weights.4 = (bf16[2,512,768]{2,1,0:T(8,128)(2,1)}, bf16[2,512,768]{2,1,0:T(8,128)(2,1)}) custom-call(bf16[128,2048]{1,0:T(8,128)(2,1)} %refs_0_.6, bf16[128,2048]{1,0:T(8,128)(2,1)} %copy-done.25, bf16[128,2048]{1,0:T(8,128)(2,1)} %copy-done.24, bf16[128,2048]{1,0:T(8,128)(2,1)} %collective-permute-done.6.refs_2_.refs_3_, ...), custom_call_target="tpu_custom_call" | custom-call | flops 3221225472 | bytes 8912896 | tf_op jit(solution)/shard_map/weights/pallas_call | solution.py:217
  129.8 6.5 %weights.5 = (bf16[2,512,512]{2,1,0:T(8,128)(2,1)}, bf16[2,512,512]{2,1,0:T(8,128)(2,1)}) custom-call(bf16[128,2048]{1,0:T(8,128)(2,1)} %refs_0_.7, bf16[128,2048]{1,0:T(8,128)(2,1)} %copy-done.23, bf16[128,2048]{1,0:T(8,128)(2,1)} %copy-done.22, bf16[128,2048]{1,0:T(8,128)(2,1)} %collective-permute-done.4.refs_0_.refs_3_, ...), custom_call_target="tpu_custom_call" | custom-call | flops 2147483648 | bytes 7340032 | tf_op jit(solution)/shard_map/weights/pallas_call | solution.py:217
  136.9 9.4 %weights.3 = (bf16[2,512,1024]{2,1,0:T(8,128)(2,1)}, bf16[2,512,1024]{2,1,0:T(8,128)(2,1)}) custom-call(bf16[128,2048]{1,0:T(8,128)(2,1)} %refs_0_.7, bf16[128,2048]{1,0:T(8,128)(2,1)} %copy-done.23, bf16[128,2048]{1,0:T(8,128)(2,1)} %copy-done.22, bf16[128,2048]{1,0:T(8,128)(2,1)} %collective-permute-done.4.refs_0_.refs_3_, ...), custom_call_target="tpu_custom_call" | custom-call | flops 4294967296 | bytes 10485760 | tf_op jit(solution)/shard_map/weights/pallas_call | solution.py:217
  149.7 12.8 %collective-permute-done.17 = bf16[128,2176]{1,0:T(8,128)(2,1)S(1)} collective-permute-done((bf16[128,2176]{1,0:T(8,128)(2,1)S(1)}, bf16[128,2176]{1,0:T(8,128)(2,1)S(1)}, u32[]{:S(2)}, u32[]{:S(2)}) %collective-permute-start.17) | collective-permute-done | bytes 557088 | tf_op jit(solution)/shard_map/ppermute | solution.py:323
  166.7 10.1 %collective-permute-done.18 = bf16[128,2176]{1,0:T(8,128)(2,1)S(1)} collective-permute-done((bf16[128,2176]{1,0:T(8,128)(2,1)S(1)}, bf16[128,2176]{1,0:T(8,128)(2,1)S(1)}, u32[]{:S(2)}, u32[]{:S(2)}) %collective-permute-start.18) | collective-permute-done | bytes 557088 | tf_op jit(solution)/shard_map/ppermute | solution.py:323
  180.7 3.5 %place.3.refs_3_ = bf16[512,2,1152]{2,1,0:T(2,128)(2,1)} custom-call(bf16[2,512,512]{2,1,0:T(8,128)(2,1)} %get-tuple-element.51.refs_0_, bf16[2,512,512]{2,1,0:T(8,128)(2,1)} %copy-done.4, bf16[1,512,512]{2,1,0:T(8,128)(2,1)} %collective-permute-done.29.refs_2_), custom_call_target="tpu_custom_call" | custom-call | tf_op jit(solution)/shard_map/place/pallas_call | solution.py:257
  195.7 10.7 %collective-permute-done.27.refs_2_ = bf16[1,512,768]{2,1,0:T(8,128)(2,1)} collective-permute-done((bf16[1,512,768]{2,1,0:T(8,128)(2,1)}, bf16[1,512,768]{2,1,0:T(8,128)(2,1)}, u32[]{:S(2)}, u32[]{:S(2)}) %collective-permute-start.27) | collective-permute-done | bytes 786464 | tf_op jit(solution)/shard_map/ppermute | solution.py:359
  206.4 4.0 %place.4.refs_3_ = bf16[512,2,1152]{2,1,0:T(2,128)(2,1)} custom-call(bf16[2,512,768]{2,1,0:T(8,128)(2,1)} %get-tuple-element.49.refs_0_, bf16[2,512,768]{2,1,0:T(8,128)(2,1)} %copy-done.2, bf16[1,512,768]{2,1,0:T(8,128)(2,1)} %collective-permute-done.27.refs_2_, bf16[512,2,1152]{2,1,0:T(2,128)(2,1)} %place.3.refs_3_), custom_call_target="tpu_custom_call", output_to_operand_aliasing={{}: (3, {})} | custom-call | tf_op jit(solution)/shard_map/place/pallas_call | solution.py:257
  210.4 15.6 %collective-permute-done.25.refs_2_ = bf16[1,512,1024]{2,1,0:T(8,128)(2,1)S(1)} collective-permute-done((bf16[1,512,1024]{2,1,0:T(8,128)(2,1)S(1)}, bf16[1,512,1024]{2,1,0:T(8,128)(2,1)S(1)}, u32[]{:S(2)}, u32[]{:S(2)}) %collective-permute-start.25) | collective-permute-done | bytes 1048608 | tf_op jit(solution)/shard_map/ppermute | solution.py:359
  227.0 4.5 %place.5 = bf16[512,2,1152]{2,1,0:T(2,128)(2,1)} custom-call(bf16[2,512,1024]{2,1,0:T(8,128)(2,1)} %get-tuple-element.43.refs_0_, bf16[2,512,1024]{2,1,0:T(8,128)(2,1)} %collective-permute-done.24.refs_1_, bf16[1,512,1024]{2,1,0:T(8,128)(2,1)} %copy-done.9, bf16[512,2,1152]{2,1,0:T(2,128)(2,1)} %place.4.refs_3_), custom_call_target="tpu_custom_call", output_to_operand_aliasing={{}: (3, {})} | custom-call | tf_op jit(solution)/shard_map/place/pallas_call | solution.py:257
  (125 shorter events, 43.5 us)
Async XLA Ops:
  0.6 16.1 %collective-permute-start.3 = (bf16[128,2048]{1,0:T(8,128)(2,1)}, bf16[128,2048]{1,0:T(8,128)(2,1)S(1)}, u32[]{:S(2)}, u32[]{:S(2)}) collective-permute-start(bf16[128,2048]{1,0:T(8,128)(2,1)} %refs_0_.6), channel_id=1, source_target_pairs={{2,0},{4,2},{6,4},{7,6},{5,7},{3,5},{1,3},{0,1},{10,8},{12,10},{14... | collective-permute-start | bytes 1572872 | tf_op jit(solution)/shard_map/ppermute | solution.py:299
  3.8 24.2 %collective-permute-start.1 = (bf16[128,2048]{1,0:T(8,128)(2,1)}, bf16[128,2048]{1,0:T(8,128)(2,1)S(1)}, u32[]{:S(2)}, u32[]{:S(2)}) collective-permute-start(bf16[128,2048]{1,0:T(8,128)(2,1)} %refs_0_.7), channel_id=1, source_target_pairs={{2,0},{4,2},{6,4},{7,6},{5,7},{3,5},{1,3},{0,1},{10,8},{12,10},{14... | collective-permute-start | bytes 1572872 | tf_op jit(solution)/shard_map/ppermute | solution.py:297
  5.7 24.2 %collective-permute-start = (bf16[128,2048]{1,0:T(8,128)(2,1)}, bf16[128,2048]{1,0:T(8,128)(2,1)S(1)}, u32[]{:S(2)}, u32[]{:S(2)}) collective-permute-start(bf16[128,2048]{1,0:T(8,128)(2,1)} %refs_0_.7), channel_id=1, source_target_pairs={{0,2},{2,4},{4,6},{6,7},{7,5},{5,3},{3,1},{1,0},{8,10},{10,12},{12... | collective-permute-start | bytes 1572872 | tf_op jit(solution)/shard_map/ppermute | solution.py:296
  16.7 38.2 %collective-permute-start.7 = (bf16[128,2048]{1,0:T(8,128)(2,1)S(1)}, bf16[128,2048]{1,0:T(8,128)(2,1)}, u32[]{:S(2)}, u32[]{:S(2)}) collective-permute-start(bf16[128,2048]{1,0:T(8,128)(2,1)S(1)} %collective-permute-done.3.refs_5_.refs_2_), channel_id=1, source_target_pairs={{2,0},{4,2},{6,4},{7,6},{5,7},{3,5},{1,3},{0,1},{10,8},{12,10},{14... | collective-permute-start | bytes 1572872 | tf_op jit(solution)/shard_map/ppermute | solution.py:299
  18.7 36.8 %collective-permute-start.6 = (bf16[128,2048]{1,0:T(8,128)(2,1)S(1)}, bf16[128,2048]{1,0:T(8,128)(2,1)}, u32[]{:S(2)}, u32[]{:S(2)}) collective-permute-start(bf16[128,2048]{1,0:T(8,128)(2,1)S(1)} %collective-permute-done.2.refs_4_.refs_1_), channel_id=1, source_target_pairs={{0,2},{2,4},{4,6},{6,7},{7,5},{5,3},{3,1},{1,0},{8,10},{10,12},{12... | collective-permute-start | bytes 1572872 | tf_op jit(solution)/shard_map/ppermute | solution.py:298
  28.0 29.0 %collective-permute-start.5 = (bf16[128,2048]{1,0:T(8,128)(2,1)S(1)}, bf16[128,2048]{1,0:T(8,128)(2,1)}, u32[]{:S(2)}, u32[]{:S(2)}) collective-permute-start(bf16[128,2048]{1,0:T(8,128)(2,1)S(1)} %collective-permute-done.1.refs_2_), channel_id=1, source_target_pairs={{2,0},{4,2},{6,4},{7,6},{5,7},{3,5},{1,3},{0,1},{10,8},{12,10},{14... | collective-permute-start | bytes 1572872 | tf_op jit(solution)/shard_map/ppermute | solution.py:297
  29.9 27.6 %collective-permute-start.4 = (bf16[128,2048]{1,0:T(8,128)(2,1)S(1)}, bf16[128,2048]{1,0:T(8,128)(2,1)}, u32[]{:S(2)}, u32[]{:S(2)}) collective-permute-start(bf16[128,2048]{1,0:T(8,128)(2,1)S(1)} %collective-permute-done.refs_1_), channel_id=1, source_target_pairs={{0,2},{2,4},{4,6},{6,7},{7,5},{5,3},{3,1},{1,0},{8,10},{10,12},{12... | collective-permute-start | bytes 1572872 | tf_op jit(solution)/shard_map/ppermute | solution.py:296
  32.1 22.0 %all-to-all-start = ((bf16[128,8,2]{0,2,1:T(2,128)(2,1)}), bf16[128,8,2]{0,2,1:T(2,128)(2,1)S(1)}, u32[]{:S(2)}, u32[]{:S(2)}) async-start(bf16[128,8,2]{0,2,1:T(2,128)(2,1)} %bitcast.1), calls=%async_computation | async-start | bytes 8192 | tf_op jit(solution)/shard_map/all_to_all | solution.py:284
  54.9 18.3 %collective-permute-start.11 = (bf16[128,2048]{1,0:T(8,128)(2,1)}, bf16[128,2048]{1,0:T(8,128)(2,1)S(1)}, u32[]{:S(2)}, u32[]{:S(2)}) collective-permute-start(bf16[128,2048]{1,0:T(8,128)(2,1)} %collective-permute-done.7.refs_3_.refs_4_), channel_id=1, source_target_pairs={{2,0},{4,2},{6,4},{7,6},{5,7},{3,5},{1,3},{0,1},{10,8},{12,10},{14... | collective-permute-start | bytes 1572872 | tf_op jit(solution)/shard_map/ppermute | solution.py:299
  55.5 18.4 %collective-permute-start.10 = (bf16[128,2048]{1,0:T(8,128)(2,1)}, bf16[128,2048]{1,0:T(8,128)(2,1)S(1)}, u32[]{:S(2)}, u32[]{:S(2)}) collective-permute-start(bf16[128,2048]{1,0:T(8,128)(2,1)} %collective-permute-done.6.refs_2_.refs_3_), channel_id=1, source_target_pairs={{0,2},{2,4},{4,6},{6,7},{7,5},{5,3},{3,1},{1,0},{8,10},{10,12},{12... | collective-permute-start | bytes 1572872 | tf_op jit(solution)/shard_map/ppermute | solution.py:298
  57.0 24.2 %collective-permute-start.9 = (bf16[128,2048]{1,0:T(8,128)(2,1)}, bf16[128,2048]{1,0:T(8,128)(2,1)S(1)}, u32[]{:S(2)}, u32[]{:S(2)}) collective-permute-start(bf16[128,2048]{1,0:T(8,128)(2,1)} %collective-permute-done.5.refs_1_.refs_4_), channel_id=1, source_target_pairs={{2,0},{4,2},{6,4},{7,6},{5,7},{3,5},{1,3},{0,1},{10,8},{12,10},{14... | collective-permute-start | bytes 1572872 | tf_op jit(solution)/shard_map/ppermute | solution.py:297
  57.5 25.0 %collective-permute-start.8 = (bf16[128,2048]{1,0:T(8,128)(2,1)}, bf16[128,2048]{1,0:T(8,128)(2,1)S(1)}, u32[]{:S(2)}, u32[]{:S(2)}) collective-permute-start(bf16[128,2048]{1,0:T(8,128)(2,1)} %collective-permute-done.4.refs_0_.refs_3_), channel_id=1, source_target_pairs={{0,2},{2,4},{4,6},{6,7},{7,5},{5,3},{3,1},{1,0},{8,10},{10,12},{12... | collective-permute-start | bytes 1572872 | tf_op jit(solution)/shard_map/ppermute | solution.py:296
  73.3 30.1 %collective-permute-start.15 = (bf16[64,2048]{1,0:T(8,128)(2,1)S(1)}, bf16[64,2048]{1,0:T(8,128)(2,1)S(1)}, u32[]{:S(2)}, u32[]{:S(2)}) collective-permute-start(bf16[64,2048]{1,0:T(8,128)(2,1)S(1)} %slice.51), channel_id=1, source_target_pairs={{2,0},{4,2},{6,4},{7,6},{5,7},{3,5},{1,3},{0,1},{10,8},{12,10},{14... | collective-permute-start | bytes 786440 | tf_op jit(solution)/shard_map/ppermute | solution.py:299
  74.7 28.7 %collective-permute-start.14 = (bf16[64,2048]{1,0:T(8,128)(2,1)}, bf16[64,2048]{1,0:T(8,128)(2,1)S(1)}, u32[]{:S(2)}, u32[]{:S(2)}) collective-permute-start(bf16[64,2048]{1,0:T(8,128)(2,1)} %slice.50), channel_id=1, source_target_pairs={{0,2},{2,4},{4,6},{6,7},{7,5},{5,3},{3,1},{1,0},{8,10},{10,12},{12... | collective-permute-start | bytes 786440 | tf_op jit(solution)/shard_map/ppermute | solution.py:298
  82.0 21.5 %collective-permute-start.13 = (bf16[64,2048]{1,0:T(8,128)(2,1)}, bf16[64,2048]{1,0:T(8,128)(2,1)S(1)}, u32[]{:S(2)}, u32[]{:S(2)}) collective-permute-start(bf16[64,2048]{1,0:T(8,128)(2,1)} %slice.49), channel_id=1, source_target_pairs={{2,0},{4,2},{6,4},{7,6},{5,7},{3,5},{1,3},{0,1},{10,8},{12,10},{14... | collective-permute-start | bytes 786440 | tf_op jit(solution)/shard_map/ppermute | solution.py:297
  83.3 20.2 %collective-permute-start.12 = (bf16[64,2048]{1,0:T(8,128)(2,1)}, bf16[64,2048]{1,0:T(8,128)(2,1)S(1)}, u32[]{:S(2)}, u32[]{:S(2)}) collective-permute-start(bf16[64,2048]{1,0:T(8,128)(2,1)} %slice.48), channel_id=1, source_target_pairs={{0,2},{2,4},{4,6},{6,7},{7,5},{5,3},{3,1},{1,0},{8,10},{10,12},{12... | collective-permute-start | bytes 786440 | tf_op jit(solution)/shard_map/ppermute | solution.py:296
  118.5 27.9 %collective-permute-start.16 = (bf16[64,2176]{1,0:T(8,128)(2,1)}, bf16[64,2176]{1,0:T(8,128)(2,1)}, u32[]{:S(2)}, u32[]{:S(2)}) collective-permute-start(bf16[64,2176]{1,0:T(8,128)(2,1)} %get-tuple-element.36), channel_id=1, source_target_pairs={{2,0},{4,2},{6,4},{7,6},{5,7},{3,5},{1,3},{0,1},{10,8},{12,10},{14... | collective-permute-start | bytes 835592 | tf_op jit(solution)/shard_map/ppermute | solution.py:323
  119.1 29.0 %collective-permute-start.20 = (bf16[64,2176]{1,0:T(8,128)(2,1)}, bf16[64,2176]{1,0:T(8,128)(2,1)S(1)}, u32[]{:S(2)}, u32[]{:S(2)}) collective-permute-start(bf16[64,2176]{1,0:T(8,128)(2,1)} %get-tuple-element.40), channel_id=1, source_target_pairs={{0,2},{2,4},{4,6},{6,7},{7,5},{5,3},{3,1},{1,0},{8,10},{10,12},{12... | collective-permute-start | bytes 835592 | tf_op jit(solution)/shard_map/ppermute | solution.py:324
  129.7 54.5 %collective-permute-start.26 = (bf16[2,512,768]{2,1,0:T(8,128)(2,1)}, bf16[2,512,768]{2,1,0:T(8,128)(2,1)S(1)}, u32[]{:S(2)}, u32[]{:S(2)}) collective-permute-start(bf16[2,512,768]{2,1,0:T(8,128)(2,1)} %get-tuple-element.50), channel_id=1, source_target_pairs={{0,8},{8,0},{16,24},{24,16},{1,9},{9,1},{17,25},{25,17},{2,10},{10... | collective-permute-start | bytes 4718600 | tf_op jit(solution)/shard_map/ppermute | solution.py:352
  136.3 28.6 %collective-permute-start.28 = (bf16[2,512,512]{2,1,0:T(8,128)(2,1)}, bf16[2,512,512]{2,1,0:T(8,128)(2,1)S(1)}, u32[]{:S(2)}, u32[]{:S(2)}) collective-permute-start(bf16[2,512,512]{2,1,0:T(8,128)(2,1)} %get-tuple-element.52), channel_id=1, source_target_pairs={{0,8},{8,0},{16,24},{24,16},{1,9},{9,1},{17,25},{25,17},{2,10},{10... | collective-permute-start | bytes 3145736 | tf_op jit(solution)/shard_map/ppermute | solution.py:352
  146.3 40.9 %collective-permute-start.24 = (bf16[2,512,1024]{2,1,0:T(8,128)(2,1)}, bf16[2,512,1024]{2,1,0:T(8,128)(2,1)}, u32[]{:S(2)}, u32[]{:S(2)}) collective-permute-start(bf16[2,512,1024]{2,1,0:T(8,128)(2,1)} %get-tuple-element.44), channel_id=1, source_target_pairs={{0,8},{8,0},{16,24},{24,16},{1,9},{9,1},{17,25},{25,17},{2,10},{10... | collective-permute-start | bytes 6291464 | tf_op jit(solution)/shard_map/ppermute | solution.py:352
  165.1 15.6 %collective-permute-start.29 = (bf16[1,512,512]{2,1,0:T(8,128)(2,1)S(1)}, bf16[1,512,512]{2,1,0:T(8,128)(2,1)}, u32[]{:S(2)}, u32[]{:S(2)}) collective-permute-start(bf16[1,512,512]{2,1,0:T(8,128)(2,1)S(1)} %add_convert_fusion.9), channel_id=1, source_target_pairs={{0,16},{8,24},{16,0},{24,8},{1,17},{9,25},{17,1},{25,9},{2,18},{10... | collective-permute-start | bytes 1572872 | tf_op jit(solution)/shard_map/ppermute | solution.py:359
  185.7 20.7 %collective-permute-start.27 = (bf16[1,512,768]{2,1,0:T(8,128)(2,1)}, bf16[1,512,768]{2,1,0:T(8,128)(2,1)}, u32[]{:S(2)}, u32[]{:S(2)}) collective-permute-start(bf16[1,512,768]{2,1,0:T(8,128)(2,1)} %add_convert_fusion.1), channel_id=1, source_target_pairs={{0,16},{8,24},{16,0},{24,8},{1,17},{9,25},{17,1},{25,9},{2,18},{10... | collective-permute-start | bytes 2359304 | tf_op jit(solution)/shard_map/ppermute | solution.py:359
  188.9 37.2 %collective-permute-start.25 = (bf16[1,512,1024]{2,1,0:T(8,128)(2,1)S(1)}, bf16[1,512,1024]{2,1,0:T(8,128)(2,1)S(1)}, u32[]{:S(2)}, u32[]{:S(2)}) collective-permute-start(bf16[1,512,1024]{2,1,0:T(8,128)(2,1)S(1)} %add_convert_fusion), channel_id=1, source_target_pairs={{0,16},{8,24},{16,0},{24,8},{1,17},{9,25},{17,1},{25,9},{2,18},{10... | collective-permute-start | bytes 3145736 | tf_op jit(solution)/shard_map/ppermute | solution.py:359
  (33 other events, 412.7 us)

commit v2 on v1

--- a/solution.py
+++ b/solution.py
@@ -35,9 +35,11 @@
     @pl.when(e == last)
     def _():
         at = 0
-        for ref in row_refs:
-            ref[...] = total[at : at + ref.shape[0]].astype(jnp.bfloat16)
-            at += ref.shape[0]
+        for left, right in zip(row_refs[::2], row_refs[1::2]):
+            span, split = slice(at, at + left.shape[0]), left.shape[1]
+            left[...] = total[span, :split].astype(jnp.bfloat16)
+            right[...] = total[span, split:].astype(jnp.bfloat16)
+            at += left.shape[0]
 
 
 def times_transposed(left, right):
@@ -86,13 +88,14 @@
 def row_blocks(pres, tails, sizes, weight_in):
     experts, width, wide = weight_in.shape
     rows, full = sum(sizes), width + tails[0].shape[2]
+    halves = (width // 2, full - width // 2)
     per_expert = lambda a: pl.BlockSpec((1,) + a.shape[1:], lambda e: (e, 0, 0))
     return pl.pallas_call(
         functools.partial(row_kernel, len(pres)),
-        out_shape=[jax.ShapeDtypeStruct((n, full), jnp.bfloat16) for n in sizes],
+        out_shape=[jax.ShapeDtypeStruct((n, w), jnp.bfloat16) for n in sizes for w in halves],
         grid=(experts,),
         in_specs=[per_expert(a) for a in [*pres, *tails, weight_in]],
-        out_specs=[pl.BlockSpec((n, full), lambda e: (0, 0)) for n in sizes],
+        out_specs=[pl.BlockSpec((n, w), lambda e: (0, 0)) for n in sizes for w in halves],
         scratch_shapes=[pltpu.VMEM((rows, full), jnp.float32)],
         cost_estimate=pl.CostEstimate(
             flops=2 * rows * experts * width * wide,
@@ -117,8 +120,9 @@
 
     per_expert = lambda a, b: pl.BlockSpec((1, a, b), lambda e, s: (e, 0, 0))
     if with_rows:
-        more = [jax.ShapeDtypeStruct((n, width + extra), jnp.bfloat16) for n in sizes]
-        more_specs = [whole(n, width + extra) for n in sizes]
+        pieces = [(n, w) for n in sizes for w in (width // 2, width - width // 2 + extra)]
+        more = [jax.ShapeDtypeStruct(p, jnp.bfloat16) for p in pieces]
+        more_specs = [whole(*p) for p in pieces]
         scratch = [pltpu.VMEM((rows, width + extra), jnp.float32)]
     else:
         more = [jax.ShapeDtypeStruct((experts, rows, extra), jnp.float32)]
@@ -318,20 +322,24 @@
     )
 
     narrow = lambda a: a.astype(jnp.bfloat16)
-    to_left, to_right = partial_rows[-2], partial_rows[-1]
-    for step in range(half - 1, -1, -1):
-        from_right = lax.ppermute(to_left, "expert", backward).astype(jnp.float32)
-        from_left = lax.ppermute(to_right, "expert", forward).astype(jnp.float32)
-        if step == half - 1:
-            pad = jnp.zeros((mid, from_left.shape[1]), jnp.float32)
-            from_right = jnp.concatenate([from_right, pad])
-            from_left = jnp.concatenate([pad, from_left])
-        if step > 0:
-            to_left = narrow(partial_rows[2 * step - 1].astype(jnp.float32) + from_right)
-            to_right = narrow(partial_rows[2 * step].astype(jnp.float32) + from_left)
-    returned = narrow(partial_rows[0].astype(jnp.float32) + from_right + from_left)
-    grad_tokens = returned[:, :width]
-    probs = returned[:, width : width + expert_count].astype(jnp.float32)
+    returned = []
+    for stream in range(2):
+        mine = [r.astype(jnp.float32) for r in partial_rows[stream::2]]
+        to_left, to_right = partial_rows[stream - 4], partial_rows[stream - 2]
+        for step in range(half - 1, -1, -1):
+            from_right = lax.ppermute(to_left, "expert", backward).astype(jnp.float32)
+            from_left = lax.ppermute(to_right, "expert", forward).astype(jnp.float32)
+            if step == half - 1:
+                pad = jnp.zeros((mid, from_left.shape[1]), jnp.float32)
+                from_right = jnp.concatenate([from_right, pad])
+                from_left = jnp.concatenate([pad, from_left])
+            if step > 0:
+                to_left = narrow(mine[2 * step - 1] + from_right)
+                to_right = narrow(mine[2 * step] + from_left)
+        returned.append(narrow(mine[0] + from_right + from_left))
+    split = returned[0].shape[1]
+    grad_tokens = jnp.concatenate([returned[0], returned[1][:, : width - split]], axis=1)
+    probs = returned[1][:, width - split :][:, :expert_count].astype(jnp.float32)
     grad_probs = narrow(jnp.sum(jnp.where(onehot, probs[:, None, :], 0.0), axis=2))
 
     replicas = lax.axis_size("dp")
@@ -341,8 +349,8 @@
     pres, hiddens = [r[0] for r in results], [r[1] for r in results]
     units = down_weight.shape[1]
     third = 2 * units // 3
-    chunks = [(xs, pres, 2 * third, third), (gs, hiddens, 0, units), (xs, pres, 0, 2 * third)]
-    places = [2, 2, 0]
+    chunks = [(xs, pres, 0, 2 * third), (gs, hiddens, 0, units), (xs, pres, 2 * third, third)]
+    places = [0, 2, 2]
     parts = []
     for chunk in chunks:
         parts += weight_parts(*chunk, replicas)

time: 232 us -> 250 us (1.078)
  waiting for transfers between devices: 91.5 us -> 102 us
  starting transfers between devices: 36.9 us -> 41.6 us
    ppermute x3, waiting for transfers between devices: 26.3 us -> 34.9 us  [layer(): pieces.append(lax.ppermute(narrow(both)[None], 'dp', pairs))]
    ppermute x4 -> x8, waiting for transfers between devices: 1.25 us -> 7.67 us  [layer(): from_left = lax.ppermute(to_right, 'expert', forward).astype(jnp.float32)]
    ppermute x4 -> x8, waiting for transfers between devices: 24.4 us -> 19.5 us  [layer(): from_right = lax.ppermute(to_left, 'expert', backward).astype(jnp.float32)]
    ppermute x4 -> x8, starting transfers between devices: 2.32 us -> 6.47 us  [layer(): from_right = lax.ppermute(to_left, 'expert', backward).astype(jnp.float32)]
    ppermute x4 -> x8, starting transfers between devices: 5.99 us -> 7.28 us  [layer(): from_left = lax.ppermute(to_right, 'expert', forward).astype(jnp.float32)]
    convert_element_type x10 -> x17, other arithmetic: 7.64 us -> 8.64 us  [layer(): narrow = lambda a: a.astype(jnp.bfloat16)]
  transfers between devices with their start and end apart: 31 -> 39, of which waited for: 10 -> 13; matrix products, arithmetic and copies ran while one was open for 7% -> 7% of each run, Pallas kernels for 28% -> 27%
where the time goes in v2:
time: 250 us; the launch traced here: 249 us
  waiting for transfers between devices  102 us (41%)
  Pallas kernels  83.5 us (33%)
  starting transfers between devices  41.6 us (17%)
  other arithmetic  13.5 us (5%)
  local copies, waits for them, and re-layouts  7.95 us (3%)
    pallas_call x4, Pallas kernels, expert_blocks(): pl.pallas_call(functools.partial(expert_kernel, count, gates.shape[0], wi...  39.4 us
    ppermute x3, waiting for transfers between devices, layer(): pieces.append(lax.ppermute(narrow(both)[None], 'dp', pairs))  34.9 us
    pallas_call x3, Pallas kernels, weight_parts(): pl.pallas_call(functools.partial(weight_kernel, x_rows, p_rows, start, de...  25.1 us
    ppermute x8, waiting for transfers between devices, layer(): from_right = lax.ppermute(to_left, 'expert', backward).astype(jnp.float32)  19.5 us
    all_to_all x1, waiting for transfers between devices, layer(): lax.all_to_all(dense_gates, 'expert', split_axis=1, concat_axis=0, tiled=...  14.5 us
    ppermute x4, waiting for transfers between devices, layer(): xr = lax.ppermute(right[0], 'expert', backward)  14.2 us
    pallas_call x3, Pallas kernels, place_chunk(): pl.pallas_call(functools.partial(place_kernel, len(pieces)), out_shape=ja...  12 us
    ppermute x4, waiting for transfers between devices, layer(): right = (xr, lax.ppermute(right[1], 'expert', backward))  10.9 us
  transfers between devices with their start and end apart: 39, of which 13 were waited for; matrix products, arithmetic and copies ran while one was open for 7% of the time, Pallas kernels for 27%

profile of v2, /device:TPU:0, one launch (start us, length us, event | category | flops | bytes accessed | tf_op | source)
XLA Modules:
  0.0 249.4 jit_solution(5228050393291766407)
XLA Ops:
  0.6 3.0 %collective-permute-start.3 = (bf16[128,2048]{1,0:T(8,128)(2,1)}, bf16[128,2048]{1,0:T(8,128)(2,1)S(1)}, u32[]{:S(2)}, u32[]{:S(2)}) collective-permute-start(bf16[128,2048]{1,0:T(8,128)(2,1)} %refs_0_.6), channel_id=1, source_target_pairs={{2,0},{4,2},{6,4},{7,6},{5,7},{3,5},{1,3},{0,1},{10,8},{12,10},{14... | collective-permute-start | bytes 1572872 | tf_op jit(solution)/shard_map/ppermute | solution.py:303
  5.8 10.9 %collective-permute-done.3.refs_5_.refs_2_ = bf16[128,2048]{1,0:T(8,128)(2,1)S(1)} collective-permute-done((bf16[128,2048]{1,0:T(8,128)(2,1)}, bf16[128,2048]{1,0:T(8,128)(2,1)S(1)}, u32[]{:S(2)}, u32[]{:S(2)}) %collective-permute-start.3) | collective-permute-done | bytes 524320 | tf_op jit(solution)/shard_map/ppermute | solution.py:303
  18.8 9.1 %collective-permute-done.1.refs_2_ = bf16[128,2048]{1,0:T(8,128)(2,1)S(1)} collective-permute-done((bf16[128,2048]{1,0:T(8,128)(2,1)}, bf16[128,2048]{1,0:T(8,128)(2,1)S(1)}, u32[]{:S(2)}, u32[]{:S(2)}) %collective-permute-start.1) | collective-permute-done | bytes 524320 | tf_op jit(solution)/shard_map/ppermute | solution.py:301
  32.1 6.1 %all-to-all-start = ((bf16[128,8,2]{0,2,1:T(2,128)(2,1)}), bf16[128,8,2]{0,2,1:T(2,128)(2,1)S(1)}, u32[]{:S(2)}, u32[]{:S(2)}) async-start(bf16[128,8,2]{0,2,1:T(2,128)(2,1)} %bitcast.1), calls=%async_computation | async-start | bytes 8192 | tf_op jit(solution)/shard_map/all_to_all | solution.py:288
  39.6 14.5 %all-to-all-done = bf16[128,8,2]{0,2,1:T(2,128)(2,1)S(1)} async-done(((bf16[128,8,2]{0,2,1:T(2,128)(2,1)}), bf16[128,8,2]{0,2,1:T(2,128)(2,1)S(1)}, u32[]{:S(2)}, u32[]{:S(2)}) %all-to-all-start) | async-done | bytes 4128 | tf_op jit(solution)/shard_map/all_to_all | solution.py:288
  59.0 14.2 %experts.4 = (bf16[2,384,768]{2,1,0:T(8,128)(2,1)}, bf16[2,384,384]{2,1,0:T(8,128)(2,1)}, bf16[128,1024]{1,0:T(8,128)(2,1)}, bf16[128,1152]{1,0:T(8,128)(2,1)}, ...) custom-call(s32[9]{0:T(128)} %pad_add_fusion.scalars, ...), custom_call_target="tpu_custom_call" | custom-call | flops 6039797760 | bytes 15728640 | tf_op jit(solution)/shard_map/experts/pallas_call | solution.py:130
  76.1 5.1 %collective-permute-done.9.refs_1_.refs_6_ = bf16[128,2048]{1,0:T(8,128)(2,1)S(1)} collective-permute-done((bf16[128,2048]{1,0:T(8,128)(2,1)}, bf16[128,2048]{1,0:T(8,128)(2,1)S(1)}, u32[]{:S(2)}, u32[]{:S(2)}) %collective-permute-start.9) | collective-permute-done | bytes 524320 | tf_op jit(solution)/shard_map/ppermute | solution.py:301
  84.9 11.0 %experts.5 = (bf16[2,256,768]{2,1,0:T(8,128)(2,1)}, bf16[2,256,384]{2,1,0:T(8,128)(2,1)}, bf16[128,1024]{1,0:T(8,128)(2,1)}, bf16[128,1152]{1,0:T(8,128)(2,1)}, ...) custom-call(s32[9]{0:T(128)} %pad_add_fusion.scalars, bf16[128,2048]{1,0:T(8,128)(2,1)} %collective-permute-done.4.refs_0_.refs_3_, ...), custom_call_target="tpu_custom_call" | custom-call | flops 4026531840 | bytes 13631488 | tf_op jit(solution)/shard_map/experts/pallas_call | solution.py:130
  95.9 7.7 %experts.6 = (bf16[2,256,768]{2,1,0:T(8,128)(2,1)}, bf16[2,256,384]{2,1,0:T(8,128)(2,1)}, f32[2,256,128]{2,1,0:T(8,128)}) custom-call(s32[9]{0:T(128)} %pad_add_fusion.scalars, bf16[128,2048]{1,0:T(8,128)(2,1)} %copy-done.5, bf16[128,2048]{1,0:T(8,128)(2,1)} %copy-done.4, bf16[128,2048]{1,0:T(8,128)(2,1)} %copy-done.7, bf16[128,2048]{1,0:T(8,128)(2,1)} %copy-done.6, ...), custom_call_target="tpu_custom_call" | custom-call | flops 2415919104 | bytes 13631488 | tf_op jit(solution)/shard_map/experts/pallas_call | solution.py:130
  105.3 6.5 %experts.7 = (bf16[2,128,768]{2,1,0:T(8,128)(2,1)}, bf16[2,128,384]{2,1,0:T(8,128)(2,1)}, f32[2,128,128]{2,1,0:T(8,128)}) custom-call(s32[9]{0:T(128)} %pad_add_fusion.scalars, bf16[64,2048]{1,0:T(8,128)(2,1)} %copy-done.20, bf16[64,2048]{1,0:T(8,128)(2,1)} %copy-done.19, bf16[64,2048]{1,0:T(8,128)(2,1)} %copy-done.26, bf16[64,2048]{1,0:T(8,128)(2,1)} %copy-done.25, ...), custom_call_target="tpu_custom_call" | custom-call | flops 1207959552 | bytes 11534336 | tf_op jit(solution)/shard_map/experts/pallas_call | solution.py:130
  111.8 7.0 %rows.1 = (bf16[128,1024]{1,0:T(8,128)(2,1)}, bf16[128,1152]{1,0:T(8,128)(2,1)}, bf16[128,1024]{1,0:T(8,128)(2,1)}, bf16[128,1152]{1,0:T(8,128)(2,1)}, bf16[64,1...) custom-call(bf16[2,256,768]{2,1,0:T(8,128)(2,1)} %get-tuple-element.40.refs_0_., ...), custom_call_target="tpu_custom_call" | custom-call | flops 2415919104 | bytes 9437184 | tf_op jit(solution)/shard_map/rows/pallas_call | solution.py:93
  122.9 9.1 %weights.4 = (bf16[2,512,768]{2,1,0:T(8,128)(2,1)}, bf16[2,512,768]{2,1,0:T(8,128)(2,1)}) custom-call(bf16[128,2048]{1,0:T(8,128)(2,1)} %refs_0_.6, bf16[128,2048]{1,0:T(8,128)(2,1)} %copy-done.34, bf16[128,2048]{1,0:T(8,128)(2,1)} %copy-done.33, bf16[128,2048]{1,0:T(8,128)(2,1)} %collective-permute-done.6.refs_2_.refs_3_, ...), custom_call_target="tpu_custom_call" | custom-call | flops 3221225472 | bytes 8912896 | tf_op jit(solution)/shard_map/weights/pallas_call | solution.py:221
  132.1 9.4 %weights.5 = (bf16[2,512,1024]{2,1,0:T(8,128)(2,1)}, bf16[2,512,1024]{2,1,0:T(8,128)(2,1)}) custom-call(bf16[128,2048]{1,0:T(8,128)(2,1)} %refs_0_.7, bf16[128,2048]{1,0:T(8,128)(2,1)} %copy-done.32, bf16[128,2048]{1,0:T(8,128)(2,1)} %copy-done.31, bf16[128,2048]{1,0:T(8,128)(2,1)} %collective-permute-done.4.refs_0_.refs_3_, ...), custom_call_target="tpu_custom_call" | custom-call | flops 4294967296 | bytes 10485760 | tf_op jit(solution)/shard_map/weights/pallas_call | solution.py:221
  145.1 6.3 %collective-permute-done.21 = bf16[128,1024]{1,0:T(8,128)(2,1)S(1)} collective-permute-done((bf16[128,1024]{1,0:T(8,128)(2,1)S(1)}, bf16[128,1024]{1,0:T(8,128)(2,1)S(1)}, u32[]{:S(2)}, u32[]{:S(2)}) %collective-permute-start.21) | collective-permute-done | bytes 262176 | tf_op jit(solution)/shard_map/ppermute | solution.py:331
  153.6 5.0 %collective-permute-done.25 = bf16[128,1152]{1,0:T(8,128)(2,1)S(1)} collective-permute-done((bf16[128,1152]{1,0:T(8,128)(2,1)S(1)}, bf16[128,1152]{1,0:T(8,128)(2,1)S(1)}, u32[]{:S(2)}, u32[]{:S(2)}) %collective-permute-start.25) | collective-permute-done | bytes 294944 | tf_op jit(solution)/shard_map/ppermute | solution.py:330
  159.9 7.8 %collective-permute-done.18 = bf16[128,1024]{1,0:T(8,128)(2,1)S(1)} collective-permute-done((bf16[128,1024]{1,0:T(8,128)(2,1)S(1)}, bf16[128,1024]{1,0:T(8,128)(2,1)S(1)}, u32[]{:S(2)}, u32[]{:S(2)}) %collective-permute-start.18) | collective-permute-done | bytes 262176 | tf_op jit(solution)/shard_map/ppermute | solution.py:330
  170.0 4.1 %collective-permute-done.26 = bf16[128,1152]{1,0:T(8,128)(2,1)S(1)} collective-permute-done((bf16[128,1152]{1,0:T(8,128)(2,1)S(1)}, bf16[128,1152]{1,0:T(8,128)(2,1)S(1)}, u32[]{:S(2)}, u32[]{:S(2)}) %collective-permute-start.26) | collective-permute-done | bytes 294944 | tf_op jit(solution)/shard_map/ppermute | solution.py:330
  179.9 6.5 %weights.3 = (bf16[2,512,512]{2,1,0:T(8,128)(2,1)}, bf16[2,512,512]{2,1,0:T(8,128)(2,1)}) custom-call(bf16[128,2048]{1,0:T(8,128)(2,1)} %refs_0_.7, bf16[128,2048]{1,0:T(8,128)(2,1)} %copy-done.32, bf16[128,2048]{1,0:T(8,128)(2,1)} %copy-done.31, bf16[128,2048]{1,0:T(8,128)(2,1)} %collective-permute-done.4.refs_0_.refs_3_, ...), custom_call_target="tpu_custom_call" | custom-call | flops 2147483648 | bytes 7340032 | tf_op jit(solution)/shard_map/weights/pallas_call | solution.py:221
  199.7 17.8 %collective-permute-done.37.refs_2_ = bf16[1,512,1024]{2,1,0:T(8,128)(2,1)S(1)} collective-permute-done((bf16[1,512,1024]{2,1,0:T(8,128)(2,1)}, bf16[1,512,1024]{2,1,0:T(8,128)(2,1)S(1)}, u32[]{:S(2)}, u32[]{:S(2)}) %collective-permute-start.37) | collective-permute-done | bytes 1048608 | tf_op jit(solution)/shard_map/ppermute | solution.py:367
  218.5 4.5 %place.3.refs_3_ = bf16[512,2,1152]{2,1,0:T(2,128)(2,1)} custom-call(bf16[2,512,1024]{2,1,0:T(8,128)(2,1)} %get-tuple-element.69.refs_0_, bf16[2,512,1024]{2,1,0:T(8,128)(2,1)} %collective-permute-done.36.refs_1_, bf16[1,512,1024]{2,1,0:T(8,128)(2,1)} %copy-done.9), custom_call_target="tpu_custom_call" | custom-call | tf_op jit(solution)/shard_map/place/pallas_call | solution.py:261
  223.1 11.3 %collective-permute-done.35.refs_2_ = bf16[1,512,768]{2,1,0:T(8,128)(2,1)S(1)} collective-permute-done((bf16[1,512,768]{2,1,0:T(8,128)(2,1)}, bf16[1,512,768]{2,1,0:T(8,128)(2,1)S(1)}, u32[]{:S(2)}, u32[]{:S(2)}) %collective-permute-start.35) | collective-permute-done | bytes 786464 | tf_op jit(solution)/shard_map/ppermute | solution.py:367
  235.3 4.0 %place.4.refs_3_ = bf16[512,2,1152]{2,1,0:T(2,128)(2,1)} custom-call(bf16[2,512,768]{2,1,0:T(8,128)(2,1)} %get-tuple-element.67.refs_0_, bf16[2,512,768]{2,1,0:T(8,128)(2,1)} %collective-permute-done.34.refs_1_, bf16[1,512,768]{2,1,0:T(8,128)(2,1)} %copy-done.10, bf16[512,2,1152]{2,1,0:T(2,128)(2,1)} %place.3.refs_3_), custom_call_target="tpu_custom_call", output_to_operand_aliasing={{}: (3, {})} | custom-call | tf_op jit(solution)/shard_map/place/pallas_call | solution.py:261
  239.3 5.8 %collective-permute-done.33.refs_2_ = bf16[1,512,512]{2,1,0:T(8,128)(2,1)S(1)} collective-permute-done((bf16[1,512,512]{2,1,0:T(8,128)(2,1)}, bf16[1,512,512]{2,1,0:T(8,128)(2,1)S(1)}, u32[]{:S(2)}, u32[]{:S(2)}) %collective-permute-start.33) | collective-permute-done | bytes 524320 | tf_op jit(solution)/shard_map/ppermute | solution.py:367
  245.9 3.5 %place.5 = bf16[512,2,1152]{2,1,0:T(2,128)(2,1)} custom-call(bf16[2,512,512]{2,1,0:T(8,128)(2,1)} %get-tuple-element.61.refs_0_, bf16[2,512,512]{2,1,0:T(8,128)(2,1)} %copy-done.3, bf16[1,512,512]{2,1,0:T(8,128)(2,1)} %copy-done.11, bf16[512,2,1152]{2,1,0:T(2,128)(2,1)} %place.4.refs_3_), custom_call_target="tpu_custom_call", output_to_operand_aliasing={{}: (3, {})} | custom-call | tf_op jit(solution)/shard_map/place/pallas_call | solution.py:261
  (167 shorter events, 57.9 us)
Async XLA Ops:
  3.8 24.2 %collective-permute-start.1 = (bf16[128,2048]{1,0:T(8,128)(2,1)}, bf16[128,2048]{1,0:T(8,128)(2,1)S(1)}, u32[]{:S(2)}, u32[]{:S(2)}) collective-permute-start(bf16[128,2048]{1,0:T(8,128)(2,1)} %refs_0_.7), channel_id=1, source_target_pairs={{2,0},{4,2},{6,4},{7,6},{5,7},{3,5},{1,3},{0,1},{10,8},{12,10},{14... | collective-permute-start | bytes 1572872 | tf_op jit(solution)/shard_map/ppermute | solution.py:301
  5.7 24.2 %collective-permute-start = (bf16[128,2048]{1,0:T(8,128)(2,1)}, bf16[128,2048]{1,0:T(8,128)(2,1)S(1)}, u32[]{:S(2)}, u32[]{:S(2)}) collective-permute-start(bf16[128,2048]{1,0:T(8,128)(2,1)} %refs_0_.7), channel_id=1, source_target_pairs={{0,2},{2,4},{4,6},{6,7},{7,5},{5,3},{3,1},{1,0},{8,10},{10,12},{12... | collective-permute-start | bytes 1572872 | tf_op jit(solution)/shard_map/ppermute | solution.py:300
  16.7 38.2 %collective-permute-start.7 = (bf16[128,2048]{1,0:T(8,128)(2,1)S(1)}, bf16[128,2048]{1,0:T(8,128)(2,1)}, u32[]{:S(2)}, u32[]{:S(2)}) collective-permute-start(bf16[128,2048]{1,0:T(8,128)(2,1)S(1)} %collective-permute-done.3.refs_5_.refs_2_), channel_id=1, source_target_pairs={{2,0},{4,2},{6,4},{7,6},{5,7},{3,5},{1,3},{0,1},{10,8},{12,10},{14... | collective-permute-start | bytes 1572872 | tf_op jit(solution)/shard_map/ppermute | solution.py:303
  18.7 36.8 %collective-permute-start.6 = (bf16[128,2048]{1,0:T(8,128)(2,1)S(1)}, bf16[128,2048]{1,0:T(8,128)(2,1)}, u32[]{:S(2)}, u32[]{:S(2)}) collective-permute-start(bf16[128,2048]{1,0:T(8,128)(2,1)S(1)} %collective-permute-done.2.refs_4_.refs_1_), channel_id=1, source_target_pairs={{0,2},{2,4},{4,6},{6,7},{7,5},{5,3},{3,1},{1,0},{8,10},{10,12},{12... | collective-permute-start | bytes 1572872 | tf_op jit(solution)/shard_map/ppermute | solution.py:302
  28.0 29.0 %collective-permute-start.5 = (bf16[128,2048]{1,0:T(8,128)(2,1)S(1)}, bf16[128,2048]{1,0:T(8,128)(2,1)}, u32[]{:S(2)}, u32[]{:S(2)}) collective-permute-start(bf16[128,2048]{1,0:T(8,128)(2,1)S(1)} %collective-permute-done.1.refs_2_), channel_id=1, source_target_pairs={{2,0},{4,2},{6,4},{7,6},{5,7},{3,5},{1,3},{0,1},{10,8},{12,10},{14... | collective-permute-start | bytes 1572872 | tf_op jit(solution)/shard_map/ppermute | solution.py:301
  29.9 27.6 %collective-permute-start.4 = (bf16[128,2048]{1,0:T(8,128)(2,1)S(1)}, bf16[128,2048]{1,0:T(8,128)(2,1)}, u32[]{:S(2)}, u32[]{:S(2)}) collective-permute-start(bf16[128,2048]{1,0:T(8,128)(2,1)S(1)} %collective-permute-done.refs_1_), channel_id=1, source_target_pairs={{0,2},{2,4},{4,6},{6,7},{7,5},{5,3},{3,1},{1,0},{8,10},{10,12},{12... | collective-permute-start | bytes 1572872 | tf_op jit(solution)/shard_map/ppermute | solution.py:300
  32.1 22.0 %all-to-all-start = ((bf16[128,8,2]{0,2,1:T(2,128)(2,1)}), bf16[128,8,2]{0,2,1:T(2,128)(2,1)S(1)}, u32[]{:S(2)}, u32[]{:S(2)}) async-start(bf16[128,8,2]{0,2,1:T(2,128)(2,1)} %bitcast.1), calls=%async_computation | async-start | bytes 8192 | tf_op jit(solution)/shard_map/all_to_all | solution.py:288
  54.9 18.3 %collective-permute-start.11 = (bf16[128,2048]{1,0:T(8,128)(2,1)}, bf16[128,2048]{1,0:T(8,128)(2,1)S(1)}, u32[]{:S(2)}, u32[]{:S(2)}) collective-permute-start(bf16[128,2048]{1,0:T(8,128)(2,1)} %collective-permute-done.7.refs_3_.refs_4_), channel_id=1, source_target_pairs={{2,0},{4,2},{6,4},{7,6},{5,7},{3,5},{1,3},{0,1},{10,8},{12,10},{14... | collective-permute-start | bytes 1572872 | tf_op jit(solution)/shard_map/ppermute | solution.py:303
  55.5 18.3 %collective-permute-start.10 = (bf16[128,2048]{1,0:T(8,128)(2,1)}, bf16[128,2048]{1,0:T(8,128)(2,1)S(1)}, u32[]{:S(2)}, u32[]{:S(2)}) collective-permute-start(bf16[128,2048]{1,0:T(8,128)(2,1)} %collective-permute-done.6.refs_2_.refs_3_), channel_id=1, source_target_pairs={{0,2},{2,4},{4,6},{6,7},{7,5},{5,3},{3,1},{1,0},{8,10},{10,12},{12... | collective-permute-start | bytes 1572872 | tf_op jit(solution)/shard_map/ppermute | solution.py:302
  57.0 24.2 %collective-permute-start.9 = (bf16[128,2048]{1,0:T(8,128)(2,1)}, bf16[128,2048]{1,0:T(8,128)(2,1)S(1)}, u32[]{:S(2)}, u32[]{:S(2)}) collective-permute-start(bf16[128,2048]{1,0:T(8,128)(2,1)} %collective-permute-done.5.refs_1_.refs_4_), channel_id=1, source_target_pairs={{2,0},{4,2},{6,4},{7,6},{5,7},{3,5},{1,3},{0,1},{10,8},{12,10},{14... | collective-permute-start | bytes 1572872 | tf_op jit(solution)/shard_map/ppermute | solution.py:301
  57.5 25.1 %collective-permute-start.8 = (bf16[128,2048]{1,0:T(8,128)(2,1)}, bf16[128,2048]{1,0:T(8,128)(2,1)S(1)}, u32[]{:S(2)}, u32[]{:S(2)}) collective-permute-start(bf16[128,2048]{1,0:T(8,128)(2,1)} %collective-permute-done.4.refs_0_.refs_3_), channel_id=1, source_target_pairs={{0,2},{2,4},{4,6},{6,7},{7,5},{5,3},{3,1},{1,0},{8,10},{10,12},{12... | collective-permute-start | bytes 1572872 | tf_op jit(solution)/shard_map/ppermute | solution.py:300
  73.2 30.4 %collective-permute-start.15 = (bf16[64,2048]{1,0:T(8,128)(2,1)S(1)}, bf16[64,2048]{1,0:T(8,128)(2,1)S(1)}, u32[]{:S(2)}, u32[]{:S(2)}) collective-permute-start(bf16[64,2048]{1,0:T(8,128)(2,1)S(1)} %slice.53), channel_id=1, source_target_pairs={{2,0},{4,2},{6,4},{7,6},{5,7},{3,5},{1,3},{0,1},{10,8},{12,10},{14... | collective-permute-start | bytes 786440 | tf_op jit(solution)/shard_map/ppermute | solution.py:303
  74.6 29.0 %collective-permute-start.14 = (bf16[64,2048]{1,0:T(8,128)(2,1)}, bf16[64,2048]{1,0:T(8,128)(2,1)S(1)}, u32[]{:S(2)}, u32[]{:S(2)}) collective-permute-start(bf16[64,2048]{1,0:T(8,128)(2,1)} %slice.52), channel_id=1, source_target_pairs={{0,2},{2,4},{4,6},{6,7},{7,5},{5,3},{3,1},{1,0},{8,10},{10,12},{12... | collective-permute-start | bytes 786440 | tf_op jit(solution)/shard_map/ppermute | solution.py:302
  82.0 21.6 %collective-permute-start.13 = (bf16[64,2048]{1,0:T(8,128)(2,1)}, bf16[64,2048]{1,0:T(8,128)(2,1)S(1)}, u32[]{:S(2)}, u32[]{:S(2)}) collective-permute-start(bf16[64,2048]{1,0:T(8,128)(2,1)} %slice.51), channel_id=1, source_target_pairs={{2,0},{4,2},{6,4},{7,6},{5,7},{3,5},{1,3},{0,1},{10,8},{12,10},{14... | collective-permute-start | bytes 786440 | tf_op jit(solution)/shard_map/ppermute | solution.py:301
  83.4 20.3 %collective-permute-start.12 = (bf16[64,2048]{1,0:T(8,128)(2,1)}, bf16[64,2048]{1,0:T(8,128)(2,1)S(1)}, u32[]{:S(2)}, u32[]{:S(2)}) collective-permute-start(bf16[64,2048]{1,0:T(8,128)(2,1)} %slice.50), channel_id=1, source_target_pairs={{0,2},{2,4},{4,6},{6,7},{7,5},{5,3},{3,1},{1,0},{8,10},{10,12},{12... | collective-permute-start | bytes 786440 | tf_op jit(solution)/shard_map/ppermute | solution.py:300
  118.8 23.3 %collective-permute-start.16 = (bf16[64,1024]{1,0:T(8,128)(2,1)}, bf16[64,1024]{1,0:T(8,128)(2,1)S(1)}, u32[]{:S(2)}, u32[]{:S(2)}) collective-permute-start(bf16[64,1024]{1,0:T(8,128)(2,1)} %get-tuple-element.45), channel_id=1, source_target_pairs={{2,0},{4,2},{6,4},{7,6},{5,7},{3,5},{1,3},{0,1},{10,8},{12,10},{14... | collective-permute-start | bytes 393224 | tf_op jit(solution)/shard_map/ppermute | solution.py:330
  119.4 22.2 %collective-permute-start.20 = (bf16[64,1024]{1,0:T(8,128)(2,1)}, bf16[64,1024]{1,0:T(8,128)(2,1)S(1)}, u32[]{:S(2)}, u32[]{:S(2)}) collective-permute-start(bf16[64,1024]{1,0:T(8,128)(2,1)} %get-tuple-element.49), channel_id=1, source_target_pairs={{0,2},{2,4},{4,6},{6,7},{7,5},{5,3},{3,1},{1,0},{8,10},{10,12},{12... | collective-permute-start | bytes 393224 | tf_op jit(solution)/shard_map/ppermute | solution.py:331
  120.8 23.6 %collective-permute-start.24 = (bf16[64,1152]{1,0:T(8,128)(2,1)}, bf16[64,1152]{1,0:T(8,128)(2,1)S(1)}, u32[]{:S(2)}, u32[]{:S(2)}) collective-permute-start(bf16[64,1152]{1,0:T(8,128)(2,1)} %get-tuple-element.54), channel_id=1, source_target_pairs={{2,0},{4,2},{6,4},{7,6},{5,7},{3,5},{1,3},{0,1},{10,8},{12,10},{14... | collective-permute-start | bytes 442376 | tf_op jit(solution)/shard_map/ppermute | solution.py:330
  121.4 21.4 %collective-permute-start.28 = (bf16[64,1152]{1,0:T(8,128)(2,1)}, bf16[64,1152]{1,0:T(8,128)(2,1)S(1)}, u32[]{:S(2)}, u32[]{:S(2)}) collective-permute-start(bf16[64,1152]{1,0:T(8,128)(2,1)} %get-tuple-element.58), channel_id=1, source_target_pairs={{0,2},{2,4},{4,6},{6,7},{7,5},{5,3},{3,1},{1,0},{8,10},{10,12},{12... | collective-permute-start | bytes 442376 | tf_op jit(solution)/shard_map/ppermute | solution.py:331
  132.0 60.8 %collective-permute-start.34 = (bf16[2,512,768]{2,1,0:T(8,128)(2,1)}, bf16[2,512,768]{2,1,0:T(8,128)(2,1)}, u32[]{:S(2)}, u32[]{:S(2)}) collective-permute-start(bf16[2,512,768]{2,1,0:T(8,128)(2,1)} %get-tuple-element.68), channel_id=1, source_target_pairs={{0,8},{8,0},{16,24},{24,16},{1,9},{9,1},{17,25},{25,17},{2,10},{10... | collective-permute-start | bytes 4718600 | tf_op jit(solution)/shard_map/ppermute | solution.py:360
  141.6 46.9 %collective-permute-start.36 = (bf16[2,512,1024]{2,1,0:T(8,128)(2,1)}, bf16[2,512,1024]{2,1,0:T(8,128)(2,1)}, u32[]{:S(2)}, u32[]{:S(2)}) collective-permute-start(bf16[2,512,1024]{2,1,0:T(8,128)(2,1)} %get-tuple-element.70), channel_id=1, source_target_pairs={{0,8},{8,0},{16,24},{24,16},{1,9},{9,1},{17,25},{25,17},{2,10},{10... | collective-permute-start | bytes 6291464 | tf_op jit(solution)/shard_map/ppermute | solution.py:360
  191.3 26.2 %collective-permute-start.37 = (bf16[1,512,1024]{2,1,0:T(8,128)(2,1)}, bf16[1,512,1024]{2,1,0:T(8,128)(2,1)S(1)}, u32[]{:S(2)}, u32[]{:S(2)}) collective-permute-start(bf16[1,512,1024]{2,1,0:T(8,128)(2,1)} %add_convert_fusion), channel_id=1, source_target_pairs={{0,16},{8,24},{16,0},{24,8},{1,17},{9,25},{17,1},{25,9},{2,18},{10... | collective-permute-start | bytes 3145736 | tf_op jit(solution)/shard_map/ppermute | solution.py:367
  195.0 39.3 %collective-permute-start.35 = (bf16[1,512,768]{2,1,0:T(8,128)(2,1)}, bf16[1,512,768]{2,1,0:T(8,128)(2,1)S(1)}, u32[]{:S(2)}, u32[]{:S(2)}) collective-permute-start(bf16[1,512,768]{2,1,0:T(8,128)(2,1)} %add_convert_fusion.1), channel_id=1, source_target_pairs={{0,16},{8,24},{16,0},{24,8},{1,17},{9,25},{17,1},{25,9},{2,18},{10... | collective-permute-start | bytes 2359304 | tf_op jit(solution)/shard_map/ppermute | solution.py:367
  196.7 48.4 %collective-permute-start.33 = (bf16[1,512,512]{2,1,0:T(8,128)(2,1)}, bf16[1,512,512]{2,1,0:T(8,128)(2,1)S(1)}, u32[]{:S(2)}, u32[]{:S(2)}) collective-permute-start(bf16[1,512,512]{2,1,0:T(8,128)(2,1)} %add_convert_fusion.2), channel_id=1, source_target_pairs={{0,16},{8,24},{16,0},{24,8},{1,17},{9,25},{17,1},{25,9},{2,18},{10... | collective-permute-start | bytes 1572872 | tf_op jit(solution)/shard_map/ppermute | solution.py:367
  (50 other events, 617.3 us)

commit v3 on v0

--- a/solution.py
+++ b/solution.py
@@ -6,6 +6,9 @@
 from jax.experimental import pallas as pl
 from jax.experimental.pallas import tpu as pltpu
 from jax.sharding import PartitionSpec as P
+
+
+VMEM_BYTES = 67043328
 
 
 def ring_order(size):
@@ -103,6 +106,7 @@
             bytes_accessed=2 * experts * width * (wide + units) + 8 * rows * width,
             transcendentals=0,
         ),
+        compiler_params=pltpu.CompilerParams(vmem_limit_bytes=VMEM_BYTES),
         name="experts",
     )(table, *[b[4] for b in blocks], *[gates] * count, *[b[3] for b in blocks], weight_in, weight_out)
     return out[0], out[1], out[2:]
@@ -214,6 +218,7 @@
         + ([] if held is None else [pl.BlockSpec(memory_space=pl.ANY)]),
         out_specs=pl.BlockSpec((tile, experts, size), lambda i: (i, 0, at)),
         input_output_aliases={} if held is None else {len(pieces): 0},
+        compiler_params=pltpu.CompilerParams(vmem_limit_bytes=VMEM_BYTES),
         name="place",
     )(*args)
 
@@ -286,9 +291,8 @@
     xs, gs = [b[3] for b in blocks], [b[4] for b in blocks]
     pres, hiddens = [r[0] for r in results], [r[1] for r in results]
     units = down_weight.shape[1]
-    third = 2 * units // 3
-    chunks = [(xs, pres, 2 * third, third), (gs, hiddens, 0, units), (xs, pres, 0, 2 * third)]
-    places = [2, 2, 0]
+    chunks = [(xs, pres, 0, units), (gs, hiddens, 0, units), (xs, pres, units, units)]
+    places = [0, 2, 1]
     parts = []
     for chunk in chunks:
         parts += weight_parts(*chunk, replicas)

time: 224 us -> 235 us (1.049)
  waiting for transfers between devices: 86.5 us -> 94.8 us
  local copies, waits for them, and re-layouts: 4.99 us -> 8.54 us
    ppermute x3, waiting for transfers between devices: 26.2 us -> 31.6 us  [layer(): pieces.append(lax.ppermute(narrow(both)[None], 'dp', pairs))]
    ppermute x4, waiting for transfers between devices: 24.4 us -> 28 us  [layer(): from_right = lax.ppermute(to_left, 'expert', backward).astype(jnp.float32)]
    slice x2, local copies, waits for them, and re-layouts: 0.04 us -> 3.36 us  [layer(): a[:mid]]
    slice x2, local copies, waits for them, and re-layouts: 0.04 us -> 3.34 us  [layer(): a[mid:]]
    unnamed x52 -> x34, local copies, waits for them, and re-layouts: 3.13 us -> 0.06 us
  transfers between devices with their start and end apart: 31 -> 31, of which waited for: 9 -> 9; matrix products, arithmetic and copies ran while one was open for 6% -> 8% of each run, Pallas kernels for 31% -> 30%
where the time goes in v3:
time: 235 us
  waiting for transfers between devices  94.8 us (40%)
  Pallas kernels  84.2 us (36%)
  starting transfers between devices  36.6 us (16%)
  other arithmetic  9.9 us (4%)
  local copies, waits for them, and re-layouts  8.54 us (4%)
    pallas_call x4, Pallas kernels, expert_blocks(): pl.pallas_call(functools.partial(expert_kernel, count, gates.shape[0]), o...  44.8 us
    ppermute x3, waiting for transfers between devices, layer(): pieces.append(lax.ppermute(narrow(both)[None], 'dp', pairs))  31.6 us
    ppermute x4, waiting for transfers between devices, layer(): from_right = lax.ppermute(to_left, 'expert', backward).astype(jnp.float32)  28 us
    pallas_call x3, Pallas kernels, weight_parts(): pl.pallas_call(functools.partial(weight_kernel, x_rows, p_rows, start, de...  27.2 us
    all_to_all x1, waiting for transfers between devices, layer(): lax.all_to_all(dense_gates, 'expert', split_axis=1, concat_axis=0, tiled=...  14.4 us
    pallas_call x3, Pallas kernels, place_chunk(): pl.pallas_call(functools.partial(place_kernel, len(pieces)), out_shape=ja...  12.1 us
    ppermute x4, waiting for transfers between devices, layer(): right = (xr, lax.ppermute(right[1], 'expert', backward))  10.9 us
    ppermute x4, waiting for transfers between devices, layer(): xr = lax.ppermute(right[0], 'expert', backward)  9.15 us
  transfers between devices with their start and end apart: 31, of which 9 were waited for; matrix products, arithmetic and copies ran while one was open for 8% of the time, Pallas kernels for 30%

profile of v3, /device:TPU:0, one launch (start us, length us, event | category | flops | bytes accessed | tf_op | source)
XLA Modules:
  0.0 234.8 jit_solution(18172060302754576974)
XLA Ops:
  0.6 3.0 %collective-permute-start.1 = (bf16[128,2048]{1,0:T(8,128)(2,1)}, bf16[128,2048]{1,0:T(8,128)(2,1)S(1)}, u32[]{:S(2)}, u32[]{:S(2)}) collective-permute-start(bf16[128,2048]{1,0:T(8,128)(2,1)} %refs_0_.6), channel_id=1, source_target_pairs={{2,0},{4,2},{6,4},{7,6},{5,7},{3,5},{1,3},{0,1},{10,8},{12,10},{14... | collective-permute-start | bytes 1572872 | tf_op jit(solution)/shard_map/ppermute | solution.py:256
  3.8 1.9 collective-permute-start.3
  5.8 10.9 %collective-permute-done.1.refs_2_ = bf16[128,2048]{1,0:T(8,128)(2,1)S(1)} collective-permute-done((bf16[128,2048]{1,0:T(8,128)(2,1)}, bf16[128,2048]{1,0:T(8,128)(2,1)S(1)}, u32[]{:S(2)}, u32[]{:S(2)}) %collective-permute-start.1) | collective-permute-done | bytes 524320 | tf_op jit(solution)/shard_map/ppermute | solution.py:256
  16.7 1.9 collective-permute-start.5
  18.8 9.1 %collective-permute-done.3.refs_8_.refs_2_ = bf16[128,2048]{1,0:T(8,128)(2,1)S(1)} collective-permute-done((bf16[128,2048]{1,0:T(8,128)(2,1)}, bf16[128,2048]{1,0:T(8,128)(2,1)S(1)}, u32[]{:S(2)}, u32[]{:S(2)}) %collective-permute-start.3) | collective-permute-done | bytes 524320 | tf_op jit(solution)/shard_map/ppermute | solution.py:254
  28.0 1.9 collective-permute-start.7
  32.1 6.1 %all-to-all-start = ((bf16[128,8,2]{0,2,1:T(2,128)(2,1)}), bf16[128,8,2]{0,2,1:T(2,128)(2,1)S(1)}, u32[]{:S(2)}, u32[]{:S(2)}) async-start(bf16[128,8,2]{0,2,1:T(2,128)(2,1)} %bitcast.1), calls=%async_computation | async-start | bytes 8192 | tf_op jit(solution)/shard_map/all_to_all | solution.py:241
  39.6 14.4 %all-to-all-done = bf16[128,8,2]{0,2,1:T(2,128)(2,1)S(1)} async-done(((bf16[128,8,2]{0,2,1:T(2,128)(2,1)}), bf16[128,8,2]{0,2,1:T(2,128)(2,1)S(1)}, u32[]{:S(2)}, u32[]{:S(2)}) %all-to-all-start) | async-done | bytes 4128 | tf_op jit(solution)/shard_map/all_to_all | solution.py:241
  59.0 14.2 %experts.4 = (bf16[2,384,768]{2,1,0:T(8,128)(2,1)}, bf16[2,384,384]{2,1,0:T(8,128)(2,1)}, bf16[128,2176]{1,0:T(8,128)(2,1)}, bf16[128,2176]{1,0:T(8,128)(2,1)}, bf16[128,2176]{1,0:T(8,128)(2,1)}) custom-call(s32[9]{0:T(128)} %pad_add_fusion.scalars, bf16[128,2048]{1,0:T(8,128)(2,1)} %refs_0_.6, bf16[128,2048]{1,0:T(8,128)(2,1)} %copy-done.16, ...), custom_call_target="tpu_custom_call" | custom-call | flops 6039797760 | bytes 15728640 | tf_op jit(solution)/shard_map/experts/pallas_call | solution.py:86
  73.2 11.0 %experts.5 = (bf16[2,256,768]{2,1,0:T(8,128)(2,1)}, bf16[2,256,384]{2,1,0:T(8,128)(2,1)}, bf16[128,2176]{1,0:T(8,128)(2,1)}, bf16[128,2176]{1,0:T(8,128)(2,1)}) custom-call(s32[9]{0:T(128)} %pad_add_fusion.scalars, bf16[128,2048]{1,0:T(8,128)(2,1)} %collective-permute-done.4.refs_0_.refs_3_, bf16[128,2048]{1,0:T(8,128)(2,1)} %collective-permute-done.5.refs_1_.refs_4_, ...), custom_call_target="tpu_custom_call" | custom-call | flops 4026531840 | bytes 13631488 | tf_op jit(solution)/shard_map/experts/pallas_call | solution.py:86
  95.0 10.9 %experts.6 = (bf16[2,256,768]{2,1,0:T(8,128)(2,1)}, bf16[2,256,384]{2,1,0:T(8,128)(2,1)}, bf16[128,2176]{1,0:T(8,128)(2,1)}, bf16[128,2176]{1,0:T(8,128)(2,1)}) custom-call(s32[9]{0:T(128)} %pad_add_fusion.scalars, bf16[128,2048]{1,0:T(8,128)(2,1)} %collective-permute-done.8.refs_0_.refs_5_, bf16[128,2048]{1,0:T(8,128)(2,1)} %collective-permute-done.9.refs_1_.refs_6_, ...), custom_call_target="tpu_custom_call" | custom-call | flops 4026531840 | bytes 13631488 | tf_op jit(solution)/shard_map/experts/pallas_call | solution.py:86
  105.9 8.7 %experts.7 = (bf16[2,128,768]{2,1,0:T(8,128)(2,1)}, bf16[2,128,384]{2,1,0:T(8,128)(2,1)}, bf16[64,2176]{1,0:T(8,128)(2,1)}, bf16[64,2176]{1,0:T(8,128)(2,1)}) custom-call(s32[9]{0:T(128)} %pad_add_fusion.scalars, bf16[64,2048]{1,0:T(8,128)(2,1)} %collective-permute-done.12.refs_0_.refs_7_, bf16[64,2048]{1,0:T(8,128)(2,1)} %collective-permute-done.13.refs_1_.refs_8_, ...), custom_call_target="tpu_custom_call" | custom-call | flops 2013265920 | bytes 11534336 | tf_op jit(solution)/shard_map/experts/pallas_call | solution.py:86
  116.7 9.1 %weights.4 = (bf16[2,512,768]{2,1,0:T(8,128)(2,1)}, bf16[2,512,768]{2,1,0:T(8,128)(2,1)}) custom-call(bf16[128,2048]{1,0:T(8,128)(2,1)} %refs_0_.6, bf16[128,2048]{1,0:T(8,128)(2,1)} %copy-done.16, bf16[128,2048]{1,0:T(8,128)(2,1)} %copy-done.15, bf16[128,2048]{1,0:T(8,128)(2,1)} %collective-permute-done.4.refs_0_.refs_3_, ...), custom_call_target="tpu_custom_call" | custom-call | flops 3221225472 | bytes 8912896 | tf_op jit(solution)/shard_map/weights/pallas_call | solution.py:173
  125.9 9.1 %weights.5 = (bf16[2,512,768]{2,1,0:T(8,128)(2,1)}, bf16[2,512,768]{2,1,0:T(8,128)(2,1)}) custom-call(bf16[128,2048]{1,0:T(8,128)(2,1)} %refs_0_.7, bf16[128,2048]{1,0:T(8,128)(2,1)} %copy-done.14, bf16[128,2048]{1,0:T(8,128)(2,1)} %copy-done.13, bf16[128,2048]{1,0:T(8,128)(2,1)} %collective-permute-done.6.refs_4_.refs_3_, ...), custom_call_target="tpu_custom_call" | custom-call | flops 3221225472 | bytes 8912896 | tf_op jit(solution)/shard_map/weights/pallas_call | solution.py:173
  135.5 9.1 %weights.3 = (bf16[2,512,768]{2,1,0:T(8,128)(2,1)}, bf16[2,512,768]{2,1,0:T(8,128)(2,1)}) custom-call(bf16[128,2048]{1,0:T(8,128)(2,1)} %refs_0_.7, bf16[128,2048]{1,0:T(8,128)(2,1)} %copy-done.14, bf16[128,2048]{1,0:T(8,128)(2,1)} %copy-done.13, bf16[128,2048]{1,0:T(8,128)(2,1)} %collective-permute-done.6.refs_4_.refs_3_, ...), custom_call_target="tpu_custom_call" | custom-call | flops 3221225472 | bytes 8912896 | tf_op jit(solution)/shard_map/weights/pallas_call | solution.py:173
  148.2 12.8 %collective-permute-done.17 = bf16[128,2176]{1,0:T(8,128)(2,1)S(1)} collective-permute-done((bf16[128,2176]{1,0:T(8,128)(2,1)S(1)}, bf16[128,2176]{1,0:T(8,128)(2,1)S(1)}, u32[]{:S(2)}, u32[]{:S(2)}) %collective-permute-start.17) | collective-permute-done | bytes 557088 | tf_op jit(solution)/shard_map/ppermute | solution.py:274
  163.4 11.8 %collective-permute-done.18 = bf16[128,2176]{1,0:T(8,128)(2,1)S(1)} collective-permute-done((bf16[128,2176]{1,0:T(8,128)(2,1)S(1)}, bf16[128,2176]{1,0:T(8,128)(2,1)S(1)}, u32[]{:S(2)}, u32[]{:S(2)}) %collective-permute-start.18) | collective-permute-done | bytes 557088 | tf_op jit(solution)/shard_map/ppermute | solution.py:274
  176.2 1.8 collective-permute-start.23
  185.3 3.4 %collective-permute-done.19 = bf16[128,2176]{1,0:T(8,128)(2,1)S(1)} collective-permute-done((bf16[128,2176]{1,0:T(8,128)(2,1)S(1)}, bf16[128,2176]{1,0:T(8,128)(2,1)S(1)}, u32[]{:S(2)}, u32[]{:S(2)}) %collective-permute-start.19) | collective-permute-done | bytes 557088 | tf_op jit(solution)/shard_map/ppermute | solution.py:274
  191.1 25.6 %collective-permute-done.29.refs_2_ = bf16[1,512,768]{2,1,0:T(8,128)(2,1)} collective-permute-done((bf16[1,512,768]{2,1,0:T(8,128)(2,1)}, bf16[1,512,768]{2,1,0:T(8,128)(2,1)}, u32[]{:S(2)}, u32[]{:S(2)}) %collective-permute-start.29) | collective-permute-done | bytes 786464 | tf_op jit(solution)/shard_map/ppermute | solution.py:309
  216.7 4.0 %place.3.refs_3_ = bf16[512,2,1152]{2,1,0:T(2,128)(2,1)} custom-call(bf16[2,512,768]{2,1,0:T(8,128)(2,1)} %get-tuple-element.47.refs_0_, bf16[2,512,768]{2,1,0:T(8,128)(2,1)} %copy-done.1, bf16[1,512,768]{2,1,0:T(8,128)(2,1)} %collective-permute-done.29.refs_2_), custom_call_target="tpu_custom_call" | custom-call | tf_op jit(solution)/shard_map/place/pallas_call | solution.py:213
  220.8 4.0 %place.4.refs_3_ = bf16[512,2,1152]{2,1,0:T(2,128)(2,1)} custom-call(bf16[2,512,768]{2,1,0:T(8,128)(2,1)} %get-tuple-element.45.refs_0_, bf16[2,512,768]{2,1,0:T(8,128)(2,1)} %copy-done.3, bf16[1,512,768]{2,1,0:T(8,128)(2,1)} %collective-permute-done.27.refs_2_, bf16[512,2,1152]{2,1,0:T(2,128)(2,1)} %place.3.refs_3_), custom_call_target="tpu_custom_call", output_to_operand_aliasing={{}: (3, {})} | custom-call | tf_op jit(solution)/shard_map/place/pallas_call | solution.py:213
  224.8 5.9 %collective-permute-done.25.refs_2_ = bf16[1,512,768]{2,1,0:T(8,128)(2,1)} collective-permute-done((bf16[1,512,768]{2,1,0:T(8,128)(2,1)}, bf16[1,512,768]{2,1,0:T(8,128)(2,1)}, u32[]{:S(2)}, u32[]{:S(2)}) %collective-permute-start.25) | collective-permute-done | bytes 786464 | tf_op jit(solution)/shard_map/ppermute | solution.py:309
  230.8 4.0 %place.5 = bf16[512,2,1152]{2,1,0:T(2,128)(2,1)} custom-call(bf16[2,512,768]{2,1,0:T(8,128)(2,1)} %get-tuple-element.39.refs_0_, bf16[2,512,768]{2,1,0:T(8,128)(2,1)} %copy-done.5, bf16[1,512,768]{2,1,0:T(8,128)(2,1)} %collective-permute-done.25.refs_2_, bf16[512,2,1152]{2,1,0:T(2,128)(2,1)} %place.4.refs_3_), custom_call_target="tpu_custom_call", output_to_operand_aliasing={{}: (3, {})} | custom-call | tf_op jit(solution)/shard_map/place/pallas_call | solution.py:213
  (106 shorter events, 39.1 us)
Async XLA Ops:
  0.6 16.1 %collective-permute-start.1 = (bf16[128,2048]{1,0:T(8,128)(2,1)}, bf16[128,2048]{1,0:T(8,128)(2,1)S(1)}, u32[]{:S(2)}, u32[]{:S(2)}) collective-permute-start(bf16[128,2048]{1,0:T(8,128)(2,1)} %refs_0_.6), channel_id=1, source_target_pairs={{2,0},{4,2},{6,4},{7,6},{5,7},{3,5},{1,3},{0,1},{10,8},{12,10},{14... | collective-permute-start | bytes 1572872 | tf_op jit(solution)/shard_map/ppermute | solution.py:256
  3.6 15.0 %collective-permute-start = (bf16[128,2048]{1,0:T(8,128)(2,1)}, bf16[128,2048]{1,0:T(8,128)(2,1)S(1)}, u32[]{:S(2)}, u32[]{:S(2)}) collective-permute-start(bf16[128,2048]{1,0:T(8,128)(2,1)} %refs_0_.6), channel_id=1, source_target_pairs={{0,2},{2,4},{4,6},{6,7},{7,5},{5,3},{3,1},{1,0},{8,10},{10,12},{12... | collective-permute-start | bytes 1572872 | tf_op jit(solution)/shard_map/ppermute | solution.py:255
  3.8 24.2 %collective-permute-start.3 = (bf16[128,2048]{1,0:T(8,128)(2,1)}, bf16[128,2048]{1,0:T(8,128)(2,1)S(1)}, u32[]{:S(2)}, u32[]{:S(2)}) collective-permute-start(bf16[128,2048]{1,0:T(8,128)(2,1)} %refs_0_.7), channel_id=1, source_target_pairs={{2,0},{4,2},{6,4},{7,6},{5,7},{3,5},{1,3},{0,1},{10,8},{12,10},{14... | collective-permute-start | bytes 1572872 | tf_op jit(solution)/shard_map/ppermute | solution.py:254
  5.7 24.2 %collective-permute-start.2 = (bf16[128,2048]{1,0:T(8,128)(2,1)}, bf16[128,2048]{1,0:T(8,128)(2,1)S(1)}, u32[]{:S(2)}, u32[]{:S(2)}) collective-permute-start(bf16[128,2048]{1,0:T(8,128)(2,1)} %refs_0_.7), channel_id=1, source_target_pairs={{0,2},{2,4},{4,6},{6,7},{7,5},{5,3},{3,1},{1,0},{8,10},{10,12},{12... | collective-permute-start | bytes 1572872 | tf_op jit(solution)/shard_map/ppermute | solution.py:253
  16.7 38.2 %collective-permute-start.5 = (bf16[128,2048]{1,0:T(8,128)(2,1)S(1)}, bf16[128,2048]{1,0:T(8,128)(2,1)}, u32[]{:S(2)}, u32[]{:S(2)}) collective-permute-start(bf16[128,2048]{1,0:T(8,128)(2,1)S(1)} %collective-permute-done.1.refs_2_), channel_id=1, source_target_pairs={{2,0},{4,2},{6,4},{7,6},{5,7},{3,5},{1,3},{0,1},{10,8},{12,10},{14... | collective-permute-start | bytes 1572872 | tf_op jit(solution)/shard_map/ppermute | solution.py:256
  18.7 36.8 %collective-permute-start.4 = (bf16[128,2048]{1,0:T(8,128)(2,1)S(1)}, bf16[128,2048]{1,0:T(8,128)(2,1)}, u32[]{:S(2)}, u32[]{:S(2)}) collective-permute-start(bf16[128,2048]{1,0:T(8,128)(2,1)S(1)} %collective-permute-done.refs_1_), channel_id=1, source_target_pairs={{0,2},{2,4},{4,6},{6,7},{7,5},{5,3},{3,1},{1,0},{8,10},{10,12},{12... | collective-permute-start | bytes 1572872 | tf_op jit(solution)/shard_map/ppermute | solution.py:255
  28.0 29.0 %collective-permute-start.7 = (bf16[128,2048]{1,0:T(8,128)(2,1)S(1)}, bf16[128,2048]{1,0:T(8,128)(2,1)}, u32[]{:S(2)}, u32[]{:S(2)}) collective-permute-start(bf16[128,2048]{1,0:T(8,128)(2,1)S(1)} %collective-permute-done.3.refs_8_.refs_2_), channel_id=1, source_target_pairs={{2,0},{4,2},{6,4},{7,6},{5,7},{3,5},{1,3},{0,1},{10,8},{12,10},{14... | collective-permute-start | bytes 1572872 | tf_op jit(solution)/shard_map/ppermute | solution.py:254
  29.9 27.6 %collective-permute-start.6 = (bf16[128,2048]{1,0:T(8,128)(2,1)S(1)}, bf16[128,2048]{1,0:T(8,128)(2,1)}, u32[]{:S(2)}, u32[]{:S(2)}) collective-permute-start(bf16[128,2048]{1,0:T(8,128)(2,1)S(1)} %collective-permute-done.2.refs_7_.refs_1_), channel_id=1, source_target_pairs={{0,2},{2,4},{4,6},{6,7},{7,5},{5,3},{3,1},{1,0},{8,10},{10,12},{12... | collective-permute-start | bytes 1572872 | tf_op jit(solution)/shard_map/ppermute | solution.py:253
  32.1 22.0 %all-to-all-start = ((bf16[128,8,2]{0,2,1:T(2,128)(2,1)}), bf16[128,8,2]{0,2,1:T(2,128)(2,1)S(1)}, u32[]{:S(2)}, u32[]{:S(2)}) async-start(bf16[128,8,2]{0,2,1:T(2,128)(2,1)} %bitcast.1), calls=%async_computation | async-start | bytes 8192 | tf_op jit(solution)/shard_map/all_to_all | solution.py:241
  54.9 29.3 %collective-permute-start.9 = (bf16[128,2048]{1,0:T(8,128)(2,1)}, bf16[128,2048]{1,0:T(8,128)(2,1)}, u32[]{:S(2)}, u32[]{:S(2)}) collective-permute-start(bf16[128,2048]{1,0:T(8,128)(2,1)} %collective-permute-done.5.refs_1_.refs_4_), channel_id=1, source_target_pairs={{2,0},{4,2},{6,4},{7,6},{5,7},{3,5},{1,3},{0,1},{10,8},{12,10},{14... | collective-permute-start | bytes 1572872 | tf_op jit(solution)/shard_map/ppermute | solution.py:256
  55.5 30.9 %collective-permute-start.8 = (bf16[128,2048]{1,0:T(8,128)(2,1)}, bf16[128,2048]{1,0:T(8,128)(2,1)}, u32[]{:S(2)}, u32[]{:S(2)}) collective-permute-start(bf16[128,2048]{1,0:T(8,128)(2,1)} %collective-permute-done.4.refs_0_.refs_3_), channel_id=1, source_target_pairs={{0,2},{2,4},{4,6},{6,7},{7,5},{5,3},{3,1},{1,0},{8,10},{10,12},{12... | collective-permute-start | bytes 1572872 | tf_op jit(solution)/shard_map/ppermute | solution.py:255
  57.0 32.6 %collective-permute-start.11 = (bf16[128,2048]{1,0:T(8,128)(2,1)}, bf16[128,2048]{1,0:T(8,128)(2,1)}, u32[]{:S(2)}, u32[]{:S(2)}) collective-permute-start(bf16[128,2048]{1,0:T(8,128)(2,1)} %collective-permute-done.7.refs_5_.refs_4_), channel_id=1, source_target_pairs={{2,0},{4,2},{6,4},{7,6},{5,7},{3,5},{1,3},{0,1},{10,8},{12,10},{14... | collective-permute-start | bytes 1572872 | tf_op jit(solution)/shard_map/ppermute | solution.py:254
  57.5 34.3 %collective-permute-start.10 = (bf16[128,2048]{1,0:T(8,128)(2,1)}, bf16[128,2048]{1,0:T(8,128)(2,1)}, u32[]{:S(2)}, u32[]{:S(2)}) collective-permute-start(bf16[128,2048]{1,0:T(8,128)(2,1)} %collective-permute-done.6.refs_4_.refs_3_), channel_id=1, source_target_pairs={{0,2},{2,4},{4,6},{6,7},{7,5},{5,3},{3,1},{1,0},{8,10},{10,12},{12... | collective-permute-start | bytes 1572872 | tf_op jit(solution)/shard_map/ppermute | solution.py:253
  85.9 20.0 %collective-permute-start.13 = (bf16[64,2048]{1,0:T(8,128)(2,1)}, bf16[64,2048]{1,0:T(8,128)(2,1)}, u32[]{:S(2)}, u32[]{:S(2)}) collective-permute-start(bf16[64,2048]{1,0:T(8,128)(2,1)} %slice.49), channel_id=1, source_target_pairs={{2,0},{4,2},{6,4},{7,6},{5,7},{3,5},{1,3},{0,1},{10,8},{12,10},{14... | collective-permute-start | bytes 786440 | tf_op jit(solution)/shard_map/ppermute | solution.py:256
  88.1 17.8 %collective-permute-start.12 = (bf16[64,2048]{1,0:T(8,128)(2,1)}, bf16[64,2048]{1,0:T(8,128)(2,1)}, u32[]{:S(2)}, u32[]{:S(2)}) collective-permute-start(bf16[64,2048]{1,0:T(8,128)(2,1)} %slice.48), channel_id=1, source_target_pairs={{0,2},{2,4},{4,6},{6,7},{7,5},{5,3},{3,1},{1,0},{8,10},{10,12},{12... | collective-permute-start | bytes 786440 | tf_op jit(solution)/shard_map/ppermute | solution.py:255
  114.7 30.1 %collective-permute-start.16 = (bf16[64,2176]{1,0:T(8,128)(2,1)}, bf16[64,2176]{1,0:T(8,128)(2,1)}, u32[]{:S(2)}, u32[]{:S(2)}) collective-permute-start(bf16[64,2176]{1,0:T(8,128)(2,1)} %get-tuple-element.30), channel_id=1, source_target_pairs={{2,0},{4,2},{6,4},{7,6},{5,7},{3,5},{1,3},{0,1},{10,8},{12,10},{14... | collective-permute-start | bytes 835592 | tf_op jit(solution)/shard_map/ppermute | solution.py:274
  115.3 31.4 %collective-permute-start.20 = (bf16[64,2176]{1,0:T(8,128)(2,1)}, bf16[64,2176]{1,0:T(8,128)(2,1)S(1)}, u32[]{:S(2)}, u32[]{:S(2)}) collective-permute-start(bf16[64,2176]{1,0:T(8,128)(2,1)} %get-tuple-element.34), channel_id=1, source_target_pairs={{0,2},{2,4},{4,6},{6,7},{7,5},{5,3},{3,1},{1,0},{8,10},{10,12},{12... | collective-permute-start | bytes 835592 | tf_op jit(solution)/shard_map/ppermute | solution.py:275
  125.8 52.1 %collective-permute-start.26 = (bf16[2,512,768]{2,1,0:T(8,128)(2,1)}, bf16[2,512,768]{2,1,0:T(8,128)(2,1)S(1)}, u32[]{:S(2)}, u32[]{:S(2)}) collective-permute-start(bf16[2,512,768]{2,1,0:T(8,128)(2,1)} %get-tuple-element.46), channel_id=1, source_target_pairs={{0,8},{8,0},{16,24},{24,16},{1,9},{9,1},{17,25},{25,17},{2,10},{10... | collective-permute-start | bytes 4718600 | tf_op jit(solution)/shard_map/ppermute | solution.py:302
  135.0 45.7 %collective-permute-start.28 = (bf16[2,512,768]{2,1,0:T(8,128)(2,1)}, bf16[2,512,768]{2,1,0:T(8,128)(2,1)S(1)}, u32[]{:S(2)}, u32[]{:S(2)}) collective-permute-start(bf16[2,512,768]{2,1,0:T(8,128)(2,1)} %get-tuple-element.48), channel_id=1, source_target_pairs={{0,8},{8,0},{16,24},{24,16},{1,9},{9,1},{17,25},{25,17},{2,10},{10... | collective-permute-start | bytes 4718600 | tf_op jit(solution)/shard_map/ppermute | solution.py:302
  144.6 37.8 %collective-permute-start.24 = (bf16[2,512,768]{2,1,0:T(8,128)(2,1)}, bf16[2,512,768]{2,1,0:T(8,128)(2,1)S(1)}, u32[]{:S(2)}, u32[]{:S(2)}) collective-permute-start(bf16[2,512,768]{2,1,0:T(8,128)(2,1)} %get-tuple-element.40), channel_id=1, source_target_pairs={{0,8},{8,0},{16,24},{24,16},{1,9},{9,1},{17,25},{25,17},{2,10},{10... | collective-permute-start | bytes 4718600 | tf_op jit(solution)/shard_map/ppermute | solution.py:302
  146.7 15.0 %collective-permute-start.21 = (bf16[128,2176]{1,0:T(8,128)(2,1)S(1)}, bf16[128,2176]{1,0:T(8,128)(2,1)S(1)}, u32[]{:S(2)}, u32[]{:S(2)}) collective-permute-start(bf16[128,2176]{1,0:T(8,128)(2,1)S(1)} %add_convert_fusion.6), channel_id=1, source_target_pairs={{0,2},{2,4},{4,6},{6,7},{7,5},{5,3},{3,1},{1,0},{8,10},{10,12},{12... | collective-permute-start | bytes 1671176 | tf_op jit(solution)/shard_map/ppermute | solution.py:275
  179.2 41.6 %collective-permute-start.27 = (bf16[1,512,768]{2,1,0:T(8,128)(2,1)}, bf16[1,512,768]{2,1,0:T(8,128)(2,1)}, u32[]{:S(2)}, u32[]{:S(2)}) collective-permute-start(bf16[1,512,768]{2,1,0:T(8,128)(2,1)} %add_convert_fusion.1), channel_id=1, source_target_pairs={{0,16},{8,24},{16,0},{24,8},{1,17},{9,25},{17,1},{25,9},{2,18},{10... | collective-permute-start | bytes 2359304 | tf_op jit(solution)/shard_map/ppermute | solution.py:309
  182.0 34.8 %collective-permute-start.29 = (bf16[1,512,768]{2,1,0:T(8,128)(2,1)}, bf16[1,512,768]{2,1,0:T(8,128)(2,1)}, u32[]{:S(2)}, u32[]{:S(2)}) collective-permute-start(bf16[1,512,768]{2,1,0:T(8,128)(2,1)} %add_convert_fusion), channel_id=1, source_target_pairs={{0,16},{8,24},{16,0},{24,8},{1,17},{9,25},{17,1},{25,9},{2,18},{10... | collective-permute-start | bytes 2359304 | tf_op jit(solution)/shard_map/ppermute | solution.py:309
  183.8 47.0 %collective-permute-start.25 = (bf16[1,512,768]{2,1,0:T(8,128)(2,1)}, bf16[1,512,768]{2,1,0:T(8,128)(2,1)}, u32[]{:S(2)}, u32[]{:S(2)}) collective-permute-start(bf16[1,512,768]{2,1,0:T(8,128)(2,1)} %add_convert_fusion.2), channel_id=1, source_target_pairs={{0,16},{8,24},{16,0},{24,8},{1,17},{9,25},{17,1},{25,9},{2,18},{10... | collective-permute-start | bytes 2359304 | tf_op jit(solution)/shard_map/ppermute | solution.py:309
  (24 other events, 327.9 us)

commit v4 on v3

--- a/solution.py
+++ b/solution.py
@@ -70,7 +70,7 @@
             at += ref.shape[0]
 
 
-def expert_blocks(blocks, table, gates, weight_in, weight_out):
+def expert_blocks(blocks, table, gates, weight_in, weight_out, vmem):
     count = len(blocks)
     experts, width, wide = weight_in.shape
     units = weight_out.shape[1]
@@ -106,7 +106,7 @@
             bytes_accessed=2 * experts * width * (wide + units) + 8 * rows * width,
             transcendentals=0,
         ),
-        compiler_params=pltpu.CompilerParams(vmem_limit_bytes=VMEM_BYTES),
+        compiler_params=pltpu.CompilerParams(vmem_limit_bytes=vmem),
         name="experts",
     )(table, *[b[4] for b in blocks], *[gates] * count, *[b[3] for b in blocks], weight_in, weight_out)
     return out[0], out[1], out[2:]
@@ -262,9 +262,12 @@
 
     groups = [blocks[:3]] + [blocks[i : i + 2] for i in range(3, len(blocks), 2)]
     results = []
-    for group in groups:
+    for number, group in enumerate(groups):
         results.append(
-            expert_blocks(group, table, gates, gate_up_weight, down_weight)
+            expert_blocks(
+                group, table, gates, gate_up_weight, down_weight,
+                VMEM_BYTES if number == half - 1 else None,
+            )
         )
     partial_rows = [r for result in results for r in result[2]]
 

time: 235 us -> 229 us (0.974)
  local copies, waits for them, and re-layouts: 8.54 us -> 1.94 us
    slice x2, local copies, waits for them, and re-layouts: 3.36 us -> 0.04 us  [layer(): a[:mid]]
    slice x2, local copies, waits for them, and re-layouts: 3.34 us -> 0.04 us  [layer(): a[mid:]]
  transfers between devices with their start and end apart: 31 -> 31, of which waited for: 9 -> 9; matrix products, arithmetic and copies ran while one was open for 8% -> 5% of each run, Pallas kernels for 30% -> 31%
where the time goes in v4:
time: 229 us
  waiting for transfers between devices  94.8 us (41%)
  Pallas kernels  84.2 us (37%)
  starting transfers between devices  37 us (16%)
  other arithmetic  9.84 us (4%)
    pallas_call x4, Pallas kernels, expert_blocks(): pl.pallas_call(functools.partial(expert_kernel, count, gates.shape[0]), o...  44.9 us
    ppermute x3, waiting for transfers between devices, layer(): pieces.append(lax.ppermute(narrow(both)[None], 'dp', pairs))  31.5 us
    ppermute x4, waiting for transfers between devices, layer(): from_right = lax.ppermute(to_left, 'expert', backward).astype(jnp.float32)  28 us
    pallas_call x3, Pallas kernels, weight_parts(): pl.pallas_call(functools.partial(weight_kernel, x_rows, p_rows, start, de...  27.2 us
    all_to_all x1, waiting for transfers between devices, layer(): lax.all_to_all(dense_gates, 'expert', split_axis=1, concat_axis=0, tiled=...  14.4 us
    pallas_call x3, Pallas kernels, place_chunk(): pl.pallas_call(functools.partial(place_kernel, len(pieces)), out_shape=ja...  12.1 us
    ppermute x4, waiting for transfers between devices, layer(): right = (xr, lax.ppermute(right[1], 'expert', backward))  10.9 us
    ppermute x4, waiting for transfers between devices, layer(): xr = lax.ppermute(right[0], 'expert', backward)  9.15 us
  transfers between devices with their start and end apart: 31, of which 9 were waited for; matrix products, arithmetic and copies ran while one was open for 5% of the time, Pallas kernels for 31%

profile of v4, /device:TPU:0, one launch (start us, length us, event | category | flops | bytes accessed | tf_op | source)
XLA Modules:
  0.0 228.6 jit_solution(3446228500674322002)
XLA Ops:
  0.6 3.0 %collective-permute-start.1 = (bf16[128,2048]{1,0:T(8,128)(2,1)}, bf16[128,2048]{1,0:T(8,128)(2,1)S(1)}, u32[]{:S(2)}, u32[]{:S(2)}) collective-permute-start(bf16[128,2048]{1,0:T(8,128)(2,1)} %refs_0_.6), channel_id=1, source_target_pairs={{2,0},{4,2},{6,4},{7,6},{5,7},{3,5},{1,3},{0,1},{10,8},{12,10},{14... | collective-permute-start | bytes 1572872 | tf_op jit(solution)/shard_map/ppermute | solution.py:256
  3.8 1.9 collective-permute-start.3
  5.8 10.9 %collective-permute-done.1.refs_2_ = bf16[128,2048]{1,0:T(8,128)(2,1)S(1)} collective-permute-done((bf16[128,2048]{1,0:T(8,128)(2,1)}, bf16[128,2048]{1,0:T(8,128)(2,1)S(1)}, u32[]{:S(2)}, u32[]{:S(2)}) %collective-permute-start.1) | collective-permute-done | bytes 524320 | tf_op jit(solution)/shard_map/ppermute | solution.py:256
  16.7 1.9 collective-permute-start.5
  18.8 9.1 %collective-permute-done.3.refs_8_.refs_2_ = bf16[128,2048]{1,0:T(8,128)(2,1)S(1)} collective-permute-done((bf16[128,2048]{1,0:T(8,128)(2,1)}, bf16[128,2048]{1,0:T(8,128)(2,1)S(1)}, u32[]{:S(2)}, u32[]{:S(2)}) %collective-permute-start.3) | collective-permute-done | bytes 524320 | tf_op jit(solution)/shard_map/ppermute | solution.py:254
  28.0 1.9 collective-permute-start.7
  32.1 6.1 %all-to-all-start = ((bf16[128,8,2]{0,2,1:T(2,128)(2,1)}), bf16[128,8,2]{0,2,1:T(2,128)(2,1)S(1)}, u32[]{:S(2)}, u32[]{:S(2)}) async-start(bf16[128,8,2]{0,2,1:T(2,128)(2,1)} %bitcast.1), calls=%async_computation | async-start | bytes 8192 | tf_op jit(solution)/shard_map/all_to_all | solution.py:241
  39.6 14.4 %all-to-all-done = bf16[128,8,2]{0,2,1:T(2,128)(2,1)S(1)} async-done(((bf16[128,8,2]{0,2,1:T(2,128)(2,1)}), bf16[128,8,2]{0,2,1:T(2,128)(2,1)S(1)}, u32[]{:S(2)}, u32[]{:S(2)}) %all-to-all-start) | async-done | bytes 4128 | tf_op jit(solution)/shard_map/all_to_all | solution.py:241
  59.0 14.2 %experts.4 = (bf16[2,384,768]{2,1,0:T(8,128)(2,1)}, bf16[2,384,384]{2,1,0:T(8,128)(2,1)}, bf16[128,2176]{1,0:T(8,128)(2,1)}, bf16[128,2176]{1,0:T(8,128)(2,1)}, bf16[128,2176]{1,0:T(8,128)(2,1)}) custom-call(s32[9]{0:T(128)} %pad_add_fusion.scalars, bf16[128,2048]{1,0:T(8,128)(2,1)} %refs_0_.6, bf16[128,2048]{1,0:T(8,128)(2,1)} %copy-done.20, ...), custom_call_target="tpu_custom_call" | custom-call | flops 6039797760 | bytes 15728640 | tf_op jit(solution)/shard_map/experts/pallas_call | solution.py:86
  73.2 11.0 %experts.5 = (bf16[2,256,768]{2,1,0:T(8,128)(2,1)}, bf16[2,256,384]{2,1,0:T(8,128)(2,1)}, bf16[128,2176]{1,0:T(8,128)(2,1)}, bf16[128,2176]{1,0:T(8,128)(2,1)}) custom-call(s32[9]{0:T(128)} %pad_add_fusion.scalars, bf16[128,2048]{1,0:T(8,128)(2,1)} %collective-permute-done.4.refs_0_.refs_3_, bf16[128,2048]{1,0:T(8,128)(2,1)} %collective-permute-done.5.refs_1_.refs_4_, ...), custom_call_target="tpu_custom_call" | custom-call | flops 4026531840 | bytes 13631488 | tf_op jit(solution)/shard_map/experts/pallas_call | solution.py:86
  88.8 10.9 %experts.6 = (bf16[2,256,768]{2,1,0:T(8,128)(2,1)}, bf16[2,256,384]{2,1,0:T(8,128)(2,1)}, bf16[128,2176]{1,0:T(8,128)(2,1)}, bf16[128,2176]{1,0:T(8,128)(2,1)}) custom-call(s32[9]{0:T(128)} %pad_add_fusion.scalars, bf16[128,2048]{1,0:T(8,128)(2,1)} %copy-done.15, bf16[128,2048]{1,0:T(8,128)(2,1)} %copy-done.14, bf16[8,128,2]{2,1,0:T(8,128)(2,1)} %bitcast.8, ...), custom_call_target="tpu_custom_call" | custom-call | flops 4026531840 | bytes 13631488 | tf_op jit(solution)/shard_map/experts/pallas_call | solution.py:86
  99.8 8.7 %experts.7 = (bf16[2,128,768]{2,1,0:T(8,128)(2,1)}, bf16[2,128,384]{2,1,0:T(8,128)(2,1)}, bf16[64,2176]{1,0:T(8,128)(2,1)}, bf16[64,2176]{1,0:T(8,128)(2,1)}) custom-call(s32[9]{0:T(128)} %pad_add_fusion.scalars, bf16[64,2048]{1,0:T(8,128)(2,1)} %collective-permute-done.12.refs_0_.refs_7_, bf16[64,2048]{1,0:T(8,128)(2,1)} %collective-permute-done.13.refs_1_.refs_8_, ...), custom_call_target="tpu_custom_call" | custom-call | flops 2013265920 | bytes 11534336 | tf_op jit(solution)/shard_map/experts/pallas_call | solution.py:86
  110.6 9.1 %weights.4 = (bf16[2,512,768]{2,1,0:T(8,128)(2,1)}, bf16[2,512,768]{2,1,0:T(8,128)(2,1)}) custom-call(bf16[128,2048]{1,0:T(8,128)(2,1)} %refs_0_.6, bf16[128,2048]{1,0:T(8,128)(2,1)} %copy-done.20, bf16[128,2048]{1,0:T(8,128)(2,1)} %copy-done.19, bf16[128,2048]{1,0:T(8,128)(2,1)} %collective-permute-done.4.refs_0_.refs_3_, ...), custom_call_target="tpu_custom_call" | custom-call | flops 3221225472 | bytes 8912896 | tf_op jit(solution)/shard_map/weights/pallas_call | solution.py:173
  119.8 9.1 %weights.5 = (bf16[2,512,768]{2,1,0:T(8,128)(2,1)}, bf16[2,512,768]{2,1,0:T(8,128)(2,1)}) custom-call(bf16[128,2048]{1,0:T(8,128)(2,1)} %refs_0_.7, bf16[128,2048]{1,0:T(8,128)(2,1)} %copy-done.18, bf16[128,2048]{1,0:T(8,128)(2,1)} %copy-done.17, bf16[128,2048]{1,0:T(8,128)(2,1)} %collective-permute-done.6.refs_4_.refs_3_, ...), custom_call_target="tpu_custom_call" | custom-call | flops 3221225472 | bytes 8912896 | tf_op jit(solution)/shard_map/weights/pallas_call | solution.py:173
  129.4 9.0 %weights.3 = (bf16[2,512,768]{2,1,0:T(8,128)(2,1)}, bf16[2,512,768]{2,1,0:T(8,128)(2,1)}) custom-call(bf16[128,2048]{1,0:T(8,128)(2,1)} %refs_0_.7, bf16[128,2048]{1,0:T(8,128)(2,1)} %copy-done.18, bf16[128,2048]{1,0:T(8,128)(2,1)} %copy-done.17, bf16[128,2048]{1,0:T(8,128)(2,1)} %collective-permute-done.6.refs_4_.refs_3_, ...), custom_call_target="tpu_custom_call" | custom-call | flops 3221225472 | bytes 8912896 | tf_op jit(solution)/shard_map/weights/pallas_call | solution.py:173
  142.1 12.8 %collective-permute-done.17 = bf16[128,2176]{1,0:T(8,128)(2,1)S(1)} collective-permute-done((bf16[128,2176]{1,0:T(8,128)(2,1)S(1)}, bf16[128,2176]{1,0:T(8,128)(2,1)S(1)}, u32[]{:S(2)}, u32[]{:S(2)}) %collective-permute-start.17) | collective-permute-done | bytes 557088 | tf_op jit(solution)/shard_map/ppermute | solution.py:277
  157.3 11.8 %collective-permute-done.18 = bf16[128,2176]{1,0:T(8,128)(2,1)S(1)} collective-permute-done((bf16[128,2176]{1,0:T(8,128)(2,1)S(1)}, bf16[128,2176]{1,0:T(8,128)(2,1)S(1)}, u32[]{:S(2)}, u32[]{:S(2)}) %collective-permute-start.18) | collective-permute-done | bytes 557088 | tf_op jit(solution)/shard_map/ppermute | solution.py:277
  170.0 1.7 collective-permute-start.23
  179.1 3.4 %collective-permute-done.19 = bf16[128,2176]{1,0:T(8,128)(2,1)S(1)} collective-permute-done((bf16[128,2176]{1,0:T(8,128)(2,1)S(1)}, bf16[128,2176]{1,0:T(8,128)(2,1)S(1)}, u32[]{:S(2)}, u32[]{:S(2)}) %collective-permute-start.19) | collective-permute-done | bytes 557088 | tf_op jit(solution)/shard_map/ppermute | solution.py:277
  185.0 25.6 %collective-permute-done.29.refs_2_ = bf16[1,512,768]{2,1,0:T(8,128)(2,1)} collective-permute-done((bf16[1,512,768]{2,1,0:T(8,128)(2,1)}, bf16[1,512,768]{2,1,0:T(8,128)(2,1)}, u32[]{:S(2)}, u32[]{:S(2)}) %collective-permute-start.29) | collective-permute-done | bytes 786464 | tf_op jit(solution)/shard_map/ppermute | solution.py:312
  210.6 4.0 %place.3.refs_3_ = bf16[512,2,1152]{2,1,0:T(2,128)(2,1)} custom-call(bf16[2,512,768]{2,1,0:T(8,128)(2,1)} %get-tuple-element.47.refs_0_, bf16[2,512,768]{2,1,0:T(8,128)(2,1)} %copy-done.1, bf16[1,512,768]{2,1,0:T(8,128)(2,1)} %collective-permute-done.29.refs_2_), custom_call_target="tpu_custom_call" | custom-call | tf_op jit(solution)/shard_map/place/pallas_call | solution.py:213
  214.6 4.0 %place.4.refs_3_ = bf16[512,2,1152]{2,1,0:T(2,128)(2,1)} custom-call(bf16[2,512,768]{2,1,0:T(8,128)(2,1)} %get-tuple-element.45.refs_0_, bf16[2,512,768]{2,1,0:T(8,128)(2,1)} %copy-done.3, bf16[1,512,768]{2,1,0:T(8,128)(2,1)} %collective-permute-done.27.refs_2_, bf16[512,2,1152]{2,1,0:T(2,128)(2,1)} %place.3.refs_3_), custom_call_target="tpu_custom_call", output_to_operand_aliasing={{}: (3, {})} | custom-call | tf_op jit(solution)/shard_map/place/pallas_call | solution.py:213
  218.7 5.9 %collective-permute-done.25.refs_2_ = bf16[1,512,768]{2,1,0:T(8,128)(2,1)} collective-permute-done((bf16[1,512,768]{2,1,0:T(8,128)(2,1)}, bf16[1,512,768]{2,1,0:T(8,128)(2,1)}, u32[]{:S(2)}, u32[]{:S(2)}) %collective-permute-start.25) | collective-permute-done | bytes 786464 | tf_op jit(solution)/shard_map/ppermute | solution.py:312
  224.6 4.0 %place.5 = bf16[512,2,1152]{2,1,0:T(2,128)(2,1)} custom-call(bf16[2,512,768]{2,1,0:T(8,128)(2,1)} %get-tuple-element.39.refs_0_, bf16[2,512,768]{2,1,0:T(8,128)(2,1)} %copy-done.5, bf16[1,512,768]{2,1,0:T(8,128)(2,1)} %collective-permute-done.25.refs_2_, bf16[512,2,1152]{2,1,0:T(2,128)(2,1)} %place.4.refs_3_), custom_call_target="tpu_custom_call", output_to_operand_aliasing={{}: (3, {})} | custom-call | tf_op jit(solution)/shard_map/place/pallas_call | solution.py:213
  (114 shorter events, 32.8 us)
Async XLA Ops:
  0.6 16.1 %collective-permute-start.1 = (bf16[128,2048]{1,0:T(8,128)(2,1)}, bf16[128,2048]{1,0:T(8,128)(2,1)S(1)}, u32[]{:S(2)}, u32[]{:S(2)}) collective-permute-start(bf16[128,2048]{1,0:T(8,128)(2,1)} %refs_0_.6), channel_id=1, source_target_pairs={{2,0},{4,2},{6,4},{7,6},{5,7},{3,5},{1,3},{0,1},{10,8},{12,10},{14... | collective-permute-start | bytes 1572872 | tf_op jit(solution)/shard_map/ppermute | solution.py:256
  3.6 15.0 %collective-permute-start = (bf16[128,2048]{1,0:T(8,128)(2,1)}, bf16[128,2048]{1,0:T(8,128)(2,1)S(1)}, u32[]{:S(2)}, u32[]{:S(2)}) collective-permute-start(bf16[128,2048]{1,0:T(8,128)(2,1)} %refs_0_.6), channel_id=1, source_target_pairs={{0,2},{2,4},{4,6},{6,7},{7,5},{5,3},{3,1},{1,0},{8,10},{10,12},{12... | collective-permute-start | bytes 1572872 | tf_op jit(solution)/shard_map/ppermute | solution.py:255
  3.8 24.2 %collective-permute-start.3 = (bf16[128,2048]{1,0:T(8,128)(2,1)}, bf16[128,2048]{1,0:T(8,128)(2,1)S(1)}, u32[]{:S(2)}, u32[]{:S(2)}) collective-permute-start(bf16[128,2048]{1,0:T(8,128)(2,1)} %refs_0_.7), channel_id=1, source_target_pairs={{2,0},{4,2},{6,4},{7,6},{5,7},{3,5},{1,3},{0,1},{10,8},{12,10},{14... | collective-permute-start | bytes 1572872 | tf_op jit(solution)/shard_map/ppermute | solution.py:254
  5.7 24.2 %collective-permute-start.2 = (bf16[128,2048]{1,0:T(8,128)(2,1)}, bf16[128,2048]{1,0:T(8,128)(2,1)S(1)}, u32[]{:S(2)}, u32[]{:S(2)}) collective-permute-start(bf16[128,2048]{1,0:T(8,128)(2,1)} %refs_0_.7), channel_id=1, source_target_pairs={{0,2},{2,4},{4,6},{6,7},{7,5},{5,3},{3,1},{1,0},{8,10},{10,12},{12... | collective-permute-start | bytes 1572872 | tf_op jit(solution)/shard_map/ppermute | solution.py:253
  16.7 38.2 %collective-permute-start.5 = (bf16[128,2048]{1,0:T(8,128)(2,1)S(1)}, bf16[128,2048]{1,0:T(8,128)(2,1)}, u32[]{:S(2)}, u32[]{:S(2)}) collective-permute-start(bf16[128,2048]{1,0:T(8,128)(2,1)S(1)} %collective-permute-done.1.refs_2_), channel_id=1, source_target_pairs={{2,0},{4,2},{6,4},{7,6},{5,7},{3,5},{1,3},{0,1},{10,8},{12,10},{14... | collective-permute-start | bytes 1572872 | tf_op jit(solution)/shard_map/ppermute | solution.py:256
  18.7 36.8 %collective-permute-start.4 = (bf16[128,2048]{1,0:T(8,128)(2,1)S(1)}, bf16[128,2048]{1,0:T(8,128)(2,1)}, u32[]{:S(2)}, u32[]{:S(2)}) collective-permute-start(bf16[128,2048]{1,0:T(8,128)(2,1)S(1)} %collective-permute-done.refs_1_), channel_id=1, source_target_pairs={{0,2},{2,4},{4,6},{6,7},{7,5},{5,3},{3,1},{1,0},{8,10},{10,12},{12... | collective-permute-start | bytes 1572872 | tf_op jit(solution)/shard_map/ppermute | solution.py:255
  28.0 29.0 %collective-permute-start.7 = (bf16[128,2048]{1,0:T(8,128)(2,1)S(1)}, bf16[128,2048]{1,0:T(8,128)(2,1)}, u32[]{:S(2)}, u32[]{:S(2)}) collective-permute-start(bf16[128,2048]{1,0:T(8,128)(2,1)S(1)} %collective-permute-done.3.refs_8_.refs_2_), channel_id=1, source_target_pairs={{2,0},{4,2},{6,4},{7,6},{5,7},{3,5},{1,3},{0,1},{10,8},{12,10},{14... | collective-permute-start | bytes 1572872 | tf_op jit(solution)/shard_map/ppermute | solution.py:254
  29.9 27.6 %collective-permute-start.6 = (bf16[128,2048]{1,0:T(8,128)(2,1)S(1)}, bf16[128,2048]{1,0:T(8,128)(2,1)}, u32[]{:S(2)}, u32[]{:S(2)}) collective-permute-start(bf16[128,2048]{1,0:T(8,128)(2,1)S(1)} %collective-permute-done.2.refs_7_.refs_1_), channel_id=1, source_target_pairs={{0,2},{2,4},{4,6},{6,7},{7,5},{5,3},{3,1},{1,0},{8,10},{10,12},{12... | collective-permute-start | bytes 1572872 | tf_op jit(solution)/shard_map/ppermute | solution.py:253
  32.1 22.0 %all-to-all-start = ((bf16[128,8,2]{0,2,1:T(2,128)(2,1)}), bf16[128,8,2]{0,2,1:T(2,128)(2,1)S(1)}, u32[]{:S(2)}, u32[]{:S(2)}) async-start(bf16[128,8,2]{0,2,1:T(2,128)(2,1)} %bitcast.1), calls=%async_computation | async-start | bytes 8192 | tf_op jit(solution)/shard_map/all_to_all | solution.py:241
  54.9 29.3 %collective-permute-start.9 = (bf16[128,2048]{1,0:T(8,128)(2,1)}, bf16[128,2048]{1,0:T(8,128)(2,1)S(1)}, u32[]{:S(2)}, u32[]{:S(2)}) collective-permute-start(bf16[128,2048]{1,0:T(8,128)(2,1)} %collective-permute-done.5.refs_1_.refs_4_), channel_id=1, source_target_pairs={{2,0},{4,2},{6,4},{7,6},{5,7},{3,5},{1,3},{0,1},{10,8},{12,10},{14... | collective-permute-start | bytes 1572872 | tf_op jit(solution)/shard_map/ppermute | solution.py:256
  55.5 29.4 %collective-permute-start.8 = (bf16[128,2048]{1,0:T(8,128)(2,1)}, bf16[128,2048]{1,0:T(8,128)(2,1)S(1)}, u32[]{:S(2)}, u32[]{:S(2)}) collective-permute-start(bf16[128,2048]{1,0:T(8,128)(2,1)} %collective-permute-done.4.refs_0_.refs_3_), channel_id=1, source_target_pairs={{0,2},{2,4},{4,6},{6,7},{7,5},{5,3},{3,1},{1,0},{8,10},{10,12},{12... | collective-permute-start | bytes 1572872 | tf_op jit(solution)/shard_map/ppermute | solution.py:255
  57.0 29.5 %collective-permute-start.11 = (bf16[128,2048]{1,0:T(8,128)(2,1)}, bf16[128,2048]{1,0:T(8,128)(2,1)S(1)}, u32[]{:S(2)}, u32[]{:S(2)}) collective-permute-start(bf16[128,2048]{1,0:T(8,128)(2,1)} %collective-permute-done.7.refs_5_.refs_4_), channel_id=1, source_target_pairs={{2,0},{4,2},{6,4},{7,6},{5,7},{3,5},{1,3},{0,1},{10,8},{12,10},{14... | collective-permute-start | bytes 1572872 | tf_op jit(solution)/shard_map/ppermute | solution.py:254
  57.5 29.5 %collective-permute-start.10 = (bf16[128,2048]{1,0:T(8,128)(2,1)}, bf16[128,2048]{1,0:T(8,128)(2,1)S(1)}, u32[]{:S(2)}, u32[]{:S(2)}) collective-permute-start(bf16[128,2048]{1,0:T(8,128)(2,1)} %collective-permute-done.6.refs_4_.refs_3_), channel_id=1, source_target_pairs={{0,2},{2,4},{4,6},{6,7},{7,5},{5,3},{3,1},{1,0},{8,10},{10,12},{12... | collective-permute-start | bytes 1572872 | tf_op jit(solution)/shard_map/ppermute | solution.py:253
  84.3 15.5 %collective-permute-start.13 = (bf16[64,2048]{1,0:T(8,128)(2,1)S(1)}, bf16[64,2048]{1,0:T(8,128)(2,1)}, u32[]{:S(2)}, u32[]{:S(2)}) collective-permute-start(bf16[64,2048]{1,0:T(8,128)(2,1)S(1)} %slice.49), channel_id=1, source_target_pairs={{2,0},{4,2},{6,4},{7,6},{5,7},{3,5},{1,3},{0,1},{10,8},{12,10},{14... | collective-permute-start | bytes 786440 | tf_op jit(solution)/shard_map/ppermute | solution.py:256
  108.5 30.1 %collective-permute-start.16 = (bf16[64,2176]{1,0:T(8,128)(2,1)}, bf16[64,2176]{1,0:T(8,128)(2,1)}, u32[]{:S(2)}, u32[]{:S(2)}) collective-permute-start(bf16[64,2176]{1,0:T(8,128)(2,1)} %get-tuple-element.30), channel_id=1, source_target_pairs={{2,0},{4,2},{6,4},{7,6},{5,7},{3,5},{1,3},{0,1},{10,8},{12,10},{14... | collective-permute-start | bytes 835592 | tf_op jit(solution)/shard_map/ppermute | solution.py:277
  109.1 31.3 %collective-permute-start.20 = (bf16[64,2176]{1,0:T(8,128)(2,1)}, bf16[64,2176]{1,0:T(8,128)(2,1)S(1)}, u32[]{:S(2)}, u32[]{:S(2)}) collective-permute-start(bf16[64,2176]{1,0:T(8,128)(2,1)} %get-tuple-element.34), channel_id=1, source_target_pairs={{0,2},{2,4},{4,6},{6,7},{7,5},{5,3},{3,1},{1,0},{8,10},{10,12},{12... | collective-permute-start | bytes 835592 | tf_op jit(solution)/shard_map/ppermute | solution.py:278
  119.7 52.1 %collective-permute-start.26 = (bf16[2,512,768]{2,1,0:T(8,128)(2,1)}, bf16[2,512,768]{2,1,0:T(8,128)(2,1)S(1)}, u32[]{:S(2)}, u32[]{:S(2)}) collective-permute-start(bf16[2,512,768]{2,1,0:T(8,128)(2,1)} %get-tuple-element.46), channel_id=1, source_target_pairs={{0,8},{8,0},{16,24},{24,16},{1,9},{9,1},{17,25},{25,17},{2,10},{10... | collective-permute-start | bytes 4718600 | tf_op jit(solution)/shard_map/ppermute | solution.py:305
  128.9 45.6 %collective-permute-start.28 = (bf16[2,512,768]{2,1,0:T(8,128)(2,1)}, bf16[2,512,768]{2,1,0:T(8,128)(2,1)S(1)}, u32[]{:S(2)}, u32[]{:S(2)}) collective-permute-start(bf16[2,512,768]{2,1,0:T(8,128)(2,1)} %get-tuple-element.48), channel_id=1, source_target_pairs={{0,8},{8,0},{16,24},{24,16},{1,9},{9,1},{17,25},{25,17},{2,10},{10... | collective-permute-start | bytes 4718600 | tf_op jit(solution)/shard_map/ppermute | solution.py:305
  138.5 37.8 %collective-permute-start.24 = (bf16[2,512,768]{2,1,0:T(8,128)(2,1)}, bf16[2,512,768]{2,1,0:T(8,128)(2,1)S(1)}, u32[]{:S(2)}, u32[]{:S(2)}) collective-permute-start(bf16[2,512,768]{2,1,0:T(8,128)(2,1)} %get-tuple-element.40), channel_id=1, source_target_pairs={{0,8},{8,0},{16,24},{24,16},{1,9},{9,1},{17,25},{25,17},{2,10},{10... | collective-permute-start | bytes 4718600 | tf_op jit(solution)/shard_map/ppermute | solution.py:305
  139.9 15.0 %collective-permute-start.17 = (bf16[128,2176]{1,0:T(8,128)(2,1)S(1)}, bf16[128,2176]{1,0:T(8,128)(2,1)S(1)}, u32[]{:S(2)}, u32[]{:S(2)}) collective-permute-start(bf16[128,2176]{1,0:T(8,128)(2,1)S(1)} %add_convert_fusion.9), channel_id=1, source_target_pairs={{2,0},{4,2},{6,4},{7,6},{5,7},{3,5},{1,3},{0,1},{10,8},{12,10},{14... | collective-permute-start | bytes 1671176 | tf_op jit(solution)/shard_map/ppermute | solution.py:277
  140.6 15.0 %collective-permute-start.21 = (bf16[128,2176]{1,0:T(8,128)(2,1)S(1)}, bf16[128,2176]{1,0:T(8,128)(2,1)S(1)}, u32[]{:S(2)}, u32[]{:S(2)}) collective-permute-start(bf16[128,2176]{1,0:T(8,128)(2,1)S(1)} %add_convert_fusion.6), channel_id=1, source_target_pairs={{0,2},{2,4},{4,6},{6,7},{7,5},{5,3},{3,1},{1,0},{8,10},{10,12},{12... | collective-permute-start | bytes 1671176 | tf_op jit(solution)/shard_map/ppermute | solution.py:278
  173.0 41.6 %collective-permute-start.27 = (bf16[1,512,768]{2,1,0:T(8,128)(2,1)}, bf16[1,512,768]{2,1,0:T(8,128)(2,1)}, u32[]{:S(2)}, u32[]{:S(2)}) collective-permute-start(bf16[1,512,768]{2,1,0:T(8,128)(2,1)} %add_convert_fusion.1), channel_id=1, source_target_pairs={{0,16},{8,24},{16,0},{24,8},{1,17},{9,25},{17,1},{25,9},{2,18},{10... | collective-permute-start | bytes 2359304 | tf_op jit(solution)/shard_map/ppermute | solution.py:312
  175.8 34.8 %collective-permute-start.29 = (bf16[1,512,768]{2,1,0:T(8,128)(2,1)}, bf16[1,512,768]{2,1,0:T(8,128)(2,1)}, u32[]{:S(2)}, u32[]{:S(2)}) collective-permute-start(bf16[1,512,768]{2,1,0:T(8,128)(2,1)} %add_convert_fusion), channel_id=1, source_target_pairs={{0,16},{8,24},{16,0},{24,8},{1,17},{9,25},{17,1},{25,9},{2,18},{10... | collective-permute-start | bytes 2359304 | tf_op jit(solution)/shard_map/ppermute | solution.py:312
  177.6 47.0 %collective-permute-start.25 = (bf16[1,512,768]{2,1,0:T(8,128)(2,1)}, bf16[1,512,768]{2,1,0:T(8,128)(2,1)}, u32[]{:S(2)}, u32[]{:S(2)}) collective-permute-start(bf16[1,512,768]{2,1,0:T(8,128)(2,1)} %add_convert_fusion.2), channel_id=1, source_target_pairs={{0,16},{8,24},{16,0},{24,8},{1,17},{9,25},{17,1},{25,9},{2,18},{10... | collective-permute-start | bytes 2359304 | tf_op jit(solution)/shard_map/ppermute | solution.py:312
  (28 other events, 339.4 us)

commit v5 on v4

--- a/solution.py
+++ b/solution.py
@@ -112,9 +112,43 @@
     return out[0], out[1], out[2:]
 
 
-def weight_kernel(x_rows, p_rows, start, depth, *refs):
+def begun_kernel(nx, *refs):
+    p_refs = refs[nx:-1]
+    experts = p_refs[0].shape[0]
+    right = [jnp.concatenate([ref[e] for ref in p_refs], axis=0) for e in range(experts)]
+    refs[-1][...] = lax.dot_general(
+        joined(refs[:nx]),
+        jnp.concatenate(right, axis=1),
+        (((0,), (0,)), ((), ())),
+        preferred_element_type=jnp.float32,
+    ).astype(jnp.bfloat16)
+
+
+def begun_weights(xs, ps, size):
+    width, experts = xs[0].shape[1], ps[0].shape[0]
+    depth, columns = width // 4, experts * size
+    rows = sum(x.shape[0] for x in xs)
+    return pl.pallas_call(
+        functools.partial(begun_kernel, len(xs)),
+        out_shape=jax.ShapeDtypeStruct((width, columns), jnp.bfloat16),
+        grid=(width // depth,),
+        in_specs=[pl.BlockSpec((x.shape[0], depth), lambda i: (0, i)) for x in xs]
+        + [pl.BlockSpec((experts, p.shape[1], size), lambda i: (0, 0, 0)) for p in ps],
+        out_specs=pl.BlockSpec((depth, columns), lambda i: (i, 0)),
+        cost_estimate=pl.CostEstimate(
+            flops=2 * rows * width * columns,
+            bytes_accessed=2 * (rows * (width + columns) + width * columns),
+            transcendentals=0,
+        ),
+        name="begun",
+    )(*xs, *ps)
+
+
+def weight_kernel(x_rows, p_rows, start, depth, begun_count, *refs):
     x_refs, p_refs = refs[: len(x_rows)], refs[len(x_rows) : len(x_rows) + len(p_rows)]
-    sent, kept, held, gradients, result, x_sems, p_sems, sems = refs[len(x_rows) + len(p_rows) :]
+    begun = refs[len(x_rows) + len(p_rows) :][:begun_count]
+    refs = refs[len(x_rows) + len(p_rows) + begun_count :]
+    sent, kept, held, gradients, result, x_sems, p_sems, sems = refs[:8]
     outer, experts = sent.shape[0], p_refs[0].shape[0]
     size = sent.shape[2] // experts
 
@@ -132,6 +166,10 @@
                     x_sems.at[i, place, k],
                 )
                 row += n
+            for ref in begun:
+                yield pltpu.make_async_copy(
+                    ref.at[pl.ds(column, depth), :], refs[8].at[i, place], refs[9].at[i, place]
+                )
 
     def gradient_copies():
         row = 0
@@ -155,14 +193,17 @@
         part = lax.dot_general(
             held[i], gradients[...], (((0,), (0,)), ((), ())), preferred_element_type=jnp.float32
         )
-        result[i] = part.astype(jnp.bfloat16).reshape(result.shape[1:])
+        part = part.reshape(result.shape[1:])
+        if begun:
+            part += refs[8][i].astype(jnp.float32)
+        result[i] = part.astype(jnp.bfloat16)
         stores.append(pltpu.make_async_copy(result.at[i], out, sems.at[i]))
         stores[-1].start()
     for store in stores:
         store.wait()
 
 
-def weight_parts(xs, ps, start, size, replicas):
+def weight_parts(xs, ps, start, size, replicas, *begun):
     width = xs[0].shape[1]
     experts = ps[0].shape[0]
     outer, depth = replicas // 2, width // replicas
@@ -171,9 +212,9 @@
 
     anywhere = pl.BlockSpec(memory_space=pl.ANY)
     return pl.pallas_call(
-        functools.partial(weight_kernel, x_rows, p_rows, start, depth),
+        functools.partial(weight_kernel, x_rows, p_rows, start, depth, len(begun)),
         out_shape=[jax.ShapeDtypeStruct((outer, depth, columns), jnp.bfloat16)] * 2,
-        in_specs=[anywhere] * (len(xs) + len(ps)),
+        in_specs=[anywhere] * (len(xs) + len(ps) + len(begun)),
         out_specs=[anywhere] * 2,
         scratch_shapes=[
             pltpu.VMEM((2, rows, outer * depth), jnp.bfloat16),
@@ -182,14 +223,19 @@
             pltpu.SemaphoreType.DMA((2, outer, len(xs))),
             pltpu.SemaphoreType.DMA((len(ps), experts)),
             pltpu.SemaphoreType.DMA((2,)),
-        ],
+        ]
+        + [
+            pltpu.VMEM((2, outer, depth, columns), jnp.bfloat16),
+            pltpu.SemaphoreType.DMA((2, outer)),
+        ]
+        * len(begun),
         cost_estimate=pl.CostEstimate(
             flops=2 * rows * width * columns,
             bytes_accessed=2 * (rows * (width + columns) + width * columns),
             transcendentals=0,
         ),
         name="weights",
-    )(*xs, *ps)
+    )(*xs, *ps, *begun)
 
 
 def place_kernel(count, *refs):
@@ -296,8 +342,9 @@
     units = down_weight.shape[1]
     chunks = [(xs, pres, 0, units), (gs, hiddens, 0, units), (xs, pres, units, units)]
     places = [0, 2, 1]
-    parts = []
-    for chunk in chunks:
+    begun = begun_weights(xs[:-4], pres[:-2], units)
+    parts = weight_parts(xs[-4:], pres[-2:], 0, units, replicas, begun)
+    for number, chunk in enumerate(chunks[1:], 1):
         parts += weight_parts(*chunk, replicas)
     weight_total = None
     for number, at in enumerate(places):

time: 229 us -> 230 us (level)
  Pallas kernels: 84.2 us -> 88 us
  waiting for transfers between devices: 94.8 us -> 91.2 us
    ppermute x4, waiting for transfers between devices: 10.9 us -> 0.01 us  [layer(): right = (xr, lax.ppermute(right[1], 'expert', backward))]
    ppermute x3, waiting for transfers between devices: 31.5 us -> 39.7 us  [layer(): pieces.append(lax.ppermute(narrow(both)[None], 'dp', pairs))]
    pallas_call x0 -> x1, Pallas kernels: none -> 6.5 us  [begun_weights(): pl.pallas_call(functools.partial(begun_kernel, len(xs)), out_shape=jax.Sh...]
    ppermute x4, waiting for transfers between devices: 9.15 us -> 5.64 us  [layer(): xr = lax.ppermute(right[0], 'expert', backward)]
    pallas_call x3, Pallas kernels: 27.2 us -> 24.6 us  [weight_parts(): pl.pallas_call(functools.partial(weight_kernel, x_rows, p_rows, start, de...]
  transfers between devices with their start and end apart: 31 -> 31, of which waited for: 9 -> 7; matrix products, arithmetic and copies ran while one was open for 5% -> 5% of each run, Pallas kernels for 31% -> 33%
where the time goes in v5:
time: 230 us
  waiting for transfers between devices  91.2 us (40%)
  Pallas kernels  88 us (38%)
  starting transfers between devices  37 us (16%)
  other arithmetic  8.78 us (4%)
  local copies, waits for them, and re-layouts  3.83 us (2%)
    pallas_call x4, Pallas kernels, expert_blocks(): pl.pallas_call(functools.partial(expert_kernel, count, gates.shape[0]), o...  44.8 us
    ppermute x3, waiting for transfers between devices, layer(): pieces.append(lax.ppermute(narrow(both)[None], 'dp', pairs))  39.7 us
    ppermute x4, waiting for transfers between devices, layer(): from_right = lax.ppermute(to_left, 'expert', backward).astype(jnp.float32)  29 us
    pallas_call x3, Pallas kernels, weight_parts(): pl.pallas_call(functools.partial(weight_kernel, x_rows, p_rows, start, de...  24.6 us
    all_to_all x1, waiting for transfers between devices, layer(): lax.all_to_all(dense_gates, 'expert', split_axis=1, concat_axis=0, tiled=...  16.1 us
    pallas_call x3, Pallas kernels, place_chunk(): pl.pallas_call(functools.partial(place_kernel, len(pieces)), out_shape=ja...  12.1 us
    pallas_call x1, Pallas kernels, begun_weights(): pl.pallas_call(functools.partial(begun_kernel, len(xs)), out_shape=jax.Sh...  6.5 us
    ppermute x4, starting transfers between devices, layer(): from_left = lax.ppermute(to_right, 'expert', forward).astype(jnp.float32)  6.26 us
  transfers between devices with their start and end apart: 31, of which 7 were waited for; matrix products, arithmetic and copies ran while one was open for 5% of the time, Pallas kernels for 33%

profile of v5, /device:TPU:0, one launch (start us, length us, event | category | flops | bytes accessed | tf_op | source)
XLA Modules:
  0.0 229.8 jit_solution(5958095529153889683)
XLA Ops:
  0.6 3.0 %collective-permute-start.1 = (bf16[128,2048]{1,0:T(8,128)(2,1)}, bf16[128,2048]{1,0:T(8,128)(2,1)S(1)}, u32[]{:S(2)}, u32[]{:S(2)}) collective-permute-start(bf16[128,2048]{1,0:T(8,128)(2,1)} %refs_0_.6), channel_id=1, source_target_pairs={{2,0},{4,2},{6,4},{7,6},{5,7},{3,5},{1,3},{0,1},{10,8},{12,10},{14... | collective-permute-start | bytes 1572872 | tf_op jit(solution)/shard_map/ppermute | solution.py:302
  3.8 1.9 collective-permute-start.3
  7.8 6.2 %all-to-all-start = ((bf16[128,8,2]{0,2,1:T(2,128)(2,1)}), bf16[128,8,2]{0,2,1:T(2,128)(2,1)S(1)}, u32[]{:S(2)}, u32[]{:S(2)}) async-start(bf16[128,8,2]{0,2,1:T(2,128)(2,1)} %bitcast.1), calls=%async_computation | async-start | bytes 8192 | tf_op jit(solution)/shard_map/all_to_all | solution.py:287
  15.4 16.1 %all-to-all-done = bf16[128,8,2]{0,2,1:T(2,128)(2,1)S(1)} async-done(((bf16[128,8,2]{0,2,1:T(2,128)(2,1)}), bf16[128,8,2]{0,2,1:T(2,128)(2,1)S(1)}, u32[]{:S(2)}, u32[]{:S(2)}) %all-to-all-start) | async-done | bytes 4128 | tf_op jit(solution)/shard_map/all_to_all | solution.py:287
  36.5 14.2 %experts.4 = (bf16[2,384,768]{2,1,0:T(8,128)(2,1)}, bf16[2,384,384]{2,1,0:T(8,128)(2,1)}, bf16[128,2176]{1,0:T(8,128)(2,1)}, bf16[128,2176]{1,0:T(8,128)(2,1)}, bf16[128,2176]{1,0:T(8,128)(2,1)}) custom-call(s32[9]{0:T(128)} %pad_add_fusion.scalars, bf16[128,2048]{1,0:T(8,128)(2,1)} %refs_0_.6, bf16[128,2048]{1,0:T(8,128)(2,1)} %copy-done.20, ...), custom_call_target="tpu_custom_call" | custom-call | flops 6039797760 | bytes 15728640 | tf_op jit(solution)/shard_map/experts/pallas_call | solution.py:86
  52.9 5.6 %collective-permute-done.7.refs_5_.refs_4_ = bf16[128,2048]{1,0:T(8,128)(2,1)S(1)} collective-permute-done((bf16[128,2048]{1,0:T(8,128)(2,1)S(1)}, bf16[128,2048]{1,0:T(8,128)(2,1)S(1)}, u32[]{:S(2)}, u32[]{:S(2)}) %collective-permute-start.7) | collective-permute-done | bytes 524320 | tf_op jit(solution)/shard_map/ppermute | solution.py:300
  60.5 10.9 %experts.5 = (bf16[2,256,768]{2,1,0:T(8,128)(2,1)}, bf16[2,256,384]{2,1,0:T(8,128)(2,1)}, bf16[128,2176]{1,0:T(8,128)(2,1)}, bf16[128,2176]{1,0:T(8,128)(2,1)}) custom-call(s32[9]{0:T(128)} %pad_add_fusion.scalars, bf16[128,2048]{1,0:T(8,128)(2,1)} %collective-permute-done.4.refs_0_.refs_3_, bf16[128,2048]{1,0:T(8,128)(2,1)} %collective-permute-done.5.refs_1_.refs_4_, ...), custom_call_target="tpu_custom_call" | custom-call | flops 4026531840 | bytes 13631488 | tf_op jit(solution)/shard_map/experts/pallas_call | solution.py:86
  71.5 6.5 %begun.1.refs_6_ = bf16[2048,768]{1,0:T(8,128)(2,1)} custom-call(bf16[128,2048]{1,0:T(8,128)(2,1)} %refs_0_.7, bf16[128,2048]{1,0:T(8,128)(2,1)} %copy-done.15, bf16[128,2048]{1,0:T(8,128)(2,1)} %copy-done.14, bf16[128,2048]{1,0:T(8,128)(2,1)} %copy-done.17, bf16[128,2048]{1,0:T(8,128)(2,1)} %copy-done.16, ...), custom_call_target="tpu_custom_call" | custom-call | flops 2013265920 | bytes 6750208 | tf_op jit(solution)/shard_map/begun/pallas_call | solution.py:131
  82.7 1.7 collective-permute-start.14
  84.4 10.9 %experts.6 = (bf16[2,256,768]{2,1,0:T(8,128)(2,1)}, bf16[2,256,384]{2,1,0:T(8,128)(2,1)}, bf16[128,2176]{1,0:T(8,128)(2,1)}, bf16[128,2176]{1,0:T(8,128)(2,1)}) custom-call(s32[9]{0:T(128)} %pad_add_fusion.scalars, bf16[128,2048]{1,0:T(8,128)(2,1)} %collective-permute-done.8.refs_0_.refs_5_, bf16[128,2048]{1,0:T(8,128)(2,1)} %collective-permute-done.9.refs_1_.refs_6_, ...), custom_call_target="tpu_custom_call" | custom-call | flops 4026531840 | bytes 13631488 | tf_op jit(solution)/shard_map/experts/pallas_call | solution.py:86
  95.4 8.8 %experts.7 = (bf16[2,128,768]{2,1,0:T(8,128)(2,1)}, bf16[2,128,384]{2,1,0:T(8,128)(2,1)}, bf16[64,2176]{1,0:T(8,128)(2,1)}, bf16[64,2176]{1,0:T(8,128)(2,1)}) custom-call(s32[9]{0:T(128)} %pad_add_fusion.scalars, bf16[64,2048]{1,0:T(8,128)(2,1)} %collective-permute-done.12.refs_0_.refs_7_, bf16[64,2048]{1,0:T(8,128)(2,1)} %collective-permute-done.13.refs_1_.refs_8_, ...), custom_call_target="tpu_custom_call" | custom-call | flops 2013265920 | bytes 11534336 | tf_op jit(solution)/shard_map/experts/pallas_call | solution.py:86
  106.2 9.1 %weights.4 = (bf16[2,512,768]{2,1,0:T(8,128)(2,1)}, bf16[2,512,768]{2,1,0:T(8,128)(2,1)}) custom-call(bf16[128,2048]{1,0:T(8,128)(2,1)} %refs_0_.6, bf16[128,2048]{1,0:T(8,128)(2,1)} %copy-done.20, bf16[128,2048]{1,0:T(8,128)(2,1)} %copy-done.19, bf16[128,2048]{1,0:T(8,128)(2,1)} %collective-permute-done.4.refs_0_.refs_3_, ...), custom_call_target="tpu_custom_call" | custom-call | flops 3221225472 | bytes 8912896 | tf_op jit(solution)/shard_map/weights/pallas_call | solution.py:214
  115.4 9.2 %weights.3 = (bf16[2,512,768]{2,1,0:T(8,128)(2,1)}, bf16[2,512,768]{2,1,0:T(8,128)(2,1)}) custom-call(bf16[128,2048]{1,0:T(8,128)(2,1)} %refs_0_.7, bf16[128,2048]{1,0:T(8,128)(2,1)} %copy-done.15, bf16[128,2048]{1,0:T(8,128)(2,1)} %copy-done.14, bf16[128,2048]{1,0:T(8,128)(2,1)} %copy-done.17, bf16[128,2048]{1,0:T(8,128)(2,1)} %copy-done.16, ...), custom_call_target="tpu_custom_call" | custom-call | flops 3221225472 | bytes 8912896 | tf_op jit(solution)/shard_map/weights/pallas_call | solution.py:214
  125.1 6.4 %weights.5 = (bf16[2,512,768]{2,1,0:T(8,128)(2,1)}, bf16[2,512,768]{2,1,0:T(8,128)(2,1)}) custom-call(bf16[128,2048]{1,0:T(8,128)(2,1)} %copy-done.7, bf16[128,2048]{1,0:T(8,128)(2,1)} %copy-done.6, bf16[64,2048]{1,0:T(8,128)(2,1)} %collective-permute-done.14.refs_4_.refs_7_.refs_2_, bf16[64,2048]{1,0:T(8,128)(2,1)} %collective-permute-done.15.refs_5_.refs_8_.refs_3_, ...), custom_call_target="tpu_custom_call" | custom-call | flops 1207959552 | bytes 5308416 | tf_op jit(solution)/shard_map/weights/pallas_call | solution.py:214
  133.6 1.5 collective-permute-start.21
  135.1 12.8 %collective-permute-done.17 = bf16[128,2176]{1,0:T(8,128)(2,1)S(1)} collective-permute-done((bf16[128,2176]{1,0:T(8,128)(2,1)S(1)}, bf16[128,2176]{1,0:T(8,128)(2,1)S(1)}, u32[]{:S(2)}, u32[]{:S(2)}) %collective-permute-start.17) | collective-permute-done | bytes 557088 | tf_op jit(solution)/shard_map/ppermute | solution.py:323
  150.3 11.8 %collective-permute-done.18 = bf16[128,2176]{1,0:T(8,128)(2,1)S(1)} collective-permute-done((bf16[128,2176]{1,0:T(8,128)(2,1)S(1)}, bf16[128,2176]{1,0:T(8,128)(2,1)S(1)}, u32[]{:S(2)}, u32[]{:S(2)}) %collective-permute-start.18) | collective-permute-done | bytes 557088 | tf_op jit(solution)/shard_map/ppermute | solution.py:323
  163.0 1.7 collective-permute-start.23
  169.5 1.6 collective-permute-start.29
  171.1 4.4 %collective-permute-done.19 = bf16[128,2176]{1,0:T(8,128)(2,1)S(1)} collective-permute-done((bf16[128,2176]{1,0:T(8,128)(2,1)S(1)}, bf16[128,2176]{1,0:T(8,128)(2,1)S(1)}, u32[]{:S(2)}, u32[]{:S(2)}) %collective-permute-start.19) | collective-permute-done | bytes 557088 | tf_op jit(solution)/shard_map/ppermute | solution.py:323
  178.0 39.7 %collective-permute-done.29.refs_2_ = bf16[1,512,768]{2,1,0:T(8,128)(2,1)} collective-permute-done((bf16[1,512,768]{2,1,0:T(8,128)(2,1)S(1)}, bf16[1,512,768]{2,1,0:T(8,128)(2,1)}, u32[]{:S(2)}, u32[]{:S(2)}) %collective-permute-start.29) | collective-permute-done | bytes 786464 | tf_op jit(solution)/shard_map/ppermute | solution.py:359
  217.6 4.0 %place.3.refs_3_ = bf16[512,2,1152]{2,1,0:T(2,128)(2,1)} custom-call(bf16[2,512,768]{2,1,0:T(8,128)(2,1)} %get-tuple-element.47.refs_0_, bf16[2,512,768]{2,1,0:T(8,128)(2,1)} %copy-done.1, bf16[1,512,768]{2,1,0:T(8,128)(2,1)} %collective-permute-done.29.refs_2_), custom_call_target="tpu_custom_call" | custom-call | tf_op jit(solution)/shard_map/place/pallas_call | solution.py:259
  221.7 4.0 %place.4.refs_3_ = bf16[512,2,1152]{2,1,0:T(2,128)(2,1)} custom-call(bf16[2,512,768]{2,1,0:T(8,128)(2,1)} %get-tuple-element.45.refs_0_, bf16[2,512,768]{2,1,0:T(8,128)(2,1)} %copy-done.4, bf16[1,512,768]{2,1,0:T(8,128)(2,1)} %collective-permute-done.27.refs_2_, bf16[512,2,1152]{2,1,0:T(2,128)(2,1)} %place.3.refs_3_), custom_call_target="tpu_custom_call", output_to_operand_aliasing={{}: (3, {})} | custom-call | tf_op jit(solution)/shard_map/place/pallas_call | solution.py:259
  225.7 4.0 %place.5 = bf16[512,2,1152]{2,1,0:T(2,128)(2,1)} custom-call(bf16[2,512,768]{2,1,0:T(8,128)(2,1)} %get-tuple-element.39.refs_0_, bf16[2,512,768]{2,1,0:T(8,128)(2,1)} %copy-done.5, bf16[1,512,768]{2,1,0:T(8,128)(2,1)} %collective-permute-done.25.refs_2_, bf16[512,2,1152]{2,1,0:T(2,128)(2,1)} %place.4.refs_3_), custom_call_target="tpu_custom_call", output_to_operand_aliasing={{}: (3, {})} | custom-call | tf_op jit(solution)/shard_map/place/pallas_call | solution.py:259
  (115 shorter events, 32.7 us)
Async XLA Ops:
  0.6 31.8 %collective-permute-start.1 = (bf16[128,2048]{1,0:T(8,128)(2,1)}, bf16[128,2048]{1,0:T(8,128)(2,1)S(1)}, u32[]{:S(2)}, u32[]{:S(2)}) collective-permute-start(bf16[128,2048]{1,0:T(8,128)(2,1)} %refs_0_.6), channel_id=1, source_target_pairs={{2,0},{4,2},{6,4},{7,6},{5,7},{3,5},{1,3},{0,1},{10,8},{12,10},{14... | collective-permute-start | bytes 1572872 | tf_op jit(solution)/shard_map/ppermute | solution.py:302
  3.6 29.4 %collective-permute-start = (bf16[128,2048]{1,0:T(8,128)(2,1)}, bf16[128,2048]{1,0:T(8,128)(2,1)S(1)}, u32[]{:S(2)}, u32[]{:S(2)}) collective-permute-start(bf16[128,2048]{1,0:T(8,128)(2,1)} %refs_0_.6), channel_id=1, source_target_pairs={{0,2},{2,4},{4,6},{6,7},{7,5},{5,3},{3,1},{1,0},{8,10},{10,12},{12... | collective-permute-start | bytes 1572872 | tf_op jit(solution)/shard_map/ppermute | solution.py:301
  3.8 30.7 %collective-permute-start.3 = (bf16[128,2048]{1,0:T(8,128)(2,1)}, bf16[128,2048]{1,0:T(8,128)(2,1)S(1)}, u32[]{:S(2)}, u32[]{:S(2)}) collective-permute-start(bf16[128,2048]{1,0:T(8,128)(2,1)} %refs_0_.7), channel_id=1, source_target_pairs={{2,0},{4,2},{6,4},{7,6},{5,7},{3,5},{1,3},{0,1},{10,8},{12,10},{14... | collective-permute-start | bytes 1572872 | tf_op jit(solution)/shard_map/ppermute | solution.py:300
  5.7 29.4 %collective-permute-start.2 = (bf16[128,2048]{1,0:T(8,128)(2,1)}, bf16[128,2048]{1,0:T(8,128)(2,1)S(1)}, u32[]{:S(2)}, u32[]{:S(2)}) collective-permute-start(bf16[128,2048]{1,0:T(8,128)(2,1)} %refs_0_.7), channel_id=1, source_target_pairs={{0,2},{2,4},{4,6},{6,7},{7,5},{5,3},{3,1},{1,0},{8,10},{10,12},{12... | collective-permute-start | bytes 1572872 | tf_op jit(solution)/shard_map/ppermute | solution.py:299
  7.8 23.8 %all-to-all-start = ((bf16[128,8,2]{0,2,1:T(2,128)(2,1)}), bf16[128,8,2]{0,2,1:T(2,128)(2,1)S(1)}, u32[]{:S(2)}, u32[]{:S(2)}) async-start(bf16[128,8,2]{0,2,1:T(2,128)(2,1)} %bitcast.1), calls=%async_computation | async-start | bytes 8192 | tf_op jit(solution)/shard_map/all_to_all | solution.py:287
  32.5 18.3 %collective-permute-start.5 = (bf16[128,2048]{1,0:T(8,128)(2,1)S(1)}, bf16[128,2048]{1,0:T(8,128)(2,1)}, u32[]{:S(2)}, u32[]{:S(2)}) collective-permute-start(bf16[128,2048]{1,0:T(8,128)(2,1)S(1)} %collective-permute-done.1.refs_2_), channel_id=1, source_target_pairs={{2,0},{4,2},{6,4},{7,6},{5,7},{3,5},{1,3},{0,1},{10,8},{12,10},{14... | collective-permute-start | bytes 1572872 | tf_op jit(solution)/shard_map/ppermute | solution.py:302
  33.0 18.4 %collective-permute-start.4 = (bf16[128,2048]{1,0:T(8,128)(2,1)S(1)}, bf16[128,2048]{1,0:T(8,128)(2,1)}, u32[]{:S(2)}, u32[]{:S(2)}) collective-permute-start(bf16[128,2048]{1,0:T(8,128)(2,1)S(1)} %collective-permute-done.refs_1_), channel_id=1, source_target_pairs={{0,2},{2,4},{4,6},{6,7},{7,5},{5,3},{3,1},{1,0},{8,10},{10,12},{12... | collective-permute-start | bytes 1572872 | tf_op jit(solution)/shard_map/ppermute | solution.py:301
  34.5 24.0 %collective-permute-start.7 = (bf16[128,2048]{1,0:T(8,128)(2,1)S(1)}, bf16[128,2048]{1,0:T(8,128)(2,1)S(1)}, u32[]{:S(2)}, u32[]{:S(2)}) collective-permute-start(bf16[128,2048]{1,0:T(8,128)(2,1)S(1)} %collective-permute-done.3.refs_8_.refs_2_), channel_id=1, source_target_pairs={{2,0},{4,2},{6,4},{7,6},{5,7},{3,5},{1,3},{0,1},{10,8},{12,10},{14... | collective-permute-start | bytes 1572872 | tf_op jit(solution)/shard_map/ppermute | solution.py:300
  35.1 24.0 %collective-permute-start.6 = (bf16[128,2048]{1,0:T(8,128)(2,1)S(1)}, bf16[128,2048]{1,0:T(8,128)(2,1)S(1)}, u32[]{:S(2)}, u32[]{:S(2)}) collective-permute-start(bf16[128,2048]{1,0:T(8,128)(2,1)S(1)} %collective-permute-done.2.refs_7_.refs_1_), channel_id=1, source_target_pairs={{0,2},{2,4},{4,6},{6,7},{7,5},{5,3},{3,1},{1,0},{8,10},{10,12},{12... | collective-permute-start | bytes 1572872 | tf_op jit(solution)/shard_map/ppermute | solution.py:299
  50.8 27.2 %collective-permute-start.9 = (bf16[128,2048]{1,0:T(8,128)(2,1)}, bf16[128,2048]{1,0:T(8,128)(2,1)}, u32[]{:S(2)}, u32[]{:S(2)}) collective-permute-start(bf16[128,2048]{1,0:T(8,128)(2,1)} %collective-permute-done.5.refs_1_.refs_4_), channel_id=1, source_target_pairs={{2,0},{4,2},{6,4},{7,6},{5,7},{3,5},{1,3},{0,1},{10,8},{12,10},{14... | collective-permute-start | bytes 1572872 | tf_op jit(solution)/shard_map/ppermute | solution.py:302
  51.4 28.2 %collective-permute-start.8 = (bf16[128,2048]{1,0:T(8,128)(2,1)}, bf16[128,2048]{1,0:T(8,128)(2,1)}, u32[]{:S(2)}, u32[]{:S(2)}) collective-permute-start(bf16[128,2048]{1,0:T(8,128)(2,1)} %collective-permute-done.4.refs_0_.refs_3_), channel_id=1, source_target_pairs={{0,2},{2,4},{4,6},{6,7},{7,5},{5,3},{3,1},{1,0},{8,10},{10,12},{12... | collective-permute-start | bytes 1572872 | tf_op jit(solution)/shard_map/ppermute | solution.py:301
  58.5 23.5 %collective-permute-start.11 = (bf16[128,2048]{1,0:T(8,128)(2,1)S(1)}, bf16[128,2048]{1,0:T(8,128)(2,1)S(1)}, u32[]{:S(2)}, u32[]{:S(2)}) collective-permute-start(bf16[128,2048]{1,0:T(8,128)(2,1)S(1)} %collective-permute-done.7.refs_5_.refs_4_), channel_id=1, source_target_pairs={{2,0},{4,2},{6,4},{7,6},{5,7},{3,5},{1,3},{0,1},{10,8},{12,10},{14... | collective-permute-start | bytes 1572872 | tf_op jit(solution)/shard_map/ppermute | solution.py:300
  59.1 23.6 %collective-permute-start.10 = (bf16[128,2048]{1,0:T(8,128)(2,1)S(1)}, bf16[128,2048]{1,0:T(8,128)(2,1)S(1)}, u32[]{:S(2)}, u32[]{:S(2)}) collective-permute-start(bf16[128,2048]{1,0:T(8,128)(2,1)S(1)} %collective-permute-done.6.refs_4_.refs_3_), channel_id=1, source_target_pairs={{0,2},{2,4},{4,6},{6,7},{7,5},{5,3},{3,1},{1,0},{8,10},{10,12},{12... | collective-permute-start | bytes 1572872 | tf_op jit(solution)/shard_map/ppermute | solution.py:299
  78.9 16.4 %collective-permute-start.13 = (bf16[64,2048]{1,0:T(8,128)(2,1)S(1)}, bf16[64,2048]{1,0:T(8,128)(2,1)}, u32[]{:S(2)}, u32[]{:S(2)}) collective-permute-start(bf16[64,2048]{1,0:T(8,128)(2,1)S(1)} %slice.49), channel_id=1, source_target_pairs={{2,0},{4,2},{6,4},{7,6},{5,7},{3,5},{1,3},{0,1},{10,8},{12,10},{14... | collective-permute-start | bytes 786440 | tf_op jit(solution)/shard_map/ppermute | solution.py:302
  104.2 27.4 %collective-permute-start.16 = (bf16[64,2176]{1,0:T(8,128)(2,1)}, bf16[64,2176]{1,0:T(8,128)(2,1)}, u32[]{:S(2)}, u32[]{:S(2)}) collective-permute-start(bf16[64,2176]{1,0:T(8,128)(2,1)} %get-tuple-element.30), channel_id=1, source_target_pairs={{2,0},{4,2},{6,4},{7,6},{5,7},{3,5},{1,3},{0,1},{10,8},{12,10},{14... | collective-permute-start | bytes 835592 | tf_op jit(solution)/shard_map/ppermute | solution.py:323
  104.8 28.7 %collective-permute-start.20 = (bf16[64,2176]{1,0:T(8,128)(2,1)}, bf16[64,2176]{1,0:T(8,128)(2,1)S(1)}, u32[]{:S(2)}, u32[]{:S(2)}) collective-permute-start(bf16[64,2176]{1,0:T(8,128)(2,1)} %get-tuple-element.34), channel_id=1, source_target_pairs={{0,2},{2,4},{4,6},{6,7},{7,5},{5,3},{3,1},{1,0},{8,10},{10,12},{12... | collective-permute-start | bytes 835592 | tf_op jit(solution)/shard_map/ppermute | solution.py:324
  115.3 49.4 %collective-permute-start.26 = (bf16[2,512,768]{2,1,0:T(8,128)(2,1)}, bf16[2,512,768]{2,1,0:T(8,128)(2,1)S(1)}, u32[]{:S(2)}, u32[]{:S(2)}) collective-permute-start(bf16[2,512,768]{2,1,0:T(8,128)(2,1)} %get-tuple-element.46), channel_id=1, source_target_pairs={{0,8},{8,0},{16,24},{24,16},{1,9},{9,1},{17,25},{25,17},{2,10},{10... | collective-permute-start | bytes 4718600 | tf_op jit(solution)/shard_map/ppermute | solution.py:352
  124.6 43.0 %collective-permute-start.24 = (bf16[2,512,768]{2,1,0:T(8,128)(2,1)}, bf16[2,512,768]{2,1,0:T(8,128)(2,1)S(1)}, u32[]{:S(2)}, u32[]{:S(2)}) collective-permute-start(bf16[2,512,768]{2,1,0:T(8,128)(2,1)} %get-tuple-element.40), channel_id=1, source_target_pairs={{0,8},{8,0},{16,24},{24,16},{1,9},{9,1},{17,25},{25,17},{2,10},{10... | collective-permute-start | bytes 4718600 | tf_op jit(solution)/shard_map/ppermute | solution.py:352
  131.5 37.8 %collective-permute-start.28 = (bf16[2,512,768]{2,1,0:T(8,128)(2,1)}, bf16[2,512,768]{2,1,0:T(8,128)(2,1)S(1)}, u32[]{:S(2)}, u32[]{:S(2)}) collective-permute-start(bf16[2,512,768]{2,1,0:T(8,128)(2,1)} %get-tuple-element.48), channel_id=1, source_target_pairs={{0,8},{8,0},{16,24},{24,16},{1,9},{9,1},{17,25},{25,17},{2,10},{10... | collective-permute-start | bytes 4718600 | tf_op jit(solution)/shard_map/ppermute | solution.py:352
  132.9 15.0 %collective-permute-start.17 = (bf16[128,2176]{1,0:T(8,128)(2,1)S(1)}, bf16[128,2176]{1,0:T(8,128)(2,1)S(1)}, u32[]{:S(2)}, u32[]{:S(2)}) collective-permute-start(bf16[128,2176]{1,0:T(8,128)(2,1)S(1)} %add_convert_fusion.9), channel_id=1, source_target_pairs={{2,0},{4,2},{6,4},{7,6},{5,7},{3,5},{1,3},{0,1},{10,8},{12,10},{14... | collective-permute-start | bytes 1671176 | tf_op jit(solution)/shard_map/ppermute | solution.py:323
  133.6 15.0 %collective-permute-start.21 = (bf16[128,2176]{1,0:T(8,128)(2,1)S(1)}, bf16[128,2176]{1,0:T(8,128)(2,1)S(1)}, u32[]{:S(2)}, u32[]{:S(2)}) collective-permute-start(bf16[128,2176]{1,0:T(8,128)(2,1)S(1)} %add_convert_fusion.6), channel_id=1, source_target_pairs={{0,2},{2,4},{4,6},{6,7},{7,5},{5,3},{3,1},{1,0},{8,10},{10,12},{12... | collective-permute-start | bytes 1671176 | tf_op jit(solution)/shard_map/ppermute | solution.py:324
  166.0 55.6 %collective-permute-start.27 = (bf16[1,512,768]{2,1,0:T(8,128)(2,1)}, bf16[1,512,768]{2,1,0:T(8,128)(2,1)}, u32[]{:S(2)}, u32[]{:S(2)}) collective-permute-start(bf16[1,512,768]{2,1,0:T(8,128)(2,1)} %add_convert_fusion.1), channel_id=1, source_target_pairs={{0,16},{8,24},{16,0},{24,8},{1,17},{9,25},{17,1},{25,9},{2,18},{10... | collective-permute-start | bytes 2359304 | tf_op jit(solution)/shard_map/ppermute | solution.py:359
  168.8 56.9 %collective-permute-start.25 = (bf16[1,512,768]{2,1,0:T(8,128)(2,1)}, bf16[1,512,768]{2,1,0:T(8,128)(2,1)}, u32[]{:S(2)}, u32[]{:S(2)}) collective-permute-start(bf16[1,512,768]{2,1,0:T(8,128)(2,1)} %add_convert_fusion.2), channel_id=1, source_target_pairs={{0,16},{8,24},{16,0},{24,8},{1,17},{9,25},{17,1},{25,9},{2,18},{10... | collective-permute-start | bytes 2359304 | tf_op jit(solution)/shard_map/ppermute | solution.py:359
  169.5 48.1 %collective-permute-start.29 = (bf16[1,512,768]{2,1,0:T(8,128)(2,1)S(1)}, bf16[1,512,768]{2,1,0:T(8,128)(2,1)}, u32[]{:S(2)}, u32[]{:S(2)}) collective-permute-start(bf16[1,512,768]{2,1,0:T(8,128)(2,1)S(1)} %add_convert_fusion), channel_id=1, source_target_pairs={{0,16},{8,24},{16,0},{24,8},{1,17},{9,25},{17,1},{25,9},{2,18},{10... | collective-permute-start | bytes 2359304 | tf_op jit(solution)/shard_map/ppermute | solution.py:359
  (28 other events, 209.1 us)

commit v6 on v5

--- a/solution.py
+++ b/solution.py
@@ -312,7 +312,7 @@
         results.append(
             expert_blocks(
                 group, table, gates, gate_up_weight, down_weight,
-                VMEM_BYTES if number == half - 1 else None,
+                {half - 1: VMEM_BYTES, half - 2: VMEM_BYTES * 14 // 15}.get(number),
             )
         )
     partial_rows = [r for result in results for r in result[2]]
@@ -350,13 +350,15 @@
     for number, at in enumerate(places):
         sent, kept = parts[2 * number : 2 * number + 2]
         arrived = lax.ppermute(sent, "dp", swap)
-        pieces = [kept, arrived]
+        crossed = []
         for shift in range(1, outer):
             pairs = [
                 (2 * y + c, 2 * ((y + shift) % outer) + c) for y in range(outer) for c in range(2)
             ]
             both = kept[shift - 1].astype(jnp.float32) + arrived[shift - 1].astype(jnp.float32)
-            pieces.append(lax.ppermute(narrow(both)[None], "dp", pairs))
+            crossed.append(lax.ppermute(narrow(both)[None], "dp", pairs))
+        own = narrow(kept[-1].astype(jnp.float32) + arrived[-1].astype(jnp.float32))[None]
+        pieces = [own, *crossed]
         weight_total = place_chunk(pieces, at, local_experts, 3 * units, weight_total)
     return (grad_tokens, grad_probs, weight_total)
 

time: 230 us -> 229 us (level)
  waiting for transfers between devices: 91.2 us -> 88.8 us
    ppermute x4, waiting for transfers between devices: 29 us -> 0.72 us  [layer(): from_right = lax.ppermute(to_left, 'expert', backward).astype(jnp.float32)]
    ppermute x4, waiting for transfers between devices: 0.71 us -> 27.4 us  [layer(): from_left = lax.ppermute(to_right, 'expert', forward).astype(jnp.float32)]
    ppermute x4, waiting for transfers between devices: 5.64 us -> 0.01 us  [layer(): xr = lax.ppermute(right[0], 'expert', backward)]
    ppermute x4, waiting for transfers between devices: 0.01 us -> 5.63 us  [layer(): xl = lax.ppermute(left[0], 'expert', forward)]
    ppermute x4, starting transfers between devices: 6.26 us -> 2.51 us  [layer(): from_left = lax.ppermute(to_right, 'expert', forward).astype(jnp.float32)]
    ppermute x4, starting transfers between devices: 2.43 us -> 6.18 us  [layer(): from_right = lax.ppermute(to_left, 'expert', backward).astype(jnp.float32)]
  transfers between devices with their start and end apart: 31 -> 31, of which waited for: 7 -> 7; matrix products, arithmetic and copies ran while one was open for 5% -> 6% of each run, Pallas kernels for 33% -> 32%
where the time goes in v6:
time: 229 us; the launch traced here: 228 us
  waiting for transfers between devices  88.8 us (39%)
  Pallas kernels  86.5 us (38%)
  starting transfers between devices  36.9 us (16%)
  other arithmetic  10.6 us (5%)
  local copies, waits for them, and re-layouts  4.7 us (2%)
    pallas_call x4, Pallas kernels, expert_blocks(): pl.pallas_call(functools.partial(expert_kernel, count, gates.shape[0]), o...  44.8 us
    ppermute x3, waiting for transfers between devices, layer(): crossed.append(lax.ppermute(narrow(both)[None], 'dp', pairs))  39.8 us
    ppermute x4, waiting for transfers between devices, layer(): from_left = lax.ppermute(to_right, 'expert', forward).astype(jnp.float32)  27.4 us
    pallas_call x3, Pallas kernels, weight_parts(): pl.pallas_call(functools.partial(weight_kernel, x_rows, p_rows, start, de...  24.4 us
    all_to_all x1, waiting for transfers between devices, layer(): lax.all_to_all(dense_gates, 'expert', split_axis=1, concat_axis=0, tiled=...  15.2 us
    pallas_call x3, Pallas kernels, place_chunk(): pl.pallas_call(functools.partial(place_kernel, len(pieces)), out_shape=ja...  10.8 us
    convert_element_type x10, other arithmetic, layer(): narrow = lambda a: a.astype(jnp.bfloat16)  6.52 us
    pallas_call x1, Pallas kernels, begun_weights(): pl.pallas_call(functools.partial(begun_kernel, len(xs)), out_shape=jax.Sh...  6.44 us
  transfers between devices with their start and end apart: 31, of which 7 were waited for; matrix products, arithmetic and copies ran while one was open for 6% of the time, Pallas kernels for 32%

profile of v6, /device:TPU:0, one launch (start us, length us, event | category | flops | bytes accessed | tf_op | source)
XLA Modules:
  0.0 228.4 jit_solution(4195362819288278878)
XLA Ops:
  0.6 3.1 %collective-permute-start = (bf16[128,2048]{1,0:T(8,128)(2,1)}, bf16[128,2048]{1,0:T(8,128)(2,1)S(1)}, u32[]{:S(2)}, u32[]{:S(2)}) collective-permute-start(bf16[128,2048]{1,0:T(8,128)(2,1)} %refs_0_.6), channel_id=1, source_target_pairs={{0,2},{2,4},{4,6},{6,7},{7,5},{5,3},{3,1},{1,0},{8,10},{10,12},{12... | collective-permute-start | bytes 1572872 | tf_op jit(solution)/shard_map/ppermute | solution.py:301
  3.7 2.0 collective-permute-start.2
  7.7 6.3 %all-to-all-start = ((bf16[128,8,2]{0,2,1:T(2,128)(2,1)}), bf16[128,8,2]{0,2,1:T(2,128)(2,1)S(1)}, u32[]{:S(2)}, u32[]{:S(2)}) async-start(bf16[128,8,2]{0,2,1:T(2,128)(2,1)} %bitcast.1), calls=%async_computation | async-start | bytes 8192 | tf_op jit(solution)/shard_map/all_to_all | solution.py:287
  15.4 15.2 %all-to-all-done = bf16[128,8,2]{0,2,1:T(2,128)(2,1)S(1)} async-done(((bf16[128,8,2]{0,2,1:T(2,128)(2,1)}), bf16[128,8,2]{0,2,1:T(2,128)(2,1)S(1)}, u32[]{:S(2)}, u32[]{:S(2)}) %all-to-all-start) | async-done | bytes 4128 | tf_op jit(solution)/shard_map/all_to_all | solution.py:287
  35.6 14.2 %experts.4 = (bf16[2,384,768]{2,1,0:T(8,128)(2,1)}, bf16[2,384,384]{2,1,0:T(8,128)(2,1)}, bf16[128,2176]{1,0:T(8,128)(2,1)}, bf16[128,2176]{1,0:T(8,128)(2,1)}, bf16[128,2176]{1,0:T(8,128)(2,1)}) custom-call(s32[9]{0:T(128)} %pad_add_fusion.scalars, bf16[128,2048]{1,0:T(8,128)(2,1)} %refs_0_.6, bf16[128,2048]{1,0:T(8,128)(2,1)} %copy-done.17, ...), custom_call_target="tpu_custom_call" | custom-call | flops 6039797760 | bytes 15728640 | tf_op jit(solution)/shard_map/experts/pallas_call | solution.py:86
  51.9 5.6 %collective-permute-done.6.refs_4_.refs_3_ = bf16[128,2048]{1,0:T(8,128)(2,1)S(1)} collective-permute-done((bf16[128,2048]{1,0:T(8,128)(2,1)S(1)}, bf16[128,2048]{1,0:T(8,128)(2,1)S(1)}, u32[]{:S(2)}, u32[]{:S(2)}) %collective-permute-start.6) | collective-permute-done | bytes 524320 | tf_op jit(solution)/shard_map/ppermute | solution.py:299
  59.6 10.9 %experts.5 = (bf16[2,256,768]{2,1,0:T(8,128)(2,1)}, bf16[2,256,384]{2,1,0:T(8,128)(2,1)}, bf16[128,2176]{1,0:T(8,128)(2,1)}, bf16[128,2176]{1,0:T(8,128)(2,1)}) custom-call(s32[9]{0:T(128)} %pad_add_fusion.scalars, bf16[128,2048]{1,0:T(8,128)(2,1)} %collective-permute-done.4.refs_0_.refs_3_, bf16[128,2048]{1,0:T(8,128)(2,1)} %collective-permute-done.5.refs_1_.refs_4_, ...), custom_call_target="tpu_custom_call" | custom-call | flops 4026531840 | bytes 13631488 | tf_op jit(solution)/shard_map/experts/pallas_call | solution.py:86
  70.5 6.4 %begun.1.refs_6_ = bf16[2048,768]{1,0:T(8,128)(2,1)} custom-call(bf16[128,2048]{1,0:T(8,128)(2,1)} %refs_0_.7, bf16[128,2048]{1,0:T(8,128)(2,1)} %copy-done.12, bf16[128,2048]{1,0:T(8,128)(2,1)} %copy-done.13, bf16[128,2048]{1,0:T(8,128)(2,1)} %copy-done.14, bf16[128,2048]{1,0:T(8,128)(2,1)} %copy-done.15, ...), custom_call_target="tpu_custom_call" | custom-call | flops 2013265920 | bytes 6750208 | tf_op jit(solution)/shard_map/begun/pallas_call | solution.py:131
  81.7 1.7 collective-permute-start.15
  83.4 10.9 %experts.6 = (bf16[2,256,768]{2,1,0:T(8,128)(2,1)}, bf16[2,256,384]{2,1,0:T(8,128)(2,1)}, bf16[128,2176]{1,0:T(8,128)(2,1)}, bf16[128,2176]{1,0:T(8,128)(2,1)}) custom-call(s32[9]{0:T(128)} %pad_add_fusion.scalars, bf16[128,2048]{1,0:T(8,128)(2,1)} %collective-permute-done.8.refs_0_.refs_5_, bf16[128,2048]{1,0:T(8,128)(2,1)} %collective-permute-done.9.refs_1_.refs_6_, ...), custom_call_target="tpu_custom_call" | custom-call | flops 4026531840 | bytes 13631488 | tf_op jit(solution)/shard_map/experts/pallas_call | solution.py:86
  94.4 8.7 %experts.7 = (bf16[2,128,768]{2,1,0:T(8,128)(2,1)}, bf16[2,128,384]{2,1,0:T(8,128)(2,1)}, bf16[64,2176]{1,0:T(8,128)(2,1)}, bf16[64,2176]{1,0:T(8,128)(2,1)}) custom-call(s32[9]{0:T(128)} %pad_add_fusion.scalars, bf16[64,2048]{1,0:T(8,128)(2,1)} %collective-permute-done.12.refs_0_.refs_7_, bf16[64,2048]{1,0:T(8,128)(2,1)} %collective-permute-done.13.refs_1_.refs_8_, ...), custom_call_target="tpu_custom_call" | custom-call | flops 2013265920 | bytes 11534336 | tf_op jit(solution)/shard_map/experts/pallas_call | solution.py:86
  105.2 9.0 %weights.3 = (bf16[2,512,768]{2,1,0:T(8,128)(2,1)}, bf16[2,512,768]{2,1,0:T(8,128)(2,1)}) custom-call(bf16[128,2048]{1,0:T(8,128)(2,1)} %refs_0_.7, bf16[128,2048]{1,0:T(8,128)(2,1)} %copy-done.12, bf16[128,2048]{1,0:T(8,128)(2,1)} %copy-done.13, bf16[128,2048]{1,0:T(8,128)(2,1)} %copy-done.14, bf16[128,2048]{1,0:T(8,128)(2,1)} %copy-done.15, ...), custom_call_target="tpu_custom_call" | custom-call | flops 3221225472 | bytes 8912896 | tf_op jit(solution)/shard_map/weights/pallas_call | solution.py:214
  114.3 9.1 %weights.4 = (bf16[2,512,768]{2,1,0:T(8,128)(2,1)}, bf16[2,512,768]{2,1,0:T(8,128)(2,1)}) custom-call(bf16[128,2048]{1,0:T(8,128)(2,1)} %refs_0_.6, bf16[128,2048]{1,0:T(8,128)(2,1)} %copy-done.17, bf16[128,2048]{1,0:T(8,128)(2,1)} %copy-done.18, bf16[128,2048]{1,0:T(8,128)(2,1)} %collective-permute-done.4.refs_0_.refs_3_, ...), custom_call_target="tpu_custom_call" | custom-call | flops 3221225472 | bytes 8912896 | tf_op jit(solution)/shard_map/weights/pallas_call | solution.py:214
  124.0 6.3 %weights.5 = (bf16[2,512,768]{2,1,0:T(8,128)(2,1)}, bf16[2,512,768]{2,1,0:T(8,128)(2,1)}) custom-call(bf16[128,2048]{1,0:T(8,128)(2,1)} %copy-done.3, bf16[128,2048]{1,0:T(8,128)(2,1)} %copy-done.4, bf16[64,2048]{1,0:T(8,128)(2,1)} %collective-permute-done.14.refs_4_.refs_7_.refs_2_, bf16[64,2048]{1,0:T(8,128)(2,1)} %collective-permute-done.15.refs_5_.refs_8_.refs_3_, ...), custom_call_target="tpu_custom_call" | custom-call | flops 1207959552 | bytes 5308416 | tf_op jit(solution)/shard_map/weights/pallas_call | solution.py:214
  133.9 12.8 %collective-permute-done.21 = bf16[128,2176]{1,0:T(8,128)(2,1)S(1)} collective-permute-done((bf16[128,2176]{1,0:T(8,128)(2,1)S(1)}, bf16[128,2176]{1,0:T(8,128)(2,1)S(1)}, u32[]{:S(2)}, u32[]{:S(2)}) %collective-permute-start.21) | collective-permute-done | bytes 557088 | tf_op jit(solution)/shard_map/ppermute | solution.py:324
  149.1 11.9 %collective-permute-done.22 = bf16[128,2176]{1,0:T(8,128)(2,1)S(1)} collective-permute-done((bf16[128,2176]{1,0:T(8,128)(2,1)S(1)}, bf16[128,2176]{1,0:T(8,128)(2,1)S(1)}, u32[]{:S(2)}, u32[]{:S(2)}) %collective-permute-start.22) | collective-permute-done | bytes 557088 | tf_op jit(solution)/shard_map/ppermute | solution.py:324
  161.8 1.7 collective-permute-start.19
  163.6 1.6 add_convert_fusion.4
  166.7 1.6 add_convert_fusion.2
  171.6 2.7 %collective-permute-done.23 = bf16[128,2176]{1,0:T(8,128)(2,1)S(1)} collective-permute-done((bf16[128,2176]{1,0:T(8,128)(2,1)S(1)}, bf16[128,2176]{1,0:T(8,128)(2,1)S(1)}, u32[]{:S(2)}, u32[]{:S(2)}) %collective-permute-start.23) | collective-permute-done | bytes 557088 | tf_op jit(solution)/shard_map/ppermute | solution.py:324
  176.8 39.8 %collective-permute-done.29.refs_1_ = bf16[1,512,768]{2,1,0:T(8,128)(2,1)S(1)} collective-permute-done((bf16[1,512,768]{2,1,0:T(8,128)(2,1)S(1)}, bf16[1,512,768]{2,1,0:T(8,128)(2,1)S(1)}, u32[]{:S(2)}, u32[]{:S(2)}) %collective-permute-start.29) | collective-permute-done | bytes 786464 | tf_op jit(solution)/shard_map/ppermute | solution.py:359
  217.5 3.6 %place.3.refs_2_ = bf16[512,2,1152]{2,1,0:T(2,128)(2,1)} custom-call(bf16[1,512,768]{2,1,0:T(8,128)(2,1)} %get-tuple-element.50.refs_0_, bf16[1,512,768]{2,1,0:T(8,128)(2,1)} %copy-done.5), custom_call_target="tpu_custom_call" | custom-call | tf_op jit(solution)/shard_map/place/pallas_call | solution.py:259
  221.1 3.6 %place.4.refs_2_ = bf16[512,2,1152]{2,1,0:T(2,128)(2,1)} custom-call(bf16[1,512,768]{2,1,0:T(8,128)(2,1)} %get-tuple-element.52.refs_0_, bf16[1,512,768]{2,1,0:T(8,128)(2,1)} %collective-permute-done.27.refs_1_, bf16[512,2,1152]{2,1,0:T(2,128)(2,1)} %place.3.refs_2_), custom_call_target="tpu_custom_call", output_to_operand_aliasing={{}: (2, {})} | custom-call | tf_op jit(solution)/shard_map/place/pallas_call | solution.py:259
  224.8 3.6 %place.5 = bf16[512,2,1152]{2,1,0:T(2,128)(2,1)} custom-call(bf16[1,512,768]{2,1,0:T(8,128)(2,1)} %get-tuple-element.54.refs_0_, bf16[1,512,768]{2,1,0:T(8,128)(2,1)} %collective-permute-done.25.refs_1_, bf16[512,2,1152]{2,1,0:T(2,128)(2,1)} %place.4.refs_2_), custom_call_target="tpu_custom_call", output_to_operand_aliasing={{}: (2, {})} | custom-call | tf_op jit(solution)/shard_map/place/pallas_call | solution.py:259
  (111 shorter events, 35.0 us)
Async XLA Ops:
  0.6 30.9 %collective-permute-start = (bf16[128,2048]{1,0:T(8,128)(2,1)}, bf16[128,2048]{1,0:T(8,128)(2,1)S(1)}, u32[]{:S(2)}, u32[]{:S(2)}) collective-permute-start(bf16[128,2048]{1,0:T(8,128)(2,1)} %refs_0_.6), channel_id=1, source_target_pairs={{0,2},{2,4},{4,6},{6,7},{7,5},{5,3},{3,1},{1,0},{8,10},{10,12},{12... | collective-permute-start | bytes 1572872 | tf_op jit(solution)/shard_map/ppermute | solution.py:301
  3.7 28.4 %collective-permute-start.1 = (bf16[128,2048]{1,0:T(8,128)(2,1)}, bf16[128,2048]{1,0:T(8,128)(2,1)S(1)}, u32[]{:S(2)}, u32[]{:S(2)}) collective-permute-start(bf16[128,2048]{1,0:T(8,128)(2,1)} %refs_0_.6), channel_id=1, source_target_pairs={{2,0},{4,2},{6,4},{7,6},{5,7},{3,5},{1,3},{0,1},{10,8},{12,10},{14... | collective-permute-start | bytes 1572872 | tf_op jit(solution)/shard_map/ppermute | solution.py:302
  3.7 29.8 %collective-permute-start.2 = (bf16[128,2048]{1,0:T(8,128)(2,1)}, bf16[128,2048]{1,0:T(8,128)(2,1)S(1)}, u32[]{:S(2)}, u32[]{:S(2)}) collective-permute-start(bf16[128,2048]{1,0:T(8,128)(2,1)} %refs_0_.7), channel_id=1, source_target_pairs={{0,2},{2,4},{4,6},{6,7},{7,5},{5,3},{3,1},{1,0},{8,10},{10,12},{12... | collective-permute-start | bytes 1572872 | tf_op jit(solution)/shard_map/ppermute | solution.py:299
  5.8 28.4 %collective-permute-start.3 = (bf16[128,2048]{1,0:T(8,128)(2,1)}, bf16[128,2048]{1,0:T(8,128)(2,1)S(1)}, u32[]{:S(2)}, u32[]{:S(2)}) collective-permute-start(bf16[128,2048]{1,0:T(8,128)(2,1)} %refs_0_.7), channel_id=1, source_target_pairs={{2,0},{4,2},{6,4},{7,6},{5,7},{3,5},{1,3},{0,1},{10,8},{12,10},{14... | collective-permute-start | bytes 1572872 | tf_op jit(solution)/shard_map/ppermute | solution.py:300
  7.7 22.9 %all-to-all-start = ((bf16[128,8,2]{0,2,1:T(2,128)(2,1)}), bf16[128,8,2]{0,2,1:T(2,128)(2,1)S(1)}, u32[]{:S(2)}, u32[]{:S(2)}) async-start(bf16[128,8,2]{0,2,1:T(2,128)(2,1)} %bitcast.1), calls=%async_computation | async-start | bytes 8192 | tf_op jit(solution)/shard_map/all_to_all | solution.py:287
  31.5 18.3 %collective-permute-start.4 = (bf16[128,2048]{1,0:T(8,128)(2,1)S(1)}, bf16[128,2048]{1,0:T(8,128)(2,1)}, u32[]{:S(2)}, u32[]{:S(2)}) collective-permute-start(bf16[128,2048]{1,0:T(8,128)(2,1)S(1)} %collective-permute-done.refs_1_), channel_id=1, source_target_pairs={{0,2},{2,4},{4,6},{6,7},{7,5},{5,3},{3,1},{1,0},{8,10},{10,12},{12... | collective-permute-start | bytes 1572872 | tf_op jit(solution)/shard_map/ppermute | solution.py:301
  32.1 18.4 %collective-permute-start.5 = (bf16[128,2048]{1,0:T(8,128)(2,1)S(1)}, bf16[128,2048]{1,0:T(8,128)(2,1)}, u32[]{:S(2)}, u32[]{:S(2)}) collective-permute-start(bf16[128,2048]{1,0:T(8,128)(2,1)S(1)} %collective-permute-done.1.refs_2_), channel_id=1, source_target_pairs={{2,0},{4,2},{6,4},{7,6},{5,7},{3,5},{1,3},{0,1},{10,8},{12,10},{14... | collective-permute-start | bytes 1572872 | tf_op jit(solution)/shard_map/ppermute | solution.py:302
  33.6 24.0 %collective-permute-start.6 = (bf16[128,2048]{1,0:T(8,128)(2,1)S(1)}, bf16[128,2048]{1,0:T(8,128)(2,1)S(1)}, u32[]{:S(2)}, u32[]{:S(2)}) collective-permute-start(bf16[128,2048]{1,0:T(8,128)(2,1)S(1)} %collective-permute-done.2.refs_7_.refs_1_), channel_id=1, source_target_pairs={{0,2},{2,4},{4,6},{6,7},{7,5},{5,3},{3,1},{1,0},{8,10},{10,12},{12... | collective-permute-start | bytes 1572872 | tf_op jit(solution)/shard_map/ppermute | solution.py:299
  34.2 24.0 %collective-permute-start.7 = (bf16[128,2048]{1,0:T(8,128)(2,1)S(1)}, bf16[128,2048]{1,0:T(8,128)(2,1)S(1)}, u32[]{:S(2)}, u32[]{:S(2)}) collective-permute-start(bf16[128,2048]{1,0:T(8,128)(2,1)S(1)} %collective-permute-done.3.refs_8_.refs_2_), channel_id=1, source_target_pairs={{2,0},{4,2},{6,4},{7,6},{5,7},{3,5},{1,3},{0,1},{10,8},{12,10},{14... | collective-permute-start | bytes 1572872 | tf_op jit(solution)/shard_map/ppermute | solution.py:300
  49.9 27.1 %collective-permute-start.8 = (bf16[128,2048]{1,0:T(8,128)(2,1)}, bf16[128,2048]{1,0:T(8,128)(2,1)}, u32[]{:S(2)}, u32[]{:S(2)}) collective-permute-start(bf16[128,2048]{1,0:T(8,128)(2,1)} %collective-permute-done.4.refs_0_.refs_3_), channel_id=1, source_target_pairs={{0,2},{2,4},{4,6},{6,7},{7,5},{5,3},{3,1},{1,0},{8,10},{10,12},{12... | collective-permute-start | bytes 1572872 | tf_op jit(solution)/shard_map/ppermute | solution.py:301
  50.5 28.1 %collective-permute-start.9 = (bf16[128,2048]{1,0:T(8,128)(2,1)}, bf16[128,2048]{1,0:T(8,128)(2,1)}, u32[]{:S(2)}, u32[]{:S(2)}) collective-permute-start(bf16[128,2048]{1,0:T(8,128)(2,1)} %collective-permute-done.5.refs_1_.refs_4_), channel_id=1, source_target_pairs={{2,0},{4,2},{6,4},{7,6},{5,7},{3,5},{1,3},{0,1},{10,8},{12,10},{14... | collective-permute-start | bytes 1572872 | tf_op jit(solution)/shard_map/ppermute | solution.py:302
  57.6 23.5 %collective-permute-start.10 = (bf16[128,2048]{1,0:T(8,128)(2,1)S(1)}, bf16[128,2048]{1,0:T(8,128)(2,1)S(1)}, u32[]{:S(2)}, u32[]{:S(2)}) collective-permute-start(bf16[128,2048]{1,0:T(8,128)(2,1)S(1)} %collective-permute-done.6.refs_4_.refs_3_), channel_id=1, source_target_pairs={{0,2},{2,4},{4,6},{6,7},{7,5},{5,3},{3,1},{1,0},{8,10},{10,12},{12... | collective-permute-start | bytes 1572872 | tf_op jit(solution)/shard_map/ppermute | solution.py:299
  58.1 23.6 %collective-permute-start.11 = (bf16[128,2048]{1,0:T(8,128)(2,1)S(1)}, bf16[128,2048]{1,0:T(8,128)(2,1)S(1)}, u32[]{:S(2)}, u32[]{:S(2)}) collective-permute-start(bf16[128,2048]{1,0:T(8,128)(2,1)S(1)} %collective-permute-done.7.refs_5_.refs_4_), channel_id=1, source_target_pairs={{2,0},{4,2},{6,4},{7,6},{5,7},{3,5},{1,3},{0,1},{10,8},{12,10},{14... | collective-permute-start | bytes 1572872 | tf_op jit(solution)/shard_map/ppermute | solution.py:300
  78.0 16.4 %collective-permute-start.12 = (bf16[64,2048]{1,0:T(8,128)(2,1)S(1)}, bf16[64,2048]{1,0:T(8,128)(2,1)}, u32[]{:S(2)}, u32[]{:S(2)}) collective-permute-start(bf16[64,2048]{1,0:T(8,128)(2,1)S(1)} %slice.72), channel_id=1, source_target_pairs={{0,2},{2,4},{4,6},{6,7},{7,5},{5,3},{3,1},{1,0},{8,10},{10,12},{12... | collective-permute-start | bytes 786440 | tf_op jit(solution)/shard_map/ppermute | solution.py:301
  103.2 27.3 %collective-permute-start.20 = (bf16[64,2176]{1,0:T(8,128)(2,1)}, bf16[64,2176]{1,0:T(8,128)(2,1)}, u32[]{:S(2)}, u32[]{:S(2)}) collective-permute-start(bf16[64,2176]{1,0:T(8,128)(2,1)} %get-tuple-element.34), channel_id=1, source_target_pairs={{0,2},{2,4},{4,6},{6,7},{7,5},{5,3},{3,1},{1,0},{8,10},{10,12},{12... | collective-permute-start | bytes 835592 | tf_op jit(solution)/shard_map/ppermute | solution.py:324
  103.8 28.5 %collective-permute-start.16 = (bf16[64,2176]{1,0:T(8,128)(2,1)}, bf16[64,2176]{1,0:T(8,128)(2,1)S(1)}, u32[]{:S(2)}, u32[]{:S(2)}) collective-permute-start(bf16[64,2176]{1,0:T(8,128)(2,1)} %get-tuple-element.30), channel_id=1, source_target_pairs={{2,0},{4,2},{6,4},{7,6},{5,7},{3,5},{1,3},{0,1},{10,8},{12,10},{14... | collective-permute-start | bytes 835592 | tf_op jit(solution)/shard_map/ppermute | solution.py:323
  114.3 49.3 %collective-permute-start.24 = (bf16[2,512,768]{2,1,0:T(8,128)(2,1)}, bf16[2,512,768]{2,1,0:T(8,128)(2,1)S(1)}, u32[]{:S(2)}, u32[]{:S(2)}) collective-permute-start(bf16[2,512,768]{2,1,0:T(8,128)(2,1)} %get-tuple-element.40), channel_id=1, source_target_pairs={{0,8},{8,0},{16,24},{24,16},{1,9},{9,1},{17,25},{25,17},{2,10},{10... | collective-permute-start | bytes 4718600 | tf_op jit(solution)/shard_map/ppermute | solution.py:352
  123.5 43.2 %collective-permute-start.26 = (bf16[2,512,768]{2,1,0:T(8,128)(2,1)}, bf16[2,512,768]{2,1,0:T(8,128)(2,1)S(1)}, u32[]{:S(2)}, u32[]{:S(2)}) collective-permute-start(bf16[2,512,768]{2,1,0:T(8,128)(2,1)} %get-tuple-element.46), channel_id=1, source_target_pairs={{0,8},{8,0},{16,24},{24,16},{1,9},{9,1},{17,25},{25,17},{2,10},{10... | collective-permute-start | bytes 4718600 | tf_op jit(solution)/shard_map/ppermute | solution.py:352
  130.3 38.5 %collective-permute-start.28 = (bf16[2,512,768]{2,1,0:T(8,128)(2,1)}, bf16[2,512,768]{2,1,0:T(8,128)(2,1)S(1)}, u32[]{:S(2)}, u32[]{:S(2)}) collective-permute-start(bf16[2,512,768]{2,1,0:T(8,128)(2,1)} %get-tuple-element.48), channel_id=1, source_target_pairs={{0,8},{8,0},{16,24},{24,16},{1,9},{9,1},{17,25},{25,17},{2,10},{10... | collective-permute-start | bytes 4718600 | tf_op jit(solution)/shard_map/ppermute | solution.py:352
  131.7 15.0 %collective-permute-start.21 = (bf16[128,2176]{1,0:T(8,128)(2,1)S(1)}, bf16[128,2176]{1,0:T(8,128)(2,1)S(1)}, u32[]{:S(2)}, u32[]{:S(2)}) collective-permute-start(bf16[128,2176]{1,0:T(8,128)(2,1)S(1)} %add_convert_fusion.9), channel_id=1, source_target_pairs={{0,2},{2,4},{4,6},{6,7},{7,5},{5,3},{3,1},{1,0},{8,10},{10,12},{12... | collective-permute-start | bytes 1671176 | tf_op jit(solution)/shard_map/ppermute | solution.py:324
  132.4 15.0 %collective-permute-start.17 = (bf16[128,2176]{1,0:T(8,128)(2,1)S(1)}, bf16[128,2176]{1,0:T(8,128)(2,1)S(1)}, u32[]{:S(2)}, u32[]{:S(2)}) collective-permute-start(bf16[128,2176]{1,0:T(8,128)(2,1)S(1)} %add_convert_fusion.12), channel_id=1, source_target_pairs={{2,0},{4,2},{6,4},{7,6},{5,7},{3,5},{1,3},{0,1},{10,8},{12,10},{14... | collective-permute-start | bytes 1671176 | tf_op jit(solution)/shard_map/ppermute | solution.py:323
  165.1 59.6 %collective-permute-start.25 = (bf16[1,512,768]{2,1,0:T(8,128)(2,1)}, bf16[1,512,768]{2,1,0:T(8,128)(2,1)}, u32[]{:S(2)}, u32[]{:S(2)}) collective-permute-start(bf16[1,512,768]{2,1,0:T(8,128)(2,1)} %get-tuple-element.53), channel_id=1, source_target_pairs={{0,16},{8,24},{16,0},{24,8},{1,17},{9,25},{17,1},{25,9},{2,18},{10... | collective-permute-start | bytes 2359304 | tf_op jit(solution)/shard_map/ppermute | solution.py:359
  168.3 52.9 %collective-permute-start.27 = (bf16[1,512,768]{2,1,0:T(8,128)(2,1)}, bf16[1,512,768]{2,1,0:T(8,128)(2,1)}, u32[]{:S(2)}, u32[]{:S(2)}) collective-permute-start(bf16[1,512,768]{2,1,0:T(8,128)(2,1)} %get-tuple-element.51), channel_id=1, source_target_pairs={{0,16},{8,24},{16,0},{24,8},{1,17},{9,25},{17,1},{25,9},{2,18},{10... | collective-permute-start | bytes 2359304 | tf_op jit(solution)/shard_map/ppermute | solution.py:359
  170.1 46.5 %collective-permute-start.29 = (bf16[1,512,768]{2,1,0:T(8,128)(2,1)S(1)}, bf16[1,512,768]{2,1,0:T(8,128)(2,1)S(1)}, u32[]{:S(2)}, u32[]{:S(2)}) collective-permute-start(bf16[1,512,768]{2,1,0:T(8,128)(2,1)S(1)} %get-tuple-element.49), channel_id=1, source_target_pairs={{0,16},{8,24},{16,0},{24,8},{1,17},{9,25},{17,1},{25,9},{2,18},{10... | collective-permute-start | bytes 2359304 | tf_op jit(solution)/shard_map/ppermute | solution.py:359
  (26 other events, 193.1 us)
